TPU v7x, 128 devices: a whole 4x4x4 slice. The times are simulated.
128 devices in a mesh: gz: 8 (over x, core), xy: 16 (over y, z).
Axes of the slice: x: 4, y: 4, z: 4, core: 2. Of those that a mesh axis runs over, the one named last changes fastest.
Arguments:
- thermal_load: float32 [128, 4, 256, 384], P('gz', None, 'xy'), may hold values from -12 to 12
- material: int32 [128, 256, 384], P('gz', 'xy'), may hold values from 0 to 7
- layer_ids: int32 [128, 256, 384], P('gz', 'xy'), may hold values from 0 to 5
- stiffness: float32 [8, 4, 4], replicated, may hold values from -0.7 to 13, as said below
- coupling: float32 [6, 4, 4], replicated, may hold values from -0.15 to 0.9, as said below
- pivots: float32 [8, 4, 4], replicated, may hold values from -0.015 to 0.14, as said below
- factor: float32 [6, 4, 4], replicated, may hold values from -0.01 to 1
Outputs:
- solution: float32 [128, 4, 256, 384], P('gz', None, 'xy')
- residual: float32 [128, 4, 256, 384], P('gz', None, 'xy')
Inputs may be any that keep to these rules, and one draw needn't show every extreme that they name: `stiffness`: each block is symmetric, and the operator A of the steps is positive definite. `coupling`: each block is symmetric. `pivots`: each block is symmetric positive definite.
All inputs are finite; a program needn't handle non-finite values.
Results may differ from a plain program's by a relative error of at most 0.0003.
Values sent between devices are 32-bit elements; how exact they have to be, the bound alone decides.
No kernel may reach another device: no remote copies, remote signals or barrier semaphores. Data moves between devices by JAX's collectives and lax.ppermute only.
A program may use at most 192 MiB of HBM per device.

v0:
```python
import jax
import jax.numpy as jnp
from jax import lax
from jax.experimental import pallas as pl
from jax.experimental.pallas import tpu as pltpu
from jax.sharding import Mesh
from jax.sharding import PartitionSpec as P

GZ = ("gz_0", "gz_1")
XY = ("xy_0", "xy_1")
ALL = GZ + XY
F32 = jnp.float32
I32 = jnp.int32

NZ = 16
NSEG = 8
COLS = [(xi, lj) for xi in range(2) for lj in range(3)]
SYM = [(i, j) for i in range(4) for j in range(i, 4)]
SYMI = {}
for _n, (_i, _j) in enumerate(SYM):
    SYMI[(_i, _j)] = _n
    SYMI[(_j, _i)] = _n
T_P, T_S, T_K, T_C = 0, 16, 26, 36
NTAB = 46
NONE = 127
R1, R2, R3 = 224, 72, 56
MIB = 1 << 20


def tile(xi, lj):
    return pl.ds(8 * xi, 8), pl.ds(128 * lj, 128)


def look(tabs, first, count, ids):
    return [
        jnp.take_along_axis(tabs[first + e], ids, axis=1, mode="promise_in_bounds")
        for e in range(count)
    ]


def fsum(terms):
    terms = list(terms)
    while len(terms) > 1:
        terms = [
            terms[n] + terms[n + 1] if n + 1 < len(terms) else terms[n]
            for n in range(0, len(terms), 2)
        ]
    return terms[0]


def full(blk, v):
    return [fsum(blk[4 * i + j] * v[j] for j in range(4)) for i in range(4)]


def full_t(blk, v):
    return [fsum(blk[4 * i + j] * v[i] for i in range(4)) for j in range(4)]


def symm(blk, v):
    return [fsum(blk[SYMI[(i, j)]] * v[j] for j in range(4)) for i in range(4)]


def add(a, b):
    return [x + y for x, y in zip(a, b)]


def build_tables(tabs, fac, piv, stf, cpl):
    lane = lax.broadcasted_iota(I32, (8, 128), 1)
    zero = jnp.zeros((8, 128), F32)
    for src, first, count, pairs in (
        (fac, T_P, 6, [(i, j) for i in range(4) for j in range(4)]),
        (piv, T_S, 8, SYM),
        (stf, T_K, 8, SYM),
        (cpl, T_C, 6, SYM),
    ):
        for e, (i, j) in enumerate(pairs):
            row = zero
            for m in range(count):
                row = jnp.where(lane == m, src[m, i, j], row)
            tabs[first + e] = row


def first_sweep(r, mat, lay, fac, piv, stf, cpl, send, tabs):
    build_tables(tabs, fac, piv, stf, cpl)
    for n, (xi, lj) in enumerate(COLS):
        rows, lanes = tile(xi, lj)

        def level(z, state):
            g, x, q, w = state[:4], state[4:20], state[20:30], state[30:34]
            blk = look(tabs, T_P, 16, lay[z, rows, lanes])
            g = add([r[z, c, rows, lanes] for c in range(4)], full(blk, g))
            xcols = [full(blk, [x[4 * j + c] for j in range(4)]) for c in range(4)]
            piv_blk = look(tabs, T_S, 10, mat[z, rows, lanes])
            h = symm(piv_blk, g)
            w = [w[c] + fsum(xcols[c][i] * h[i] for i in range(4)) for c in range(4)]
            q = list(q)
            for c in range(4):
                sx = symm(piv_blk, xcols[c])
                for d in range(c + 1):
                    e = SYMI[(d, c)]
                    q[e] = q[e] + fsum(xcols[d][i] * sx[i] for i in range(4))
            x = [xcols[c][j] for j in range(4) for c in range(4)]
            return tuple(list(g) + x + q + list(w))

        zero = jnp.zeros((8, 128), F32)
        one = jnp.ones((8, 128), F32)
        g = [r[0, c, rows, lanes] for c in range(4)]
        q = look(tabs, T_S, 10, mat[0, rows, lanes])
        w = symm(q, g)
        x = [one if i == j else zero for i in range(4) for j in range(4)]
        state = lax.fori_loop(1, NZ, level, tuple(g + x + q + w))
        g, x, q, w = state[:4], state[4:20], state[20:30], state[30:34]
        ids = [lay[0, rows, lanes], lay[NZ - 1, rows, lanes], mat[NZ - 1, rows, lanes]]
        values = list(g) + list(w) + list(x) + list(q) + [v.astype(F32) for v in ids]
        for v, value in enumerate(values):
            send[pl.ds(6 * v + n, 8, stride=R1), :] = value


def make_owner(first):
    out_rows = R2 if first else R3

    def owner(recv, fixed, tabs, back):
        def get(ref, per, k, v):
            return ref[pl.ds(per * k + 6 * v, 8), :]

        per = R1 if first else R3

        def ident(k, v):
            return jnp.bitwise_and(get(fixed, R1, k, v).astype(I32), 127)

        zero = jnp.zeros((8, 128), F32)
        state = [zero] * 4
        inflow = []
        bottoms = []
        for k in range(NSEG):
            for c in range(4):
                back[pl.ds(out_rows * k + 6 * c, 6), :] = state[c][:6]
            bottom = look(tabs, T_P, 16, ident(k, 34))
            bottoms.append(bottom)
            a = full(bottom, state)
            inflow.append(a)
            if k < NSEG - 1:
                x = [get(fixed, R1, k, 8 + e) for e in range(16)]
                state = add([get(recv, per, k, c) for c in range(4)], full(x, a))
        b = [zero] * 4
        t = [zero] * 4
        for k in reversed(range(NSEG)):
            for c in range(4):
                back[pl.ds(out_rows * k + 24 + 6 * c, 6), :] = b[c][:6]
            if k > 0:
                q = [get(fixed, R1, k, 24 + e) for e in range(10)]
                wb = add([get(recv, per, k, 4 + c) for c in range(4)], symm(q, inflow[k]))
                if k < NSEG - 1:
                    x = [get(fixed, R1, k, 8 + e) for e in range(16)]
                    wb = add(wb, full_t(x, t))
                b = wb
                t = full_t(bottoms[k], b)
        if first:
            none = jnp.full((6, 128), float(NONE), F32)
            for k in range(NSEG):
                above = get(fixed, R1, k + 1, 34)[:6] if k + 1 < NSEG else none
                back[pl.ds(R2 * k + 48, 6), :] = above
                for e in range(2):
                    below = get(fixed, R1, k - 1, 35 + e)[:6] if k > 0 else none
                    back[pl.ds(R2 * k + 54 + 6 * e, 6), :] = below
                back[pl.ds(R2 * k + 66, 6), :] = none

    return owner


def make_apply(first):
    per = R2 if first else R3

    def apply(r, mat, lay, back, first_back, tabs, other, u, zlow, zup, elo, ehi, dots, pscr, hscr):
        acc_r = jnp.zeros((8, 128), F32)
        acc_o = jnp.zeros((8, 128), F32)
        for n, (xi, lj) in enumerate(COLS):
            rows, lanes = tile(xi, lj)

            def get(v, ref=back, p=per):
                return ref[pl.ds(6 * v + n, 8, stride=p), :]

            inflow = [get(c) for c in range(4)]
            b = [get(4 + c) for c in range(4)]
            ids = [get(8 + e, first_back, R2).astype(I32) for e in range(3)]

            def up(z, g):
                blk = look(tabs, T_P, 16, lay[z, rows, lanes])
                for e in range(16):
                    pscr[z, e] = blk[e]
                g = add([r[z, c, rows, lanes] for c in range(4)], full(blk, g))
                h = symm(look(tabs, T_S, 10, mat[z, rows, lanes]), g)
                for c in range(4):
                    hscr[z, c] = h[c]
                return tuple(g)

            lax.fori_loop(0, NZ, up, tuple(inflow))
            t = full_t(look(tabs, T_P, 16, ids[0]), b)

            def down(s, carry):
                z = NZ - 1 - s
                t, ar, ao = carry[:4], carry[4], carry[5]
                w = add([hscr[z, c] for c in range(4)], t)
                for c in range(4):
                    u[z, c, rows, lanes] = w[c]
                ar = ar + fsum(w[c] * r[z, c, rows, lanes] for c in range(4))
                if not first:
                    ao = ao + fsum(w[c] * other[z, c, rows, lanes] for c in range(4))
                t = full_t([pscr[z, e] for e in range(16)], w)
                return tuple(t) + (ar, ao)

            carry = lax.fori_loop(0, NZ, down, tuple(t) + (acc_r, acc_o))
            t, acc_r, acc_o = carry[:4], carry[4], carry[5]
            below = add(symm(look(tabs, T_S, 10, ids[2]), inflow), t)
            pushed = symm(look(tabs, T_C, 10, ids[1]), below)
            for c in range(4):
                zlow[c, rows, lanes] = pushed[c]
                zup[c, rows, lanes] = b[c]
        dots[0] = acc_r
        dots[1] = acc_o

        def edges(z, carry):
            for c in range(4):
                elo[z, pl.ds(c, 1), :] = u[z, c, pl.ds(0, 1), :]
                ehi[z, pl.ds(c, 1), :] = u[z, c, pl.ds(15, 1), :]
            return carry

        lax.fori_loop(0, NZ, edges, 0)

    return apply


def operator(u, mat, lay, zlow, zup, tabs, out, push):
    col = lax.broadcasted_iota(I32, (8, 384), 1)
    row = lax.broadcasted_iota(I32, (8, 384), 0)
    push[...] = zlow[...]

    def level(z, carry):
        for xi in range(2):
            rows = pl.ds(8 * xi, 8)
            side = []
            for c in range(4):
                here = u[z, c, rows, :]
                west = jnp.where(col == 0, 0.0, pltpu.roll(here, 1, 1))
                east = jnp.where(col == 383, 0.0, pltpu.roll(here, 383, 1))
                other = u[z, c, pl.ds(8 * (1 - xi), 8), :]
                down = pltpu.roll(here, 1, 0)
                upw = pltpu.roll(here, 7, 0)
                if xi == 0:
                    down = jnp.where(row == 0, 0.0, down)
                    upw = jnp.where(row == 7, pltpu.roll(other, 7, 0), upw)
                else:
                    down = jnp.where(row == 0, pltpu.roll(other, 1, 0), down)
                    upw = jnp.where(row == 7, 0.0, upw)
                side.append((west + east) + (down + upw))
            for lj in range(3):
                lanes = pl.ds(128 * lj, 128)
                v = [u[z, c, rows, lanes] for c in range(4)]
                nz = jnp.minimum(z + 1, NZ - 1)
                above = [
                    jnp.where(z == NZ - 1, zup[c, rows, lanes], u[nz, c, rows, lanes])
                    for c in range(4)
                ]
                kv = symm(look(tabs, T_K, 10, mat[z, rows, lanes]), v)
                cb = look(tabs, T_C, 10, lay[z, rows, lanes])
                fa = symm(cb, above)
                fb = symm(cb, v)
                for c in range(4):
                    near = side[c][:, 128 * lj : 128 * (lj + 1)]
                    out[z, c, rows, lanes] = kv[c] - near - fa[c] - push[c, rows, lanes]
                    push[c, rows, lanes] = fb[c]
        return carry

    lax.fori_loop(0, NZ, level, 0)


def with_halo(part, lo, hi, z, c, xi, lj, row):
    rows, lanes = tile(xi, lj)
    edge = (lo if xi == 0 else hi)[z, pl.ds(c, 1), lanes]
    return part[z, c, rows, lanes] - jnp.where(row == (0 if xi == 0 else 7), edge, 0.0)


def second_sweep(part, lo, hi, u, mat, lay, tabs, image, send, dots, pscr, hscr):
    row = lax.broadcasted_iota(I32, (8, 128), 0)
    zero = jnp.zeros((8, 128), F32)
    acc = zero
    for n, (xi, lj) in enumerate(COLS):
        rows, lanes = tile(xi, lj)

        def up(z, carry):
            g, acc = carry[:4], carry[4]
            blk = look(tabs, T_P, 16, lay[z, rows, lanes])
            for e in range(16):
                pscr[z, e] = blk[e]
            img = [with_halo(part, lo, hi, z, c, xi, lj, row) for c in range(4)]
            for c in range(4):
                image[z, c, rows, lanes] = img[c]
            acc = acc + fsum(img[c] * u[z, c, rows, lanes] for c in range(4))
            g = add(img, full(blk, g))
            h = symm(look(tabs, T_S, 10, mat[z, rows, lanes]), g)
            for c in range(4):
                hscr[z, c] = h[c]
            return tuple(g) + (acc,)

        carry = lax.fori_loop(0, NZ, up, (zero,) * 4 + (acc,))
        g, acc = carry[:4], carry[4]

        def down(s, w):
            z = NZ - 2 - s
            t = full_t([pscr[z + 1, e] for e in range(16)], w)
            return tuple(add([hscr[z, c] for c in range(4)], t))

        w = lax.fori_loop(0, NZ - 1, down, tuple(hscr[NZ - 1, c] for c in range(4)))
        for v, value in enumerate(list(g) + list(w)):
            send[pl.ds(6 * v + n, 8, stride=R3), :] = value
    dots[0] = acc


def last_dots(part, lo, hi, u, w, da, db, dc, y, sums):
    row = lax.broadcasted_iota(I32, (8, 128), 0)
    zero = jnp.zeros((8, 128), F32)

    def level(z, carry):
        au, aw = carry
        for xi, lj in COLS:
            rows, lanes = tile(xi, lj)
            for c in range(4):
                val = with_halo(part, lo, hi, z, c, xi, lj, row)
                y[z, c, rows, lanes] = val
                au = au + val * u[z, c, rows, lanes]
                aw = aw + val * w[z, c, rows, lanes]
        return au, aw

    au, aw = lax.fori_loop(0, NZ, level, (zero, zero))
    lane = lax.broadcasted_iota(I32, (1, 128), 1)
    line = jnp.zeros((1, 128), F32)
    for e, part_sum in enumerate((da[0], dc[0], db[0], db[1], au, aw)):
        line = jnp.where(lane == e, jnp.sum(part_sum), line)
    sums[...] = jnp.broadcast_to(line[None], sums.shape)


def combine(sums, r, u, image, w, y, sol, res):
    tot = jnp.sum(sums[...], axis=0)
    ru, ui, iw, rw, uy, wy = [tot[:, e : e + 1] for e in range(6)]
    a0 = ru / ui
    fresh = ru - a0 * (rw + ui) + a0 * a0 * iw
    beta1 = 1.0 + fresh / ru
    curv = beta1 * beta1 * ui - beta1 * a0 * (uy + iw) + a0 * a0 * wy
    a1 = fresh / curv
    s0 = jnp.broadcast_to(a0 + a1 * beta1, (8, 128))
    s1 = jnp.broadcast_to(a1 * a0, (8, 128))

    def level(z, carry):
        for xi, lj in COLS:
            rows, lanes = tile(xi, lj)
            for c in range(4):
                at = (z, c, rows, lanes)
                sol[at] = s0 * u[at] - s1 * w[at]
                res[at] = r[at] - s0 * image[at] + s1 * y[at]
        return carry

    lax.fori_loop(0, NZ, level, 0)


def call(body, out, name, smem=(), scratch=(), nargs=0, limit=24):
    vm = pl.BlockSpec(memory_space=pltpu.VMEM)
    sm = pl.BlockSpec(memory_space=pltpu.SMEM)
    return pl.pallas_call(
        body,
        out_shape=[jax.ShapeDtypeStruct(s, F32) for s in out],
        in_specs=[sm if n in smem else vm for n in range(nargs)],
        out_specs=[vm for _ in out],
        scratch_shapes=[pltpu.VMEM(s, F32) for s in scratch],
        compiler_params=pltpu.CompilerParams(vmem_limit_bytes=limit * MIB),
        name=name,
    )


FIELD = (NZ, 4, 16, 384)
EDGE = (NZ, 4, 384)
PLANE = (4, 16, 384)
TABS = (NTAB, 8, 128)
SCR = ((NZ, 16, 8, 128), (NZ, 4, 8, 128))


def exchange(buf, per):
    buf = lax.all_to_all(buf.reshape(NSEG, per, 128), GZ, 0, 0, tiled=True)
    return buf.reshape(NSEG * per, 128)


def halo(elo, ehi):
    count = lax.axis_size(XY)
    lo = lax.ppermute(ehi, XY, [(i, i + 1) for i in range(count - 1)])
    hi = lax.ppermute(elo, XY, [(i + 1, i) for i in range(count - 1)])
    return lo, hi


def apply_m(first, r, mat, lay, back, first_back, tabs, other):
    outs = (FIELD, PLANE, PLANE, EDGE, EDGE, (2, 8, 128))
    return call(make_apply(first), outs, "apply", scratch=SCR, nargs=7)(
        r, mat, lay, back, first_back, tabs, other
    )


def per_device(load, mat, lay, stf, cpl, piv, fac):
    send, tabs = call(first_sweep, ((NSEG * R1, 128), TABS), "first_sweep", smem=(3, 4, 5, 6), nargs=7)(
        load, mat, lay, fac, piv, stf, cpl
    )
    fixed = exchange(send, R1)
    (back,) = call(make_owner(True), ((NSEG * R2, 128),), "owner1", nargs=3)(fixed, fixed, tabs)
    back1 = exchange(back, R2)
    u, zlow, zup, elo, ehi, da = apply_m(True, load, mat, lay, back1, back1, tabs, load)
    lo, hi = halo(elo, ehi)
    (part,) = call(operator, (FIELD,), "operator", scratch=(PLANE,), nargs=6)(u, mat, lay, zlow, zup, tabs)
    image, send, dc = call(
        second_sweep, (FIELD, (NSEG * R3, 128), (1, 8, 128)), "second_sweep", scratch=SCR, nargs=7
    )(part, lo, hi, u, mat, lay, tabs)
    recv = exchange(send, R3)
    (back,) = call(make_owner(False), ((NSEG * R3, 128),), "owner2", nargs=3)(recv, fixed, tabs)
    back2 = exchange(back, R3)
    w, zlow, zup, elo, ehi, db = apply_m(False, image, mat, lay, back2, back1, tabs, load)
    lo, hi = halo(elo, ehi)
    (part,) = call(operator, (FIELD,), "operator", scratch=(PLANE,), nargs=6)(w, mat, lay, zlow, zup, tabs)
    y, sums = call(last_dots, (FIELD, (128, 1, 128)), "last_dots", nargs=8)(part, lo, hi, u, w, da, db, dc)
    sums = lax.all_to_all(sums, ALL, 0, 0, tiled=True)
    return tuple(call(combine, (FIELD, FIELD), "combine", nargs=6)(sums, load, u, image, w, y))


def solution(mesh):
    finer = Mesh(mesh.devices.reshape(4, 2, 4, 4), ALL)
    return jax.shard_map(
        per_device,
        mesh=finer,
        in_specs=(P(GZ, None, XY, None), P(GZ, XY, None), P(GZ, XY, None), P(), P(), P(), P()),
        out_specs=(P(GZ, None, XY, None), P(GZ, None, XY, None)),
        check_vma=False,
    )
```

profile of v0, /device:TPU:1, one launch (start us, length us, event | category | flops | bytes accessed | tf_op | source)
XLA Modules:
  0.0 151.7 jit_solution(3306886622463579049)
XLA Ops:
  0.6 0.8 copy.12.cpl
  1.4 0.8 copy.9.fac
  2.2 0.8 copy.11.stf
  3.0 0.8 copy.10.piv
  3.8 1.4 copy-done
  5.2 1.0 copy-done.2
  6.2 1.0 copy-done.4
  7.2 14.4 %first_sweep.1 = (f32[1792,128]{1,0:T(8,128)S(1)}, f32[46,8,128]{2,1,0:T(8,128)S(1)}) custom-call(f32[16,4,16,384]{3,2,1,0:T(8,128)S(1)} %copy-done, s32[16,16,384]{2,1,0:T(8,128)S(1)} %copy-done.2, s32[16,16,384]{2,1,0:T(8,128)S(1)} %copy-done.4, f32[6,4,4]{2,1,0:T(4,128)S(1)} %copy.9.fac, f32[8,4,4]{2,1,0:T(4,128)S(1)} %copy.10.piv, ...), custom_call_target="tpu_custom_call" | custom-call | tf_op jit(solution)/shard_map/first_sweep/pallas_call | solution.py:406
  21.6 19.3 %all_to_all.25 = f32[8,224,128]{2,1,0:T(8,128)S(1)} all-to-all(f32[8,224,128]{2,1,0:T(8,128)S(1)} %bitcast.17), channel_id=1, replica_groups=mesh['gz_0'=4,'gz_1'=2,'xy_0'=4,'xy_1'=4] {'gz_0','gz_1'}, dimensions={0} | all-to-all | bytes 1835008 | tf_op jit(solution)/shard_map/all_to_all | solution.py:387
  40.9 0.3 owner1.1
  41.2 10.7 %all_to_all.26 = f32[8,72,128]{2,1,0:T(8,128)S(1)} all-to-all(f32[8,72,128]{2,1,0:T(8,128)S(1)} %bitcast.14), channel_id=1, replica_groups=mesh['gz_0'=4,'gz_1'=2,'xy_0'=4,'xy_1'=4] {'gz_0','gz_1'}, dimensions={0} | all-to-all | bytes 589824 | tf_op jit(solution)/shard_map/all_to_all | solution.py:387
  51.9 0.0 copy-done.1
  51.9 12.2 %apply.2 = (f32[16,4,16,384]{3,2,1,0:T(8,128)S(1)}, f32[4,16,384]{2,1,0:T(8,128)S(1)}, f32[4,16,384]{2,1,0:T(8,128)S(1)}, f32[16,4,384]{2,1,0:T(4,128)S(1)}, f32...) custom-call(f32[16,4,16,384]{3,2,1,0:T(8,128)S(1)} %copy-done.1, s32[16,16,384]{2,1,0:T(8,128)S(1)} %copy-done.2, ...), custom_call_target="tpu_custom_call" | custom-call | tf_op jit(solution)/shard_map/apply/pallas_call | solution.py:400
  64.1 3.5 %collective-permute-start = (f32[16,4,384]{2,1,0:T(4,128)S(1)}, f32[16,4,384]{2,1,0:T(4,128)S(1)}, u32[]{:S(2)}, u32[]{:S(2)}) collective-permute-start(f32[16,4,384]{2,1,0:T(4,128)S(1)} %get-tuple-element.26), channel_id=1, source_target_pairs={{0,1},{1,2},{2,3},{3,4},{4,5},{5,6},{6,7},{7,8},{8,9},{9,10},{10,1... | collective-permute-start | bytes 294920 | tf_op jit(solution)/shard_map/ppermute | solution.py:393
  67.7 1.3 collective-permute-start.1
  69.0 4.7 %operator.2.part = f32[16,4,16,384]{3,2,1,0:T(8,128)S(1)} custom-call(f32[16,4,16,384]{3,2,1,0:T(8,128)S(1)} %get-tuple-element.23.u, s32[16,16,384]{2,1,0:T(8,128)S(1)} %copy-done.2, s32[16,16,384]{2,1,0:T(8,128)S(1)} %copy-done.4, f32[4,16,384]{2,1,0:T(8,128)S(1)} %get-tuple-element.24.zlow, f32[4,16,384]{2,1,0:T(8,128)S(1)} %get-tuple-element.25.zup, ...), custom_call_target="tpu_custom_call" | custom-call | tf_op jit(solution)/shard_map/operator/pallas_call | solution.py:414
  73.7 0.0 collective-permute-done.lo
  73.7 0.0 collective-permute-done.1.hi
  73.7 11.1 %second_sweep.1 = (f32[16,4,16,384]{3,2,1,0:T(8,128)S(1)}, f32[448,128]{1,0:T(8,128)S(1)}, f32[1,8,128]{2,1,0:T(8,128)S(1)}) custom-call(f32[16,4,16,384]{3,2,1,0:T(8,128)S(1)} %operator.2.part, f32[16,4,384]{2,1,0:T(4,128)S(1)} %collective-permute-done.lo, f32[16,4,384]{2,1,0:T(4,128)S(1)} %collective-permute-done.1.hi, ...), custom_call_target="tpu_custom_call" | custom-call | tf_op jit(solution)/shard_map/second_sweep/pallas_call | solution.py:415
  84.8 9.9 %all_to_all.27 = f32[8,56,128]{2,1,0:T(8,128)S(1)} all-to-all(f32[8,56,128]{2,1,0:T(8,128)S(1)} %bitcast.19), channel_id=1, replica_groups=mesh['gz_0'=4,'gz_1'=2,'xy_0'=4,'xy_1'=4] {'gz_0','gz_1'}, dimensions={0} | all-to-all | bytes 458752 | tf_op jit(solution)/shard_map/all_to_all | solution.py:387
  94.7 0.3 owner2.1
  95.0 9.6 %all_to_all.28 = f32[8,56,128]{2,1,0:T(8,128)S(1)} all-to-all(f32[8,56,128]{2,1,0:T(8,128)S(1)} %bitcast.16), channel_id=1, replica_groups=mesh['gz_0'=4,'gz_1'=2,'xy_0'=4,'xy_1'=4] {'gz_0','gz_1'}, dimensions={0} | all-to-all | bytes 458752 | tf_op jit(solution)/shard_map/all_to_all | solution.py:387
  104.6 12.4 %apply.3 = (f32[16,4,16,384]{3,2,1,0:T(8,128)S(1)}, f32[4,16,384]{2,1,0:T(8,128)S(1)}, f32[4,16,384]{2,1,0:T(8,128)S(1)}, f32[16,4,384]{2,1,0:T(4,128)S(1)}, f32...) custom-call(f32[16,4,16,384]{3,2,1,0:T(8,128)S(1)} %get-tuple-element.28.r.image, s32[16,16,384]{2,1,0:T(8,128)S(1)} %copy-done.2, ...), custom_call_target="tpu_custom_call" | custom-call | tf_op jit(solution)/shard_map/apply/pallas_call | solution.py:400
  117.0 3.8 %collective-permute-start.2 = (f32[16,4,384]{2,1,0:T(4,128)S(1)}, f32[16,4,384]{2,1,0:T(4,128)S(1)}, u32[]{:S(2)}, u32[]{:S(2)}) collective-permute-start(f32[16,4,384]{2,1,0:T(4,128)S(1)} %get-tuple-element.33), channel_id=1, source_target_pairs={{0,1},{1,2},{2,3},{3,4},{4,5},{5,6},{6,7},{7,8},{8,9},{9,10},{10,1... | collective-permute-start | bytes 294920 | tf_op jit(solution)/shard_map/ppermute | solution.py:393
  120.8 1.3 collective-permute-start.3
  122.1 0.0 copy-done.3
  122.1 4.7 %operator.3.part = f32[16,4,16,384]{3,2,1,0:T(8,128)S(1)} custom-call(f32[16,4,16,384]{3,2,1,0:T(8,128)S(1)} %get-tuple-element.30.u.w, s32[16,16,384]{2,1,0:T(8,128)S(1)} %copy-done.3, s32[16,16,384]{2,1,0:T(8,128)S(1)} %copy-done.5, f32[4,16,384]{2,1,0:T(8,128)S(1)} %get-tuple-element.31.zlow, f32[4,16,384]{2,1,0:T(8,128)S(1)} %get-tuple-element.32.zup, ...), custom_call_target="tpu_custom_call" | custom-call | tf_op jit(solution)/shard_map/operator/pallas_call | solution.py:423
  126.9 0.0 collective-permute-done.2.lo
  126.9 0.0 collective-permute-done.3.hi
  126.9 0.7 last_dots.1
  127.6 21.6 %all_to_all.29.sums = f32[128,1,128]{2,1,0:T(1,128)S(1)} all-to-all(f32[128,1,128]{2,1,0:T(1,128)S(1)} %get-tuple-element.38), channel_id=1, replica_groups=mesh['gz_0'=4,'gz_1'=2,'xy_0'=4,'xy_1'=4] {'gz_0','gz_1','xy_0','xy_1'}, dimensions={0} | all-to-all | bytes 131072 | tf_op jit(solution)/shard_map/all_to_all | solution.py:425
  149.2 2.4 %combine.1 = (f32[16,4,16,384]{3,2,1,0:T(8,128)}, f32[16,4,16,384]{3,2,1,0:T(8,128)}) custom-call(f32[128,1,128]{2,1,0:T(1,128)S(1)} %all_to_all.29.sums, f32[16,4,16,384]{3,2,1,0:T(8,128)S(1)} %copy-done.1, f32[16,4,16,384]{3,2,1,0:T(8,128)S(1)} %get-tuple-element.23.u, f32[16,4,16,384]{3,2,1,0:T(8,128)S(1)} %get-tuple-element.28.r.image, ...), custom_call_target="tpu_custom_call" | custom-call | tf_op jit(solution)/shard_map/combine/pallas_call | solution.py:426
  (7 shorter events, 0.0 us)
Async XLA Ops:
  3.8 1.4 copy-start
  5.2 1.0 copy-start.2
  6.2 1.0 copy-start.4
  40.9 11.0 %copy-start.1 = (f32[16,4,16,384]{3,2,1,0:T(8,128)S(1)}, f32[16,4,16,384]{3,2,1,0:T(8,128)}, u32[]{:S(2)}) copy-start(f32[16,4,16,384]{3,2,1,0:T(8,128)} %r.5) | copy-start | bytes 4718596
  64.1 9.6 %collective-permute-start = (f32[16,4,384]{2,1,0:T(4,128)S(1)}, f32[16,4,384]{2,1,0:T(4,128)S(1)}, u32[]{:S(2)}, u32[]{:S(2)}) collective-permute-start(f32[16,4,384]{2,1,0:T(4,128)S(1)} %get-tuple-element.26), channel_id=1, source_target_pairs={{0,1},{1,2},{2,3},{3,4},{4,5},{5,6},{6,7},{7,8},{8,9},{9,10},{10,1... | collective-permute-start | bytes 294920 | tf_op jit(solution)/shard_map/ppermute | solution.py:393
  67.7 6.1 %collective-permute-start.1 = (f32[16,4,384]{2,1,0:T(4,128)S(1)}, f32[16,4,384]{2,1,0:T(4,128)S(1)}, u32[]{:S(2)}, u32[]{:S(2)}) collective-permute-start(f32[16,4,384]{2,1,0:T(4,128)S(1)} %get-tuple-element.27), channel_id=1, source_target_pairs={{1,0},{2,1},{3,2},{4,3},{5,4},{6,5},{7,6},{8,7},{9,8},{10,9},{11,1... | collective-permute-start | bytes 294920 | tf_op jit(solution)/shard_map/ppermute | solution.py:394
  104.6 17.6 %copy-start.3 = (s32[16,16,384]{2,1,0:T(8,128)S(1)}, s32[16,16,384]{2,1,0:T(8,128)}, u32[]{:S(2)}) copy-start(s32[16,16,384]{2,1,0:T(8,128)} %mat.11) | copy-start | bytes 1179652
  104.6 17.6 %copy-start.5 = (s32[16,16,384]{2,1,0:T(8,128)S(1)}, s32[16,16,384]{2,1,0:T(8,128)}, u32[]{:S(2)}) copy-start(s32[16,16,384]{2,1,0:T(8,128)} %lay.11) | copy-start | bytes 1179652
  117.0 9.9 %collective-permute-start.2 = (f32[16,4,384]{2,1,0:T(4,128)S(1)}, f32[16,4,384]{2,1,0:T(4,128)S(1)}, u32[]{:S(2)}, u32[]{:S(2)}) collective-permute-start(f32[16,4,384]{2,1,0:T(4,128)S(1)} %get-tuple-element.33), channel_id=1, source_target_pairs={{0,1},{1,2},{2,3},{3,4},{4,5},{5,6},{6,7},{7,8},{8,9},{9,10},{10,1... | collective-permute-start | bytes 294920 | tf_op jit(solution)/shard_map/ppermute | solution.py:393
  120.8 6.1 %collective-permute-start.3 = (f32[16,4,384]{2,1,0:T(4,128)S(1)}, f32[16,4,384]{2,1,0:T(4,128)S(1)}, u32[]{:S(2)}, u32[]{:S(2)}) collective-permute-start(f32[16,4,384]{2,1,0:T(4,128)S(1)} %get-tuple-element.34), channel_id=1, source_target_pairs={{1,0},{2,1},{3,2},{4,3},{5,4},{6,5},{7,6},{8,7},{9,8},{10,9},{11,1... | collective-permute-start | bytes 294920 | tf_op jit(solution)/shard_map/ppermute | solution.py:394
where the time goes:
time: 152 us
  blocking collectives  70.9 us (47%)
  Pallas kernels  63.4 us (42%)
  starting transfers between devices  9.95 us (7%)
  local copies, waits for them, and re-layouts  6.6 us (4%)
    all_to_all x4, blocking collectives, exchange(): buf = lax.all_to_all(buf.reshape(NSEG, per, 128), GZ, 0, 0, tiled=True)  49.4 us
    pallas_call x2, Pallas kernels, apply_m(): call(make_apply(first), outs, 'apply', scratch=SCR, nargs=7)  24.6 us
    all_to_all x1, blocking collectives, per_device(): sums = lax.all_to_all(sums, ALL, 0, 0, tiled=True)  21.6 us
    pallas_call x1, Pallas kernels, per_device(): call(first_sweep, ((NSEG * R1, 128), TABS), 'first_sweep', smem=(3, 4, 5,...  14.4 us
    pallas_call x1, Pallas kernels, per_device(): call(second_sweep, (FIELD, (NSEG * R3, 128), (1, 8, 128)), 'second_sweep'...  11.1 us
    pallas_call x2, Pallas kernels, per_device(): call(operator, (FIELD,), 'operator', scratch=(PLANE,), nargs=6)  9.46 us
    ppermute x2, starting transfers between devices, halo(): lo = lax.ppermute(ehi, XY, [(i, i + 1) for i in range(count - 1)])  7.37 us
    unnamed x16, local copies, waits for them, and re-layouts  6.6 us
  transfers between devices with their start and end apart: 4, of which 0 were waited for; matrix products, arithmetic and copies ran while one was open for 0% of the time, Pallas kernels for 6%

commit v1 on v0

--- a/solution.py
+++ b/solution.py
@@ -76,43 +76,85 @@
         for e, (i, j) in enumerate(pairs):
             row = zero
             for m in range(count):
-                row = jnp.where(lane == m, src[m, i, j], row)
+                row = jnp.where(lane == m, src[i, j, m], row)
             tabs[first + e] = row
 
 
-def first_sweep(r, mat, lay, fac, piv, stf, cpl, send, tabs):
+def first_sweep(
+    r_hbm, mat_hbm, lay_hbm, *refs
+):
+    tables, (send, tabs, r, mat, lay, st), (fac, piv, stf, cpl, sems, table_sems) = (
+        refs[:4],
+        refs[4:10],
+        refs[10:],
+    )
+    loads = [
+        pltpu.make_async_copy(src, dst, table_sems.at[e])
+        for e, (src, dst) in enumerate(zip(tables, (fac, piv, stf, cpl)))
+    ]
+    for cp in loads:
+        cp.start()
+
+    def copies(z):
+        return [
+            pltpu.make_async_copy(src.at[z], dst.at[z], sems.at[e, z])
+            for e, (src, dst) in enumerate(((r_hbm, r), (mat_hbm, mat), (lay_hbm, lay)))
+        ]
+
+    def start(z, carry):
+        for cp in copies(z):
+            cp.start()
+        return carry
+
+    lax.fori_loop(0, NZ, start, 0)
+    for cp in loads:
+        cp.wait()
     build_tables(tabs, fac, piv, stf, cpl)
+    for cp in copies(0):
+        cp.wait()
+    zero = jnp.zeros((8, 128), F32)
+    one = jnp.ones((8, 128), F32)
+    G, X, Q, W = 0, 4, 20, 30
     for n, (xi, lj) in enumerate(COLS):
         rows, lanes = tile(xi, lj)
-
-        def level(z, state):
-            g, x, q, w = state[:4], state[4:20], state[20:30], state[30:34]
-            blk = look(tabs, T_P, 16, lay[z, rows, lanes])
-            g = add([r[z, c, rows, lanes] for c in range(4)], full(blk, g))
-            xcols = [full(blk, [x[4 * j + c] for j in range(4)]) for c in range(4)]
-            piv_blk = look(tabs, T_S, 10, mat[z, rows, lanes])
-            h = symm(piv_blk, g)
-            w = [w[c] + fsum(xcols[c][i] * h[i] for i in range(4)) for c in range(4)]
-            q = list(q)
-            for c in range(4):
-                sx = symm(piv_blk, xcols[c])
-                for d in range(c + 1):
-                    e = SYMI[(d, c)]
-                    q[e] = q[e] + fsum(xcols[d][i] * sx[i] for i in range(4))
-            x = [xcols[c][j] for j in range(4) for c in range(4)]
-            return tuple(list(g) + x + q + list(w))
-
-        zero = jnp.zeros((8, 128), F32)
-        one = jnp.ones((8, 128), F32)
         g = [r[0, c, rows, lanes] for c in range(4)]
         q = look(tabs, T_S, 10, mat[0, rows, lanes])
-        w = symm(q, g)
-        x = [one if i == j else zero for i in range(4) for j in range(4)]
-        state = lax.fori_loop(1, NZ, level, tuple(g + x + q + w))
-        g, x, q, w = state[:4], state[4:20], state[20:30], state[30:34]
+        x = [one if i == c else zero for c in range(4) for i in range(4)]
+        for v, value in enumerate(g + x + q + symm(q, g)):
+            st[n, v] = value
+
+    def level(z, carry):
+        for cp in copies(z):
+            cp.wait()
+        for n, (xi, lj) in enumerate(COLS):
+            rows, lanes = tile(xi, lj)
+            blk = look(tabs, T_P, 16, lay[z, rows, lanes])
+            g = full(blk, [st[n, G + c] for c in range(4)])
+            g = add([r[z, c, rows, lanes] for c in range(4)], g)
+            for c in range(4):
+                st[n, G + c] = g[c]
+            x = [full(blk, [st[n, X + 4 * c + i] for i in range(4)]) for c in range(4)]
+            for c in range(4):
+                for i in range(4):
+                    st[n, X + 4 * c + i] = x[c][i]
+            blk = look(tabs, T_S, 10, mat[z, rows, lanes])
+            h = symm(blk, g)
+            for c in range(4):
+                st[n, W + c] += fsum(x[c][i] * h[i] for i in range(4))
+            for c in range(4):
+                sx = symm(blk, x[c])
+                for d in range(c + 1):
+                    st[n, Q + SYMI[(d, c)]] += fsum(x[d][i] * sx[i] for i in range(4))
+        return carry
+
+    lax.fori_loop(1, NZ, level, 0)
+    for n, (xi, lj) in enumerate(COLS):
+        rows, lanes = tile(xi, lj)
+        values = [st[n, v] for v in (*range(4), *range(W, W + 4))]
+        values += [st[n, X + 4 * j + i] for i in range(4) for j in range(4)]
+        values += [st[n, Q + e] for e in range(10)]
         ids = [lay[0, rows, lanes], lay[NZ - 1, rows, lanes], mat[NZ - 1, rows, lanes]]
-        values = list(g) + list(w) + list(x) + list(q) + [v.astype(F32) for v in ids]
-        for v, value in enumerate(values):
+        for v, value in enumerate(values + [d.astype(F32) for d in ids]):
             send[pl.ds(6 * v + n, 8, stride=R1), :] = value
 
 
@@ -171,53 +213,66 @@
 def make_apply(first):
     per = R2 if first else R3
 
-    def apply(r, mat, lay, back, first_back, tabs, other, u, zlow, zup, elo, ehi, dots, pscr, hscr):
-        acc_r = jnp.zeros((8, 128), F32)
-        acc_o = jnp.zeros((8, 128), F32)
+    def apply(r, mat, lay, back, first_back, tabs, other, u, zlow, zup, elo, ehi, dots, pscr, hscr, st):
+        def get(n, v, ref=back, p=per):
+            return ref[pl.ds(6 * v + n, 8, stride=p), :]
+
+        for n in range(6):
+            for c in range(4):
+                st[n, c] = get(n, c)
+
+        def up(z, carry):
+            for n, (xi, lj) in enumerate(COLS):
+                rows, lanes = tile(xi, lj)
+                blk = look(tabs, T_P, 16, lay[z, rows, lanes])
+                for e in range(16):
+                    pscr[z, n, e] = blk[e]
+                g = full(blk, [st[n, c] for c in range(4)])
+                g = add([r[z, c, rows, lanes] for c in range(4)], g)
+                for c in range(4):
+                    st[n, c] = g[c]
+                h = symm(look(tabs, T_S, 10, mat[z, rows, lanes]), g)
+                for c in range(4):
+                    hscr[z, n, c] = h[c]
+            return carry
+
+        lax.fori_loop(0, NZ, up, 0)
+        zero = jnp.zeros((8, 128), F32)
         for n, (xi, lj) in enumerate(COLS):
             rows, lanes = tile(xi, lj)
-
-            def get(v, ref=back, p=per):
-                return ref[pl.ds(6 * v + n, 8, stride=p), :]
-
-            inflow = [get(c) for c in range(4)]
-            b = [get(4 + c) for c in range(4)]
-            ids = [get(8 + e, first_back, R2).astype(I32) for e in range(3)]
-
-            def up(z, g):
-                blk = look(tabs, T_P, 16, lay[z, rows, lanes])
-                for e in range(16):
-                    pscr[z, e] = blk[e]
-                g = add([r[z, c, rows, lanes] for c in range(4)], full(blk, g))
-                h = symm(look(tabs, T_S, 10, mat[z, rows, lanes]), g)
-                for c in range(4):
-                    hscr[z, c] = h[c]
-                return tuple(g)
-
-            lax.fori_loop(0, NZ, up, tuple(inflow))
-            t = full_t(look(tabs, T_P, 16, ids[0]), b)
-
-            def down(s, carry):
-                z = NZ - 1 - s
-                t, ar, ao = carry[:4], carry[4], carry[5]
-                w = add([hscr[z, c] for c in range(4)], t)
+            b = [get(n, 4 + c) for c in range(4)]
+            t = full_t(look(tabs, T_P, 16, get(n, 8, first_back, R2).astype(I32)), b)
+            for c in range(4):
+                zup[c, rows, lanes] = b[c]
+                st[n, c] = t[c]
+
+        def down(s, carry):
+            z = NZ - 1 - s
+            ar, ao = carry
+            for n, (xi, lj) in enumerate(COLS):
+                rows, lanes = tile(xi, lj)
+                w = [hscr[z, n, c] + st[n, c] for c in range(4)]
                 for c in range(4):
                     u[z, c, rows, lanes] = w[c]
                 ar = ar + fsum(w[c] * r[z, c, rows, lanes] for c in range(4))
                 if not first:
                     ao = ao + fsum(w[c] * other[z, c, rows, lanes] for c in range(4))
-                t = full_t([pscr[z, e] for e in range(16)], w)
-                return tuple(t) + (ar, ao)
-
-            carry = lax.fori_loop(0, NZ, down, tuple(t) + (acc_r, acc_o))
-            t, acc_r, acc_o = carry[:4], carry[4], carry[5]
-            below = add(symm(look(tabs, T_S, 10, ids[2]), inflow), t)
-            pushed = symm(look(tabs, T_C, 10, ids[1]), below)
-            for c in range(4):
-                zlow[c, rows, lanes] = pushed[c]
-                zup[c, rows, lanes] = b[c]
+                t = full_t([pscr[z, n, e] for e in range(16)], w)
+                for c in range(4):
+                    st[n, c] = t[c]
+            return ar, ao
+
+        acc_r, acc_o = lax.fori_loop(0, NZ, down, (zero, zero))
         dots[0] = acc_r
         dots[1] = acc_o
+        for n, (xi, lj) in enumerate(COLS):
+            rows, lanes = tile(xi, lj)
+            lay_id, mat_id = [get(n, 9 + e, first_back, R2).astype(I32) for e in range(2)]
+            below = symm(look(tabs, T_S, 10, mat_id), [get(n, c) for c in range(4)])
+            below = add(below, [st[n, c] for c in range(4)])
+            pushed = symm(look(tabs, T_C, 10, lay_id), below)
+            for c in range(4):
+                zlow[c, rows, lanes] = pushed[c]
 
         def edges(z, carry):
             for c in range(4):
@@ -280,40 +335,49 @@
     return part[z, c, rows, lanes] - jnp.where(row == (0 if xi == 0 else 7), edge, 0.0)
 
 
-def second_sweep(part, lo, hi, u, mat, lay, tabs, image, send, dots, pscr, hscr):
+def second_sweep(part, lo, hi, u, mat, lay, tabs, image, send, dots, pscr, hscr, st):
     row = lax.broadcasted_iota(I32, (8, 128), 0)
     zero = jnp.zeros((8, 128), F32)
-    acc = zero
-    for n, (xi, lj) in enumerate(COLS):
-        rows, lanes = tile(xi, lj)
-
-        def up(z, carry):
-            g, acc = carry[:4], carry[4]
+    for n in range(6):
+        for c in range(4):
+            st[n, c] = zero
+
+    def up(z, acc):
+        for n, (xi, lj) in enumerate(COLS):
+            rows, lanes = tile(xi, lj)
             blk = look(tabs, T_P, 16, lay[z, rows, lanes])
             for e in range(16):
-                pscr[z, e] = blk[e]
+                pscr[z, n, e] = blk[e]
             img = [with_halo(part, lo, hi, z, c, xi, lj, row) for c in range(4)]
             for c in range(4):
                 image[z, c, rows, lanes] = img[c]
             acc = acc + fsum(img[c] * u[z, c, rows, lanes] for c in range(4))
-            g = add(img, full(blk, g))
+            g = add(img, full(blk, [st[n, c] for c in range(4)]))
+            for c in range(4):
+                st[n, c] = g[c]
             h = symm(look(tabs, T_S, 10, mat[z, rows, lanes]), g)
             for c in range(4):
-                hscr[z, c] = h[c]
-            return tuple(g) + (acc,)
-
-        carry = lax.fori_loop(0, NZ, up, (zero,) * 4 + (acc,))
-        g, acc = carry[:4], carry[4]
-
-        def down(s, w):
-            z = NZ - 2 - s
-            t = full_t([pscr[z + 1, e] for e in range(16)], w)
-            return tuple(add([hscr[z, c] for c in range(4)], t))
-
-        w = lax.fori_loop(0, NZ - 1, down, tuple(hscr[NZ - 1, c] for c in range(4)))
-        for v, value in enumerate(list(g) + list(w)):
-            send[pl.ds(6 * v + n, 8, stride=R3), :] = value
-    dots[0] = acc
+                hscr[z, n, c] = h[c]
+        return acc
+
+    dots[0] = lax.fori_loop(0, NZ, up, zero)
+    for n in range(6):
+        for c in range(4):
+            send[pl.ds(6 * c + n, 8, stride=R3), :] = st[n, c]
+            st[n, c] = hscr[NZ - 1, n, c]
+
+    def down(s, carry):
+        z = NZ - 2 - s
+        for n in range(6):
+            t = full_t([pscr[z + 1, n, e] for e in range(16)], [st[n, c] for c in range(4)])
+            for c in range(4):
+                st[n, c] = hscr[z, n, c] + t[c]
+        return carry
+
+    lax.fori_loop(0, NZ - 1, down, 0)
+    for n in range(6):
+        for c in range(4):
+            send[pl.ds(6 * (4 + c) + n, 8, stride=R3), :] = st[n, c]
 
 
 def last_dots(part, lo, hi, u, w, da, db, dc, y, sums):
@@ -362,15 +426,16 @@
     lax.fori_loop(0, NZ, level, 0)
 
 
-def call(body, out, name, smem=(), scratch=(), nargs=0, limit=24):
+def call(body, out, name, nargs, hbm=(), scratch=(), sems=(), limit=28):
     vm = pl.BlockSpec(memory_space=pltpu.VMEM)
-    sm = pl.BlockSpec(memory_space=pltpu.SMEM)
+    hb = pl.BlockSpec(memory_space=pltpu.HBM)
     return pl.pallas_call(
         body,
-        out_shape=[jax.ShapeDtypeStruct(s, F32) for s in out],
-        in_specs=[sm if n in smem else vm for n in range(nargs)],
+        out_shape=[s if hasattr(s, "dtype") else jax.ShapeDtypeStruct(s, F32) for s in out],
+        in_specs=[hb if n in hbm else vm for n in range(nargs)],
         out_specs=[vm for _ in out],
-        scratch_shapes=[pltpu.VMEM(s, F32) for s in scratch],
+        scratch_shapes=[s if hasattr(s, "dtype") else pltpu.VMEM(s, F32) for s in scratch]
+        + [pltpu.SemaphoreType.DMA(s) for s in sems],
         compiler_params=pltpu.CompilerParams(vmem_limit_bytes=limit * MIB),
         name=name,
     )
@@ -380,7 +445,8 @@
 EDGE = (NZ, 4, 384)
 PLANE = (4, 16, 384)
 TABS = (NTAB, 8, 128)
-SCR = ((NZ, 16, 8, 128), (NZ, 4, 8, 128))
+SCR = ((NZ, 6, 16, 8, 128), (NZ, 6, 4, 8, 128), (6, 4, 8, 128))
+IDS = jax.ShapeDtypeStruct((NZ, 16, 384), I32)
 
 
 def exchange(buf, per):
@@ -397,33 +463,45 @@
 
 def apply_m(first, r, mat, lay, back, first_back, tabs, other):
     outs = (FIELD, PLANE, PLANE, EDGE, EDGE, (2, 8, 128))
-    return call(make_apply(first), outs, "apply", scratch=SCR, nargs=7)(
+    return call(make_apply(first), outs, "apply", 7, scratch=SCR)(
         r, mat, lay, back, first_back, tabs, other
     )
 
 
+def operate(u, mat, lay, zlow, zup, tabs):
+    return call(operator, (FIELD,), "operator", 6, scratch=(PLANE,))(u, mat, lay, zlow, zup, tabs)[0]
+
+
 def per_device(load, mat, lay, stf, cpl, piv, fac):
-    send, tabs = call(first_sweep, ((NSEG * R1, 128), TABS), "first_sweep", smem=(3, 4, 5, 6), nargs=7)(
-        load, mat, lay, fac, piv, stf, cpl
-    )
+    hbm_args = [load, mat, lay] + [jnp.transpose(t, (1, 2, 0)) for t in (fac, piv, stf, cpl)]
+    hbm_args = [pltpu.with_memory_space_constraint(v, pltpu.HBM) for v in hbm_args]
+    send, tabs, load, mat, lay = call(
+        first_sweep,
+        ((NSEG * R1, 128), TABS, FIELD, IDS, IDS),
+        "first_sweep",
+        7,
+        hbm=range(7),
+        scratch=[(6, 34, 8, 128)] + [pltpu.SMEM(v.shape, F32) for v in hbm_args[3:]],
+        sems=((3, NZ), (4,)),
+    )(*hbm_args)
     fixed = exchange(send, R1)
-    (back,) = call(make_owner(True), ((NSEG * R2, 128),), "owner1", nargs=3)(fixed, fixed, tabs)
+    (back,) = call(make_owner(True), ((NSEG * R2, 128),), "owner1", 3)(fixed, fixed, tabs)
     back1 = exchange(back, R2)
     u, zlow, zup, elo, ehi, da = apply_m(True, load, mat, lay, back1, back1, tabs, load)
     lo, hi = halo(elo, ehi)
-    (part,) = call(operator, (FIELD,), "operator", scratch=(PLANE,), nargs=6)(u, mat, lay, zlow, zup, tabs)
+    part = operate(u, mat, lay, zlow, zup, tabs)
     image, send, dc = call(
-        second_sweep, (FIELD, (NSEG * R3, 128), (1, 8, 128)), "second_sweep", scratch=SCR, nargs=7
+        second_sweep, (FIELD, (NSEG * R3, 128), (1, 8, 128)), "second_sweep", 7, scratch=SCR
     )(part, lo, hi, u, mat, lay, tabs)
     recv = exchange(send, R3)
-    (back,) = call(make_owner(False), ((NSEG * R3, 128),), "owner2", nargs=3)(recv, fixed, tabs)
+    (back,) = call(make_owner(False), ((NSEG * R3, 128),), "owner2", 3)(recv, fixed, tabs)
     back2 = exchange(back, R3)
     w, zlow, zup, elo, ehi, db = apply_m(False, image, mat, lay, back2, back1, tabs, load)
     lo, hi = halo(elo, ehi)
-    (part,) = call(operator, (FIELD,), "operator", scratch=(PLANE,), nargs=6)(w, mat, lay, zlow, zup, tabs)
-    y, sums = call(last_dots, (FIELD, (128, 1, 128)), "last_dots", nargs=8)(part, lo, hi, u, w, da, db, dc)
+    part = operate(w, mat, lay, zlow, zup, tabs)
+    y, sums = call(last_dots, (FIELD, (128, 1, 128)), "last_dots", 8)(part, lo, hi, u, w, da, db, dc)
     sums = lax.all_to_all(sums, ALL, 0, 0, tiled=True)
-    return tuple(call(combine, (FIELD, FIELD), "combine", nargs=6)(sums, load, u, image, w, y))
+    return tuple(call(combine, (FIELD, FIELD), "combine", 6)(sums, load, u, image, w, y))
 
 
 def solution(mesh):

time: 152 us -> 120 us (0.79)
  Pallas kernels: 63.4 us -> 38 us
  local copies, waits for them, and re-layouts: 6.6 us -> 0 us
    pallas_call x9, Pallas kernels: 52.3 us -> 33.1 us  [the longest x2 11.4 us: apply_m(): call(make_apply(first), outs, 'apply', 7, scratch=SCR)]
    unnamed x16 -> x0, local copies, waits for them, and re-layouts: 6.6 us -> none
    pallas_call x1, Pallas kernels: 11.1 us -> 4.92 us  [per_device(): call(second_sweep, (FIELD, (NSEG * R3, 128), (1, 8, 128)), 'second_sweep'...]
  transfers between devices with their start and end apart: 4 -> 4, of which waited for: 0 -> 0; matrix products, arithmetic and copies ran while one was open for 0% -> 0% of each run, Pallas kernels for 6% -> 8%
where the time goes in v1:
time: 120 us
  blocking collectives  70.9 us (59%)
  Pallas kernels  38 us (32%)
  starting transfers between devices  9.9 us (8%)
    all_to_all x4, blocking collectives, exchange(): buf = lax.all_to_all(buf.reshape(NSEG, per, 128), GZ, 0, 0, tiled=True)  49.3 us
    all_to_all x1, blocking collectives, per_device(): sums = lax.all_to_all(sums, ALL, 0, 0, tiled=True)  21.6 us
    pallas_call x2, Pallas kernels, apply_m(): call(make_apply(first), outs, 'apply', 7, scratch=SCR)  11.4 us
    pallas_call x2, Pallas kernels, operate(): call(operator, (FIELD,), 'operator', 6, scratch=(PLANE,))  9.35 us
    pallas_call x1, Pallas kernels, per_device(): call(first_sweep, ((NSEG * R1, 128), TABS, FIELD, IDS, IDS), 'first_sweep...  8.61 us
    ppermute x2, starting transfers between devices, halo(): lo = lax.ppermute(ehi, XY, [(i, i + 1) for i in range(count - 1)])  7.32 us
    pallas_call x1, Pallas kernels, per_device(): call(second_sweep, (FIELD, (NSEG * R3, 128), (1, 8, 128)), 'second_sweep'...  4.92 us
    ppermute x2, starting transfers between devices, halo(): hi = lax.ppermute(elo, XY, [(i + 1, i) for i in range(count - 1)])  2.58 us
  transfers between devices with their start and end apart: 4, of which 0 were waited for; matrix products, arithmetic and copies ran while one was open for 0% of the time, Pallas kernels for 8%

profile of v1, /device:TPU:1, one launch (start us, length us, event | category | flops | bytes accessed | tf_op | source)
XLA Modules:
  0.0 119.7 jit_solution(15916880025483083940)
XLA Ops:
  0.6 8.6 %first_sweep.1 = (f32[1792,128]{1,0:T(8,128)S(1)}, f32[46,8,128]{2,1,0:T(8,128)S(1)}, f32[16,4,16,384]{3,2,1,0:T(8,128)S(1)}, s32[16,16,384]{2,1,0:T(8,128)S(1)}, s32[16,16,384]{2,1,0:T(8,128)S(1)}) custom-call(f32[16,4,16,384]{3,2,1,0:T(8,128)} %r_hbm.1, s32[16,16,384]{2,1,0:T(8,128)} %mat_hbm.1, s32[16,16,384]{2,1,0:T(8,128)} %lay_hbm.1, ...), custom_call_target="tpu_custom_call" | custom-call | tf_op jit(solution)/shard_map/first_sweep/pallas_call | solution.py:478
  9.3 19.3 %all_to_all.25 = f32[8,224,128]{2,1,0:T(8,128)S(1)} all-to-all(f32[8,224,128]{2,1,0:T(8,128)S(1)} %bitcast.21), channel_id=1, replica_groups=mesh['gz_0'=4,'gz_1'=2,'xy_0'=4,'xy_1'=4] {'gz_0','gz_1'}, dimensions={0} | all-to-all | bytes 1835008 | tf_op jit(solution)/shard_map/all_to_all | solution.py:453
  28.6 0.3 owner1.1
  28.9 10.5 %all_to_all.26 = f32[8,72,128]{2,1,0:T(8,128)S(1)} all-to-all(f32[8,72,128]{2,1,0:T(8,128)S(1)} %bitcast.18), channel_id=1, replica_groups=mesh['gz_0'=4,'gz_1'=2,'xy_0'=4,'xy_1'=4] {'gz_0','gz_1'}, dimensions={0} | all-to-all | bytes 589824 | tf_op jit(solution)/shard_map/all_to_all | solution.py:453
  39.4 5.6 %apply.2 = (f32[16,4,16,384]{3,2,1,0:T(8,128)S(1)}, f32[4,16,384]{2,1,0:T(8,128)S(1)}, f32[4,16,384]{2,1,0:T(8,128)S(1)}, f32[16,4,384]{2,1,0:T(4,128)S(1)}, f32...) custom-call(f32[16,4,16,384]{3,2,1,0:T(8,128)S(1)} %get-tuple-element.24.r.other, ...), custom_call_target="tpu_custom_call" | custom-call | tf_op jit(solution)/shard_map/apply/pallas_call | solution.py:466
  45.0 3.5 %collective-permute-start = (f32[16,4,384]{2,1,0:T(4,128)S(1)}, f32[16,4,384]{2,1,0:T(4,128)S(1)}, u32[]{:S(2)}, u32[]{:S(2)}) collective-permute-start(f32[16,4,384]{2,1,0:T(4,128)S(1)} %get-tuple-element.32), channel_id=1, source_target_pairs={{0,1},{1,2},{2,3},{3,4},{4,5},{5,6},{6,7},{7,8},{8,9},{9,10},{10,1... | collective-permute-start | bytes 294920 | tf_op jit(solution)/shard_map/ppermute | solution.py:459
  48.6 1.3 %collective-permute-start.1 = (f32[16,4,384]{2,1,0:T(4,128)S(1)}, f32[16,4,384]{2,1,0:T(4,128)S(1)}, u32[]{:S(2)}, u32[]{:S(2)}) collective-permute-start(f32[16,4,384]{2,1,0:T(4,128)S(1)} %get-tuple-element.33), channel_id=1, source_target_pairs={{1,0},{2,1},{3,2},{4,3},{5,4},{6,5},{7,6},{8,7},{9,8},{10,9},{11,1... | collective-permute-start | bytes 294920 | tf_op jit(solution)/shard_map/ppermute | solution.py:460
  49.9 4.7 %operator.2.part = f32[16,4,16,384]{3,2,1,0:T(8,128)S(1)} custom-call(f32[16,4,16,384]{3,2,1,0:T(8,128)S(1)} %get-tuple-element.29.u, s32[16,16,384]{2,1,0:T(8,128)S(1)} %get-tuple-element.25.mat, s32[16,16,384]{2,1,0:T(8,128)S(1)} %get-tuple-element.26.lay, f32[4,16,384]{2,1,0:T(8,128)S(1)} %get-tuple-element.30.zlow, ...), custom_call_target="tpu_custom_call" | custom-call | tf_op jit(solution)/shard_map/operator/pallas_call | solution.py:472
  54.6 0.0 collective-permute-done.lo
  54.6 0.0 collective-permute-done.1.hi
  54.6 4.9 %second_sweep.1 = (f32[16,4,16,384]{3,2,1,0:T(8,128)S(1)}, f32[448,128]{1,0:T(8,128)S(1)}, f32[1,8,128]{2,1,0:T(8,128)S(1)}) custom-call(f32[16,4,16,384]{3,2,1,0:T(8,128)S(1)} %operator.2.part, f32[16,4,384]{2,1,0:T(4,128)S(1)} %collective-permute-done.lo, f32[16,4,384]{2,1,0:T(4,128)S(1)} %collective-permute-done.1.hi, ...), custom_call_target="tpu_custom_call" | custom-call | tf_op jit(solution)/shard_map/second_sweep/pallas_call | solution.py:493
  59.5 9.9 %all_to_all.27 = f32[8,56,128]{2,1,0:T(8,128)S(1)} all-to-all(f32[8,56,128]{2,1,0:T(8,128)S(1)} %bitcast.23), channel_id=1, replica_groups=mesh['gz_0'=4,'gz_1'=2,'xy_0'=4,'xy_1'=4] {'gz_0','gz_1'}, dimensions={0} | all-to-all | bytes 458752 | tf_op jit(solution)/shard_map/all_to_all | solution.py:453
  69.4 0.3 owner2.1
  69.8 9.6 %all_to_all.28 = f32[8,56,128]{2,1,0:T(8,128)S(1)} all-to-all(f32[8,56,128]{2,1,0:T(8,128)S(1)} %bitcast.20), channel_id=1, replica_groups=mesh['gz_0'=4,'gz_1'=2,'xy_0'=4,'xy_1'=4] {'gz_0','gz_1'}, dimensions={0} | all-to-all | bytes 458752 | tf_op jit(solution)/shard_map/all_to_all | solution.py:453
  79.3 5.7 %apply.3 = (f32[16,4,16,384]{3,2,1,0:T(8,128)S(1)}, f32[4,16,384]{2,1,0:T(8,128)S(1)}, f32[4,16,384]{2,1,0:T(8,128)S(1)}, f32[16,4,384]{2,1,0:T(4,128)S(1)}, f32...) custom-call(f32[16,4,16,384]{3,2,1,0:T(8,128)S(1)} %get-tuple-element.34.r.image, ...), custom_call_target="tpu_custom_call" | custom-call | tf_op jit(solution)/shard_map/apply/pallas_call | solution.py:466
  85.1 3.8 %collective-permute-start.2 = (f32[16,4,384]{2,1,0:T(4,128)S(1)}, f32[16,4,384]{2,1,0:T(4,128)S(1)}, u32[]{:S(2)}, u32[]{:S(2)}) collective-permute-start(f32[16,4,384]{2,1,0:T(4,128)S(1)} %get-tuple-element.39), channel_id=1, source_target_pairs={{0,1},{1,2},{2,3},{3,4},{4,5},{5,6},{6,7},{7,8},{8,9},{9,10},{10,1... | collective-permute-start | bytes 294920 | tf_op jit(solution)/shard_map/ppermute | solution.py:459
  88.8 1.3 %collective-permute-start.3 = (f32[16,4,384]{2,1,0:T(4,128)S(1)}, f32[16,4,384]{2,1,0:T(4,128)S(1)}, u32[]{:S(2)}, u32[]{:S(2)}) collective-permute-start(f32[16,4,384]{2,1,0:T(4,128)S(1)} %get-tuple-element.40), channel_id=1, source_target_pairs={{1,0},{2,1},{3,2},{4,3},{5,4},{6,5},{7,6},{8,7},{9,8},{10,9},{11,1... | collective-permute-start | bytes 294920 | tf_op jit(solution)/shard_map/ppermute | solution.py:460
  90.1 4.7 %operator.3.part = f32[16,4,16,384]{3,2,1,0:T(8,128)S(1)} custom-call(f32[16,4,16,384]{3,2,1,0:T(8,128)S(1)} %get-tuple-element.36.u.w, s32[16,16,384]{2,1,0:T(8,128)S(1)} %get-tuple-element.25.mat, s32[16,16,384]{2,1,0:T(8,128)S(1)} %get-tuple-element.26.lay, f32[4,16,384]{2,1,0:T(8,128)S(1)} %get-tuple-element.37.zlow, ...), custom_call_target="tpu_custom_call" | custom-call | tf_op jit(solution)/shard_map/operator/pallas_call | solution.py:472
  94.8 0.0 collective-permute-done.2.lo
  94.8 0.0 collective-permute-done.3.hi
  94.8 0.7 last_dots.1
  95.6 21.6 %all_to_all.29.sums = f32[128,1,128]{2,1,0:T(1,128)S(1)} all-to-all(f32[128,1,128]{2,1,0:T(1,128)S(1)} %get-tuple-element.44), channel_id=1, replica_groups=mesh['gz_0'=4,'gz_1'=2,'xy_0'=4,'xy_1'=4] {'gz_0','gz_1','xy_0','xy_1'}, dimensions={0} | all-to-all | bytes 131072 | tf_op jit(solution)/shard_map/all_to_all | solution.py:503
  117.2 2.4 %combine.1 = (f32[16,4,16,384]{3,2,1,0:T(8,128)}, f32[16,4,16,384]{3,2,1,0:T(8,128)}) custom-call(f32[128,1,128]{2,1,0:T(1,128)S(1)} %all_to_all.29.sums, f32[16,4,16,384]{3,2,1,0:T(8,128)S(1)} %get-tuple-element.24.r.other, f32[16,4,16,384]{3,2,1,0:T(8,128)S(1)} %get-tuple-element.29.u, f32[16,4,16,384]{3,2,1,0:T(8,128)S(1)} %get-tuple-element.34.r.image, ...), custom_call_target="tpu_custom_call" | custom-call | tf_op jit(solution)/shard_map/combine/pallas_call | solution.py:504
Async XLA Ops:
  45.0 9.5 %collective-permute-start = (f32[16,4,384]{2,1,0:T(4,128)S(1)}, f32[16,4,384]{2,1,0:T(4,128)S(1)}, u32[]{:S(2)}, u32[]{:S(2)}) collective-permute-start(f32[16,4,384]{2,1,0:T(4,128)S(1)} %get-tuple-element.32), channel_id=1, source_target_pairs={{0,1},{1,2},{2,3},{3,4},{4,5},{5,6},{6,7},{7,8},{8,9},{9,10},{10,1... | collective-permute-start | bytes 294920 | tf_op jit(solution)/shard_map/ppermute | solution.py:459
  48.6 6.0 %collective-permute-start.1 = (f32[16,4,384]{2,1,0:T(4,128)S(1)}, f32[16,4,384]{2,1,0:T(4,128)S(1)}, u32[]{:S(2)}, u32[]{:S(2)}) collective-permute-start(f32[16,4,384]{2,1,0:T(4,128)S(1)} %get-tuple-element.33), channel_id=1, source_target_pairs={{1,0},{2,1},{3,2},{4,3},{5,4},{6,5},{7,6},{8,7},{9,8},{10,9},{11,1... | collective-permute-start | bytes 294920 | tf_op jit(solution)/shard_map/ppermute | solution.py:460
  85.1 9.8 %collective-permute-start.2 = (f32[16,4,384]{2,1,0:T(4,128)S(1)}, f32[16,4,384]{2,1,0:T(4,128)S(1)}, u32[]{:S(2)}, u32[]{:S(2)}) collective-permute-start(f32[16,4,384]{2,1,0:T(4,128)S(1)} %get-tuple-element.39), channel_id=1, source_target_pairs={{0,1},{1,2},{2,3},{3,4},{4,5},{5,6},{6,7},{7,8},{8,9},{9,10},{10,1... | collective-permute-start | bytes 294920 | tf_op jit(solution)/shard_map/ppermute | solution.py:459
  88.8 6.0 %collective-permute-start.3 = (f32[16,4,384]{2,1,0:T(4,128)S(1)}, f32[16,4,384]{2,1,0:T(4,128)S(1)}, u32[]{:S(2)}, u32[]{:S(2)}) collective-permute-start(f32[16,4,384]{2,1,0:T(4,128)S(1)} %get-tuple-element.40), channel_id=1, source_target_pairs={{1,0},{2,1},{3,2},{4,3},{5,4},{6,5},{7,6},{8,7},{9,8},{10,9},{11,1... | collective-permute-start | bytes 294920 | tf_op jit(solution)/shard_map/ppermute | solution.py:460

commit v2 on v1

--- a/solution.py
+++ b/solution.py
@@ -13,7 +13,7 @@
 I32 = jnp.int32
 
 NZ = 16
-NSEG = 8
+NSEG = 4
 COLS = [(xi, lj) for xi in range(2) for lj in range(3)]
 SYM = [(i, j) for i in range(4) for j in range(i, 4)]
 SYMI = {}
@@ -62,6 +62,21 @@
 
 def add(a, b):
     return [x + y for x, y in zip(a, b)]
+
+
+def half():
+    return lax.axis_index("gz_1")
+
+
+def put_rows(send, per, v, lj, value):
+    send[pl.ds(6 * v + lj, 4, stride=per), :] = value[:4]
+    send[pl.ds(6 * v + 3 + lj, 4, stride=per), :] = value[4:]
+
+
+def get_rows(recv, per, v, lj):
+    low = recv[pl.ds(6 * v + lj, 4, stride=per), :]
+    high = recv[pl.ds(6 * v + 3 + lj, 4, stride=per), :]
+    return jnp.concatenate([low, high], axis=0)
 
 
 def build_tables(tabs, fac, piv, stf, cpl):
@@ -83,7 +98,7 @@
 def first_sweep(
     r_hbm, mat_hbm, lay_hbm, *refs
 ):
-    tables, (send, tabs, r, mat, lay, st), (fac, piv, stf, cpl, sems, table_sems) = (
+    tables, (keep, give, tabs, r, ps, kc), (mat, lay, st, fac, piv, stf, cpl, sems, table_sems) = (
         refs[:4],
         refs[4:10],
         refs[10:],
@@ -115,10 +130,21 @@
     zero = jnp.zeros((8, 128), F32)
     one = jnp.ones((8, 128), F32)
     G, X, Q, W = 0, 4, 20, 30
+
+    def spread(z, n, rows, lanes):
+        lay_ids, mat_ids = lay[z, rows, lanes], mat[z, rows, lanes]
+        blk, piv_blk = look(tabs, T_P, 16, lay_ids), look(tabs, T_S, 10, mat_ids)
+        for e, value in enumerate(blk + piv_blk):
+            ps[z, n, e] = value
+        for e, value in enumerate(look(tabs, T_K, 10, mat_ids) + look(tabs, T_C, 10, lay_ids)):
+            kc[z, n, e] = value
+        return blk, piv_blk
+
     for n, (xi, lj) in enumerate(COLS):
         rows, lanes = tile(xi, lj)
         g = [r[0, c, rows, lanes] for c in range(4)]
-        q = look(tabs, T_S, 10, mat[0, rows, lanes])
+        spread(0, n, rows, lanes)
+        q = [ps[0, n, 16 + e] for e in range(10)]
         x = [one if i == c else zero for c in range(4) for i in range(4)]
         for v, value in enumerate(g + x + q + symm(q, g)):
             st[n, v] = value
@@ -128,7 +154,7 @@
             cp.wait()
         for n, (xi, lj) in enumerate(COLS):
             rows, lanes = tile(xi, lj)
-            blk = look(tabs, T_P, 16, lay[z, rows, lanes])
+            blk, piv_blk = spread(z, n, rows, lanes)
             g = full(blk, [st[n, G + c] for c in range(4)])
             g = add([r[z, c, rows, lanes] for c in range(4)], g)
             for c in range(4):
@@ -137,25 +163,96 @@
             for c in range(4):
                 for i in range(4):
                     st[n, X + 4 * c + i] = x[c][i]
-            blk = look(tabs, T_S, 10, mat[z, rows, lanes])
-            h = symm(blk, g)
+            h = symm(piv_blk, g)
             for c in range(4):
                 st[n, W + c] += fsum(x[c][i] * h[i] for i in range(4))
             for c in range(4):
-                sx = symm(blk, x[c])
+                sx = symm(piv_blk, x[c])
                 for d in range(c + 1):
                     st[n, Q + SYMI[(d, c)]] += fsum(x[d][i] * sx[i] for i in range(4))
         return carry
 
     lax.fori_loop(1, NZ, level, 0)
-    for n, (xi, lj) in enumerate(COLS):
-        rows, lanes = tile(xi, lj)
-        values = [st[n, v] for v in (*range(4), *range(W, W + 4))]
-        values += [st[n, X + 4 * j + i] for i in range(4) for j in range(4)]
-        values += [st[n, Q + e] for e in range(10)]
-        ids = [lay[0, rows, lanes], lay[NZ - 1, rows, lanes], mat[NZ - 1, rows, lanes]]
-        for v, value in enumerate(values + [d.astype(F32) for d in ids]):
-            send[pl.ds(6 * v + n, 8, stride=R1), :] = value
+    for core in range(2):
+
+        @pl.when(half() == core)
+        def _():
+            for n, (xi, lj) in enumerate(COLS):
+                rows, lanes = tile(xi, lj)
+                values = [st[n, v] for v in (*range(4), *range(W, W + 4))]
+                values += [st[n, X + 4 * j + i] for i in range(4) for j in range(4)]
+                values += [st[n, Q + e] for e in range(10)]
+                ids = [lay[0, rows, lanes], lay[NZ - 1, rows, lanes], mat[NZ - 1, rows, lanes]]
+                for v, value in enumerate(values + [d.astype(F32) for d in ids]):
+                    (keep if xi == core else give)[v, lj] = value
+
+
+def make_merge(first):
+    count, per = (37, R1) if first else (8, R3)
+
+    def merge(*refs):
+        if first:
+            keep, got, tabs, lu, send = refs
+            fixed = lu
+        else:
+            keep, got, fixed, tabs, lu, send = refs
+        lower = half() == 0
+        for lj in range(3):
+            for v in range(count):
+                mine, other = keep[v, lj], got[v, lj]
+                lu[0, v, lj] = jnp.where(lower, mine, other)
+                lu[1, v, lj] = jnp.where(lower, other, mine)
+            bottom = look(tabs, T_P, 16, fixed[1, 34, lj].astype(I32))
+            xl = [fixed[0, 8 + e, lj] for e in range(16)]
+            xu = [fixed[1, 8 + e, lj] for e in range(16)]
+            qu = [fixed[1, 24 + e, lj] for e in range(10)]
+            y = [full(bottom, [xl[4 * i + c] for i in range(4)]) for c in range(4)]
+            a = full(bottom, [lu[0, c, lj] for c in range(4)])
+            o = add([lu[1, c, lj] for c in range(4)], full(xu, a))
+            b = add([lu[1, 4 + c, lj] for c in range(4)], symm(qu, a))
+            w = [lu[0, 4 + c, lj] + fsum(y[c][i] * b[i] for i in range(4)) for c in range(4)]
+            values = o + w
+            if first:
+                xc = [full(xu, y[c]) for c in range(4)]
+                values += [xc[j][i] for i in range(4) for j in range(4)]
+                qy = [symm(qu, y[c]) for c in range(4)]
+                values += [
+                    fixed[0, 24 + e, lj] + fsum(y[d][i] * qy[c][i] for i in range(4))
+                    for e, (d, c) in enumerate(SYM)
+                ]
+                values += [fixed[0, 34, lj], fixed[1, 35, lj], fixed[1, 36, lj]]
+            for v, value in enumerate(values):
+                put_rows(send, per, v, lj, value)
+
+    return merge
+
+
+def make_split(first):
+    count, per = (11, R2) if first else (8, R3)
+
+    def split(lu, fixed, back, first_back, tabs, keep, give):
+        lower = half() == 0
+        for lj in range(3):
+            g0 = [get_rows(back, per, c, lj) for c in range(4)]
+            b1 = [get_rows(back, per, 4 + c, lj) for c in range(4)]
+            ids = [get_rows(first_back, R2, 8 + e, lj) for e in range(3)]
+            a0 = full(look(tabs, T_P, 16, fixed[0, 34, lj].astype(I32)), g0)
+            g1 = full([fixed[0, 8 + e, lj] for e in range(16)], a0)
+            g1 = add([lu[0, c, lj] for c in range(4)], g1)
+            a1 = full(look(tabs, T_P, 16, fixed[1, 34, lj].astype(I32)), g1)
+            t = full_t(look(tabs, T_P, 16, ids[0].astype(I32)), b1)
+            b0 = add(
+                symm([fixed[1, 24 + e, lj] for e in range(10)], a1),
+                full_t([fixed[1, 8 + e, lj] for e in range(16)], t),
+            )
+            b0 = add([lu[1, 4 + c, lj] for c in range(4)], b0)
+            low = g0 + b0 + [fixed[1, 34, lj], ids[1], ids[2]]
+            high = g1 + b1 + [ids[0], fixed[0, 35, lj], fixed[0, 36, lj]]
+            for v in range(count):
+                keep[v, lj] = jnp.where(lower, low[v], high[v])
+                give[v, lj] = jnp.where(lower, high[v], low[v])
+
+    return split
 
 
 def make_owner(first):
@@ -211,11 +308,12 @@
 
 
 def make_apply(first):
-    per = R2 if first else R3
-
-    def apply(r, mat, lay, back, first_back, tabs, other, u, zlow, zup, elo, ehi, dots, pscr, hscr, st):
-        def get(n, v, ref=back, p=per):
-            return ref[pl.ds(6 * v + n, 8, stride=p), :]
+    def apply(r, ps, keep, got, first_keep, first_got, tabs, other, u, zlow, zup, elo, ehi, dots, hscr, st):
+        core = half()
+
+        def get(n, v, own=keep, other=got):
+            xi, lj = COLS[n]
+            return jnp.where(core == xi, own[v, lj], other[v, lj])
 
         for n in range(6):
             for c in range(4):
@@ -224,14 +322,11 @@
         def up(z, carry):
             for n, (xi, lj) in enumerate(COLS):
                 rows, lanes = tile(xi, lj)
-                blk = look(tabs, T_P, 16, lay[z, rows, lanes])
-                for e in range(16):
-                    pscr[z, n, e] = blk[e]
-                g = full(blk, [st[n, c] for c in range(4)])
+                g = full([ps[z, n, e] for e in range(16)], [st[n, c] for c in range(4)])
                 g = add([r[z, c, rows, lanes] for c in range(4)], g)
                 for c in range(4):
                     st[n, c] = g[c]
-                h = symm(look(tabs, T_S, 10, mat[z, rows, lanes]), g)
+                h = symm([ps[z, n, 16 + e] for e in range(10)], g)
                 for c in range(4):
                     hscr[z, n, c] = h[c]
             return carry
@@ -241,7 +336,7 @@
         for n, (xi, lj) in enumerate(COLS):
             rows, lanes = tile(xi, lj)
             b = [get(n, 4 + c) for c in range(4)]
-            t = full_t(look(tabs, T_P, 16, get(n, 8, first_back, R2).astype(I32)), b)
+            t = full_t(look(tabs, T_P, 16, get(n, 8, first_keep, first_got).astype(I32)), b)
             for c in range(4):
                 zup[c, rows, lanes] = b[c]
                 st[n, c] = t[c]
@@ -257,7 +352,7 @@
                 ar = ar + fsum(w[c] * r[z, c, rows, lanes] for c in range(4))
                 if not first:
                     ao = ao + fsum(w[c] * other[z, c, rows, lanes] for c in range(4))
-                t = full_t([pscr[z, n, e] for e in range(16)], w)
+                t = full_t([ps[z, n, e] for e in range(16)], w)
                 for c in range(4):
                     st[n, c] = t[c]
             return ar, ao
@@ -267,7 +362,7 @@
         dots[1] = acc_o
         for n, (xi, lj) in enumerate(COLS):
             rows, lanes = tile(xi, lj)
-            lay_id, mat_id = [get(n, 9 + e, first_back, R2).astype(I32) for e in range(2)]
+            lay_id, mat_id = [get(n, 9 + e, first_keep, first_got).astype(I32) for e in range(2)]
             below = symm(look(tabs, T_S, 10, mat_id), [get(n, c) for c in range(4)])
             below = add(below, [st[n, c] for c in range(4)])
             pushed = symm(look(tabs, T_C, 10, lay_id), below)
@@ -285,7 +380,7 @@
     return apply
 
 
-def operator(u, mat, lay, zlow, zup, tabs, out, push):
+def operator(u, kc, zlow, zup, out, push):
     col = lax.broadcasted_iota(I32, (8, 384), 1)
     row = lax.broadcasted_iota(I32, (8, 384), 0)
     push[...] = zlow[...]
@@ -316,8 +411,9 @@
                     jnp.where(z == NZ - 1, zup[c, rows, lanes], u[nz, c, rows, lanes])
                     for c in range(4)
                 ]
-                kv = symm(look(tabs, T_K, 10, mat[z, rows, lanes]), v)
-                cb = look(tabs, T_C, 10, lay[z, rows, lanes])
+                n = 3 * xi + lj
+                kv = symm([kc[z, n, e] for e in range(10)], v)
+                cb = [kc[z, n, 10 + e] for e in range(10)]
                 fa = symm(cb, above)
                 fb = symm(cb, v)
                 for c in range(4):
@@ -335,7 +431,7 @@
     return part[z, c, rows, lanes] - jnp.where(row == (0 if xi == 0 else 7), edge, 0.0)
 
 
-def second_sweep(part, lo, hi, u, mat, lay, tabs, image, send, dots, pscr, hscr, st):
+def second_sweep(part, lo, hi, u, ps, image, keep, give, dots, hscr, st):
     row = lax.broadcasted_iota(I32, (8, 128), 0)
     zero = jnp.zeros((8, 128), F32)
     for n in range(6):
@@ -345,9 +441,7 @@
     def up(z, acc):
         for n, (xi, lj) in enumerate(COLS):
             rows, lanes = tile(xi, lj)
-            blk = look(tabs, T_P, 16, lay[z, rows, lanes])
-            for e in range(16):
-                pscr[z, n, e] = blk[e]
+            blk = [ps[z, n, e] for e in range(16)]
             img = [with_halo(part, lo, hi, z, c, xi, lj, row) for c in range(4)]
             for c in range(4):
                 image[z, c, rows, lanes] = img[c]
@@ -355,29 +449,42 @@
             g = add(img, full(blk, [st[n, c] for c in range(4)]))
             for c in range(4):
                 st[n, c] = g[c]
-            h = symm(look(tabs, T_S, 10, mat[z, rows, lanes]), g)
+            h = symm([ps[z, n, 16 + e] for e in range(10)], g)
             for c in range(4):
                 hscr[z, n, c] = h[c]
         return acc
 
     dots[0] = lax.fori_loop(0, NZ, up, zero)
+    up_last = []
     for n in range(6):
         for c in range(4):
-            send[pl.ds(6 * c + n, 8, stride=R3), :] = st[n, c]
+            up_last.append(st[n, c])
             st[n, c] = hscr[NZ - 1, n, c]
 
     def down(s, carry):
         z = NZ - 2 - s
         for n in range(6):
-            t = full_t([pscr[z + 1, n, e] for e in range(16)], [st[n, c] for c in range(4)])
+            t = full_t([ps[z + 1, n, e] for e in range(16)], [st[n, c] for c in range(4)])
             for c in range(4):
                 st[n, c] = hscr[z, n, c] + t[c]
         return carry
 
+    for core in range(2):
+
+        @pl.when(half() == core)
+        def _():
+            for n, (xi, lj) in enumerate(COLS):
+                for c in range(4):
+                    (keep if xi == core else give)[c, lj] = up_last[4 * n + c]
+
     lax.fori_loop(0, NZ - 1, down, 0)
-    for n in range(6):
-        for c in range(4):
-            send[pl.ds(6 * (4 + c) + n, 8, stride=R3), :] = st[n, c]
+    for core in range(2):
+
+        @pl.when(half() == core)
+        def _():
+            for n, (xi, lj) in enumerate(COLS):
+                for c in range(4):
+                    (keep if xi == core else give)[4 + c, lj] = st[n, c]
 
 
 def last_dots(part, lo, hi, u, w, da, db, dc, y, sums):
@@ -426,7 +533,7 @@
     lax.fori_loop(0, NZ, level, 0)
 
 
-def call(body, out, name, nargs, hbm=(), scratch=(), sems=(), limit=28):
+def call(body, out, name, nargs, hbm=(), scratch=(), sems=(), limit=10):
     vm = pl.BlockSpec(memory_space=pltpu.VMEM)
     hb = pl.BlockSpec(memory_space=pltpu.HBM)
     return pl.pallas_call(
@@ -445,13 +552,22 @@
 EDGE = (NZ, 4, 384)
 PLANE = (4, 16, 384)
 TABS = (NTAB, 8, 128)
-SCR = ((NZ, 6, 16, 8, 128), (NZ, 6, 4, 8, 128), (6, 4, 8, 128))
-IDS = jax.ShapeDtypeStruct((NZ, 16, 384), I32)
+SCR = ((NZ, 6, 4, 8, 128), (6, 4, 8, 128))
+PS = (NZ, 6, 26, 8, 128)
+KC = (NZ, 6, 20, 8, 128)
 
 
 def exchange(buf, per):
-    buf = lax.all_to_all(buf.reshape(NSEG, per, 128), GZ, 0, 0, tiled=True)
+    buf = lax.all_to_all(buf.reshape(NSEG, per, 128), "gz_0", 0, 0, tiled=True)
     return buf.reshape(NSEG * per, 128)
+
+
+def swap(buf):
+    return lax.ppermute(buf, "gz_1", [(0, 1), (1, 0)])
+
+
+def part_of(count):
+    return (count, 3, 8, 128)
 
 
 def halo(elo, ehi):
@@ -461,44 +577,54 @@
     return lo, hi
 
 
-def apply_m(first, r, mat, lay, back, first_back, tabs, other):
+def apply_m(first, r, ps, inflow, first_inflow, tabs, other):
     outs = (FIELD, PLANE, PLANE, EDGE, EDGE, (2, 8, 128))
-    return call(make_apply(first), outs, "apply", 7, scratch=SCR)(
-        r, mat, lay, back, first_back, tabs, other
+    return call(make_apply(first), outs, "apply", 8, scratch=SCR)(
+        r, ps, *inflow, *first_inflow, tabs, other
     )
 
 
-def operate(u, mat, lay, zlow, zup, tabs):
-    return call(operator, (FIELD,), "operator", 6, scratch=(PLANE,))(u, mat, lay, zlow, zup, tabs)[0]
+def operate(u, kc, zlow, zup):
+    return call(operator, (FIELD,), "operator", 4, scratch=(PLANE,))(u, kc, zlow, zup)[0]
 
 
 def per_device(load, mat, lay, stf, cpl, piv, fac):
     hbm_args = [load, mat, lay] + [jnp.transpose(t, (1, 2, 0)) for t in (fac, piv, stf, cpl)]
     hbm_args = [pltpu.with_memory_space_constraint(v, pltpu.HBM) for v in hbm_args]
-    send, tabs, load, mat, lay = call(
+    keep, give, tabs, load, ps, kc = call(
         first_sweep,
-        ((NSEG * R1, 128), TABS, FIELD, IDS, IDS),
+        (part_of(37), part_of(37), TABS, FIELD, PS, KC),
         "first_sweep",
         7,
         hbm=range(7),
-        scratch=[(6, 34, 8, 128)] + [pltpu.SMEM(v.shape, F32) for v in hbm_args[3:]],
+        scratch=[pltpu.VMEM(mat.shape, I32), pltpu.VMEM(lay.shape, I32), (6, 34, 8, 128)]
+        + [pltpu.SMEM(v.shape, F32) for v in hbm_args[3:]],
         sems=((3, NZ), (4,)),
     )(*hbm_args)
+    lu, send = call(make_merge(True), ((2, *part_of(37)), (NSEG * R1, 128)), "merge1", 3)(
+        keep, swap(give), tabs
+    )
     fixed = exchange(send, R1)
     (back,) = call(make_owner(True), ((NSEG * R2, 128),), "owner1", 3)(fixed, fixed, tabs)
     back1 = exchange(back, R2)
-    u, zlow, zup, elo, ehi, da = apply_m(True, load, mat, lay, back1, back1, tabs, load)
+    keep, give = call(make_split(True), (part_of(11),) * 2, "split1", 5)(lu, lu, back1, back1, tabs)
+    inflow1 = (keep, swap(give))
+    u, zlow, zup, elo, ehi, da = apply_m(True, load, ps, inflow1, inflow1, tabs, load)
     lo, hi = halo(elo, ehi)
-    part = operate(u, mat, lay, zlow, zup, tabs)
-    image, send, dc = call(
-        second_sweep, (FIELD, (NSEG * R3, 128), (1, 8, 128)), "second_sweep", 7, scratch=SCR
-    )(part, lo, hi, u, mat, lay, tabs)
+    part = operate(u, kc, zlow, zup)
+    image, keep, give, dc = call(
+        second_sweep, (FIELD, part_of(8), part_of(8), (1, 8, 128)), "second_sweep", 5, scratch=SCR
+    )(part, lo, hi, u, ps)
+    lu2, send = call(make_merge(False), ((2, *part_of(8)), (NSEG * R3, 128)), "merge2", 4)(
+        keep, swap(give), lu, tabs
+    )
     recv = exchange(send, R3)
     (back,) = call(make_owner(False), ((NSEG * R3, 128),), "owner2", 3)(recv, fixed, tabs)
     back2 = exchange(back, R3)
-    w, zlow, zup, elo, ehi, db = apply_m(False, image, mat, lay, back2, back1, tabs, load)
+    keep, give = call(make_split(False), (part_of(8),) * 2, "split2", 5)(lu2, lu, back2, back1, tabs)
+    w, zlow, zup, elo, ehi, db = apply_m(False, image, ps, (keep, swap(give)), inflow1, tabs, load)
     lo, hi = halo(elo, ehi)
-    part = operate(w, mat, lay, zlow, zup, tabs)
+    part = operate(w, kc, zlow, zup)
     y, sums = call(last_dots, (FIELD, (128, 1, 128)), "last_dots", 8)(part, lo, hi, u, w, da, db, dc)
     sums = lax.all_to_all(sums, ALL, 0, 0, tiled=True)
     return tuple(call(combine, (FIELD, FIELD), "combine", 6)(sums, load, u, image, w, y))

time: 120 us -> 106 us (0.88)
  blocking collectives: 70.9 us -> 53.9 us
  Pallas kernels: 38 us -> 24.8 us
  waiting for transfers between devices: 0.01 us -> 8.43 us
  starting transfers between devices: 9.9 us -> 17.9 us
    all_to_all x4, blocking collectives: 49.3 us -> 33.7 us  [exchange(): buf = lax.all_to_all(buf.reshape(NSEG, per, 128), 'gz_0', 0, 0, tiled=True)]
    pallas_call x6 -> x10, Pallas kernels: 34.2 us -> 21.1 us  [the longest x1 8.99 us: per_device(): call(first_sweep, (part_of(37), part_of(37), TABS, FIELD, PS, KC), 'first...]
    ppermute x0 -> x4, starting transfers between devices: none -> 8.33 us  [swap(): return lax.ppermute(buf, 'gz_1', [(0, 1), (1, 0)])]
    ppermute x0 -> x4, waiting for transfers between devices: none -> 4.32 us  [swap(): return lax.ppermute(buf, 'gz_1', [(0, 1), (1, 0)])]
    ppermute x2, waiting for transfers between devices: 0.01 us -> 4.1 us  [halo(): hi = lax.ppermute(elo, XY, [(i + 1, i) for i in range(count - 1)])]
    all_to_all x1, blocking collectives: 21.6 us -> 20.2 us  [per_device(): sums = lax.all_to_all(sums, ALL, 0, 0, tiled=True)]
  transfers between devices with their start and end apart: 4 -> 8, of which waited for: 0 -> 6; matrix products, arithmetic and copies ran while one was open for 0% -> 0% of each run, Pallas kernels for 8% -> 4%
where the time goes in v2:
time: 106 us
  blocking collectives  53.9 us (51%)
  Pallas kernels  24.8 us (23%)
  starting transfers between devices  17.9 us (17%)
  waiting for transfers between devices  8.43 us (8%)
    all_to_all x4, blocking collectives, exchange(): buf = lax.all_to_all(buf.reshape(NSEG, per, 128), 'gz_0', 0, 0, tiled=True)  33.7 us
    all_to_all x1, blocking collectives, per_device(): sums = lax.all_to_all(sums, ALL, 0, 0, tiled=True)  20.2 us
    pallas_call x1, Pallas kernels, per_device(): call(first_sweep, (part_of(37), part_of(37), TABS, FIELD, PS, KC), 'first...  8.99 us
    ppermute x4, starting transfers between devices, swap(): return lax.ppermute(buf, 'gz_1', [(0, 1), (1, 0)])  8.33 us
    ppermute x2, starting transfers between devices, halo(): lo = lax.ppermute(ehi, XY, [(i, i + 1) for i in range(count - 1)])  6.96 us
    pallas_call x2, Pallas kernels, operate(): call(operator, (FIELD,), 'operator', 4, scratch=(PLANE,))(u, kc, zlow, zup)  4.59 us
    pallas_call x2, Pallas kernels, apply_m(): call(make_apply(first), outs, 'apply', 8, scratch=SCR)  4.5 us
    ppermute x4, waiting for transfers between devices, swap(): return lax.ppermute(buf, 'gz_1', [(0, 1), (1, 0)])  4.32 us
  transfers between devices with their start and end apart: 8, of which 6 were waited for; matrix products, arithmetic and copies ran while one was open for 0% of the time, Pallas kernels for 4%

profile of v2, /device:TPU:1, one launch (start us, length us, event | category | flops | bytes accessed | tf_op | source)
XLA Modules:
  0.0 105.7 jit_solution(7150832772518500853)
XLA Ops:
  0.6 9.0 %first_sweep.1 = (f32[37,3,8,128]{3,2,1,0:T(8,128)S(1)}, f32[37,3,8,128]{3,2,1,0:T(8,128)S(1)}, f32[46,8,128]{2,1,0:T(8,128)S(1)}, f32[16,4,16,384]{3,2,1,0:T(8,...) custom-call(f32[16,4,16,384]{3,2,1,0:T(8,128)} %r_hbm.1, s32[16,16,384]{2,1,0:T(8,128)} %mat_hbm.1, ...), custom_call_target="tpu_custom_call" | custom-call | tf_op jit(solution)/shard_map/first_sweep/pallas_call | solution.py:594
  9.6 1.5 %collective-permute-start = (f32[37,3,8,128]{3,2,1,0:T(8,128)S(1)}, f32[37,3,8,128]{3,2,1,0:T(8,128)S(1)}, u32[]{:S(2)}, u32[]{:S(2)}) collective-permute-start(f32[37,3,8,128]{3,2,1,0:T(8,128)S(1)} %get-tuple-element.37), channel_id=1, source_target_pairs={{0,16},{16,0},{1,17},{17,1},{2,18},{18,2},{3,19},{19,3},{4,20},{20... | collective-permute-start | bytes 1363976 | tf_op jit(solution)/shard_map/ppermute | solution.py:566
  11.1 1.4 %collective-permute-done.refs_1_ = f32[37,3,8,128]{3,2,1,0:T(8,128)S(1)} collective-permute-done((f32[37,3,8,128]{3,2,1,0:T(8,128)S(1)}, f32[37,3,8,128]{3,2,1,0:T(8,128)S(1)}, u32[]{:S(2)}, u32[]{:S(2)}) %collective-permute-start) | collective-permute-done | bytes 454688 | tf_op jit(solution)/shard_map/ppermute | solution.py:566
  12.5 0.6 merge1.1
  13.1 12.1 %all_to_all.25 = f32[4,224,128]{2,1,0:T(8,128)S(1)} all-to-all(f32[4,224,128]{2,1,0:T(8,128)S(1)} %bitcast.20), channel_id=1, replica_groups=mesh['gz_0'=4,'gz_1'=2,'xy_0'=4,'xy_1'=4] {'gz_0'}, dimensions={0} | all-to-all | bytes 917504 | tf_op jit(solution)/shard_map/all_to_all | solution.py:561
  25.3 0.2 owner1.1
  25.4 7.3 %all_to_all.26 = f32[4,72,128]{2,1,0:T(8,128)S(1)} all-to-all(f32[4,72,128]{2,1,0:T(8,128)S(1)} %bitcast.18), channel_id=1, replica_groups=mesh['gz_0'=4,'gz_1'=2,'xy_0'=4,'xy_1'=4] {'gz_0'}, dimensions={0} | all-to-all | bytes 294912 | tf_op jit(solution)/shard_map/all_to_all | solution.py:561
  32.7 0.3 split1.1
  33.0 2.7 %collective-permute-start.1 = (f32[11,3,8,128]{3,2,1,0:T(8,128)S(1)}, f32[11,3,8,128]{3,2,1,0:T(8,128)S(1)}, u32[]{:S(2)}, u32[]{:S(2)}) collective-permute-start(f32[11,3,8,128]{3,2,1,0:T(8,128)S(1)} %get-tuple-element.42), channel_id=1, source_target_pairs={{0,16},{16,0},{1,17},{17,1},{2,18},{18,2},{3,19},{19,3},{4,20},{20... | collective-permute-start | bytes 405512 | tf_op jit(solution)/shard_map/ppermute | solution.py:566
  35.7 1.0 collective-permute-done.1.got.first_got
  36.7 2.3 %apply.2 = (f32[16,4,16,384]{3,2,1,0:T(8,128)S(1)}, f32[4,16,384]{2,1,0:T(8,128)S(1)}, f32[4,16,384]{2,1,0:T(8,128)S(1)}, f32[16,4,384]{2,1,0:T(4,128)S(1)}, f32...) custom-call(f32[16,4,16,384]{3,2,1,0:T(8,128)S(1)} %get-tuple-element.34.r.other, ...), custom_call_target="tpu_custom_call" | custom-call | tf_op jit(solution)/shard_map/apply/pallas_call | solution.py:582
  39.0 3.5 %collective-permute-start.2 = (f32[16,4,384]{2,1,0:T(4,128)S(1)}, f32[16,4,384]{2,1,0:T(4,128)S(1)}, u32[]{:S(2)}, u32[]{:S(2)}) collective-permute-start(f32[16,4,384]{2,1,0:T(4,128)S(1)} %get-tuple-element.47), channel_id=1, source_target_pairs={{0,1},{1,2},{2,3},{3,4},{4,5},{5,6},{6,7},{7,8},{8,9},{9,10},{10,1... | collective-permute-start | bytes 294920 | tf_op jit(solution)/shard_map/ppermute | solution.py:575
  42.5 1.3 %collective-permute-start.3 = (f32[16,4,384]{2,1,0:T(4,128)S(1)}, f32[16,4,384]{2,1,0:T(4,128)S(1)}, u32[]{:S(2)}, u32[]{:S(2)}) collective-permute-start(f32[16,4,384]{2,1,0:T(4,128)S(1)} %get-tuple-element.48), channel_id=1, source_target_pairs={{1,0},{2,1},{3,2},{4,3},{5,4},{6,5},{7,6},{8,7},{9,8},{10,9},{11,1... | collective-permute-start | bytes 294920 | tf_op jit(solution)/shard_map/ppermute | solution.py:576
  43.8 2.4 %operator.2.part = f32[16,4,16,384]{3,2,1,0:T(8,128)S(1)} custom-call(f32[16,4,16,384]{3,2,1,0:T(8,128)S(1)} %get-tuple-element.43.u, f32[16,6,20,8,128]{4,3,2,1,0:T(8,128)S(1)} %get-tuple-element.44.kc, f32[4,16,384]{2,1,0:T(8,128)S(1)} %get-tuple-element.45.zlow, f32[4,16,384]{2,1,0:T(8,128)S(1)} %get-tuple-element.46.zup), custom_call_target="tpu_custom_call" | custom-call | tf_op jit(solution)/shard_map/operator/pallas_call | solution.py:588
  46.2 2.3 %collective-permute-done.3.hi = f32[16,4,384]{2,1,0:T(4,128)S(1)} collective-permute-done((f32[16,4,384]{2,1,0:T(4,128)S(1)}, f32[16,4,384]{2,1,0:T(4,128)S(1)}, u32[]{:S(2)}, u32[]{:S(2)}) %collective-permute-start.3) | collective-permute-done | bytes 98336 | tf_op jit(solution)/shard_map/ppermute | solution.py:576
  48.5 1.7 %second_sweep.1 = (f32[16,4,16,384]{3,2,1,0:T(8,128)S(1)}, f32[8,3,8,128]{3,2,1,0:T(8,128)S(1)}, f32[8,3,8,128]{3,2,1,0:T(8,128)S(1)}, f32[1,8,128]{2,1,0:T(8,128)S(1)}) custom-call(f32[16,4,16,384]{3,2,1,0:T(8,128)S(1)} %operator.2.part, f32[16,4,384]{2,1,0:T(4,128)S(1)} %collective-permute-done.2.lo, f32[16,4,384]{2,1,0:T(4,128)S(1)} %collective-permute-done.3.hi, ...), custom_call_target="tpu_custom_call" | custom-call | tf_op jit(solution)/shard_map/second_sweep/pallas_call | solution.py:615
  50.2 1.4 %collective-permute-start.4 = (f32[8,3,8,128]{3,2,1,0:T(8,128)S(1)}, f32[8,3,8,128]{3,2,1,0:T(8,128)S(1)}, u32[]{:S(2)}, u32[]{:S(2)}) collective-permute-start(f32[8,3,8,128]{3,2,1,0:T(8,128)S(1)} %get-tuple-element.51), channel_id=1, source_target_pairs={{0,16},{16,0},{1,17},{17,1},{2,18},{18,2},{3,19},{19,3},{4,20},{20... | collective-permute-start | bytes 294920 | tf_op jit(solution)/shard_map/ppermute | solution.py:566
  51.6 0.9 collective-permute-done.4.refs_1_
  52.6 0.2 merge2.1
  52.7 7.1 %all_to_all.27 = f32[4,56,128]{2,1,0:T(8,128)S(1)} all-to-all(f32[4,56,128]{2,1,0:T(8,128)S(1)} %bitcast.23), channel_id=1, replica_groups=mesh['gz_0'=4,'gz_1'=2,'xy_0'=4,'xy_1'=4] {'gz_0'}, dimensions={0} | all-to-all | bytes 229376 | tf_op jit(solution)/shard_map/all_to_all | solution.py:561
  60.0 7.1 %all_to_all.28 = f32[4,56,128]{2,1,0:T(8,128)S(1)} all-to-all(f32[4,56,128]{2,1,0:T(8,128)S(1)} %bitcast.22), channel_id=1, replica_groups=mesh['gz_0'=4,'gz_1'=2,'xy_0'=4,'xy_1'=4] {'gz_0'}, dimensions={0} | all-to-all | bytes 229376 | tf_op jit(solution)/shard_map/all_to_all | solution.py:561
  67.2 0.3 split2.1
  67.4 2.7 %collective-permute-start.5 = (f32[8,3,8,128]{3,2,1,0:T(8,128)S(1)}, f32[8,3,8,128]{3,2,1,0:T(8,128)S(1)}, u32[]{:S(2)}, u32[]{:S(2)}) collective-permute-start(f32[8,3,8,128]{3,2,1,0:T(8,128)S(1)} %get-tuple-element.55), channel_id=1, source_target_pairs={{0,16},{16,0},{1,17},{17,1},{2,18},{18,2},{3,19},{19,3},{4,20},{20... | collective-permute-start | bytes 294920 | tf_op jit(solution)/shard_map/ppermute | solution.py:566
  70.2 0.9 collective-permute-done.5.got
  71.1 2.2 %apply.3 = (f32[16,4,16,384]{3,2,1,0:T(8,128)S(1)}, f32[4,16,384]{2,1,0:T(8,128)S(1)}, f32[4,16,384]{2,1,0:T(8,128)S(1)}, f32[16,4,384]{2,1,0:T(4,128)S(1)}, f32...) custom-call(f32[16,4,16,384]{3,2,1,0:T(8,128)S(1)} %get-tuple-element.49.r.image, ...), custom_call_target="tpu_custom_call" | custom-call | tf_op jit(solution)/shard_map/apply/pallas_call | solution.py:582
  73.3 3.4 %collective-permute-start.6 = (f32[16,4,384]{2,1,0:T(4,128)S(1)}, f32[16,4,384]{2,1,0:T(4,128)S(1)}, u32[]{:S(2)}, u32[]{:S(2)}) collective-permute-start(f32[16,4,384]{2,1,0:T(4,128)S(1)} %get-tuple-element.59), channel_id=1, source_target_pairs={{0,1},{1,2},{2,3},{3,4},{4,5},{5,6},{6,7},{7,8},{8,9},{9,10},{10,1... | collective-permute-start | bytes 294920 | tf_op jit(solution)/shard_map/ppermute | solution.py:575
  76.8 1.3 %collective-permute-start.7 = (f32[16,4,384]{2,1,0:T(4,128)S(1)}, f32[16,4,384]{2,1,0:T(4,128)S(1)}, u32[]{:S(2)}, u32[]{:S(2)}) collective-permute-start(f32[16,4,384]{2,1,0:T(4,128)S(1)} %get-tuple-element.60), channel_id=1, source_target_pairs={{1,0},{2,1},{3,2},{4,3},{5,4},{6,5},{7,6},{8,7},{9,8},{10,9},{11,1... | collective-permute-start | bytes 294920 | tf_op jit(solution)/shard_map/ppermute | solution.py:576
  78.1 2.2 %operator.3.part = f32[16,4,16,384]{3,2,1,0:T(8,128)S(1)} custom-call(f32[16,4,16,384]{3,2,1,0:T(8,128)S(1)} %get-tuple-element.56.u.w, f32[16,6,20,8,128]{4,3,2,1,0:T(8,128)S(1)} %get-tuple-element.44.kc, f32[4,16,384]{2,1,0:T(8,128)S(1)} %get-tuple-element.57.zlow, f32[4,16,384]{2,1,0:T(8,128)S(1)} %get-tuple-element.58.zup), custom_call_target="tpu_custom_call" | custom-call | tf_op jit(solution)/shard_map/operator/pallas_call | solution.py:588
  80.3 1.8 %collective-permute-done.7.hi = f32[16,4,384]{2,1,0:T(4,128)S(1)} collective-permute-done((f32[16,4,384]{2,1,0:T(4,128)S(1)}, f32[16,4,384]{2,1,0:T(4,128)S(1)}, u32[]{:S(2)}, u32[]{:S(2)}) %collective-permute-start.7) | collective-permute-done | bytes 98336 | tf_op jit(solution)/shard_map/ppermute | solution.py:576
  82.1 0.8 last_dots.1
  82.9 20.2 %all_to_all.29.sums = f32[128,1,128]{2,1,0:T(1,128)S(1)} all-to-all(f32[128,1,128]{2,1,0:T(1,128)S(1)} %get-tuple-element.64), channel_id=1, replica_groups=mesh['gz_0'=4,'gz_1'=2,'xy_0'=4,'xy_1'=4] {'gz_0','gz_1','xy_0','xy_1'}, dimensions={0} | all-to-all | bytes 131072 | tf_op jit(solution)/shard_map/all_to_all | solution.py:629
  103.1 2.6 %combine.1 = (f32[16,4,16,384]{3,2,1,0:T(8,128)}, f32[16,4,16,384]{3,2,1,0:T(8,128)}) custom-call(f32[128,1,128]{2,1,0:T(1,128)S(1)} %all_to_all.29.sums, f32[16,4,16,384]{3,2,1,0:T(8,128)S(1)} %get-tuple-element.34.r.other, f32[16,4,16,384]{3,2,1,0:T(8,128)S(1)} %get-tuple-element.43.u, f32[16,4,16,384]{3,2,1,0:T(8,128)S(1)} %get-tuple-element.49.r.image, ...), custom_call_target="tpu_custom_call" | custom-call | tf_op jit(solution)/shard_map/combine/pallas_call | solution.py:630
  (3 shorter events, 0.2 us)
Async XLA Ops:
  9.6 2.9 %collective-permute-start = (f32[37,3,8,128]{3,2,1,0:T(8,128)S(1)}, f32[37,3,8,128]{3,2,1,0:T(8,128)S(1)}, u32[]{:S(2)}, u32[]{:S(2)}) collective-permute-start(f32[37,3,8,128]{3,2,1,0:T(8,128)S(1)} %get-tuple-element.37), channel_id=1, source_target_pairs={{0,16},{16,0},{1,17},{17,1},{2,18},{18,2},{3,19},{19,3},{4,20},{20... | collective-permute-start | bytes 1363976 | tf_op jit(solution)/shard_map/ppermute | solution.py:566
  33.0 3.7 %collective-permute-start.1 = (f32[11,3,8,128]{3,2,1,0:T(8,128)S(1)}, f32[11,3,8,128]{3,2,1,0:T(8,128)S(1)}, u32[]{:S(2)}, u32[]{:S(2)}) collective-permute-start(f32[11,3,8,128]{3,2,1,0:T(8,128)S(1)} %get-tuple-element.42), channel_id=1, source_target_pairs={{0,16},{16,0},{1,17},{17,1},{2,18},{18,2},{3,19},{19,3},{4,20},{20... | collective-permute-start | bytes 405512 | tf_op jit(solution)/shard_map/ppermute | solution.py:566
  39.0 7.3 %collective-permute-start.2 = (f32[16,4,384]{2,1,0:T(4,128)S(1)}, f32[16,4,384]{2,1,0:T(4,128)S(1)}, u32[]{:S(2)}, u32[]{:S(2)}) collective-permute-start(f32[16,4,384]{2,1,0:T(4,128)S(1)} %get-tuple-element.47), channel_id=1, source_target_pairs={{0,1},{1,2},{2,3},{3,4},{4,5},{5,6},{6,7},{7,8},{8,9},{9,10},{10,1... | collective-permute-start | bytes 294920 | tf_op jit(solution)/shard_map/ppermute | solution.py:575
  42.5 6.0 %collective-permute-start.3 = (f32[16,4,384]{2,1,0:T(4,128)S(1)}, f32[16,4,384]{2,1,0:T(4,128)S(1)}, u32[]{:S(2)}, u32[]{:S(2)}) collective-permute-start(f32[16,4,384]{2,1,0:T(4,128)S(1)} %get-tuple-element.48), channel_id=1, source_target_pairs={{1,0},{2,1},{3,2},{4,3},{5,4},{6,5},{7,6},{8,7},{9,8},{10,9},{11,1... | collective-permute-start | bytes 294920 | tf_op jit(solution)/shard_map/ppermute | solution.py:576
  50.2 2.3 %collective-permute-start.4 = (f32[8,3,8,128]{3,2,1,0:T(8,128)S(1)}, f32[8,3,8,128]{3,2,1,0:T(8,128)S(1)}, u32[]{:S(2)}, u32[]{:S(2)}) collective-permute-start(f32[8,3,8,128]{3,2,1,0:T(8,128)S(1)} %get-tuple-element.51), channel_id=1, source_target_pairs={{0,16},{16,0},{1,17},{17,1},{2,18},{18,2},{3,19},{19,3},{4,20},{20... | collective-permute-start | bytes 294920 | tf_op jit(solution)/shard_map/ppermute | solution.py:566
  67.4 3.7 %collective-permute-start.5 = (f32[8,3,8,128]{3,2,1,0:T(8,128)S(1)}, f32[8,3,8,128]{3,2,1,0:T(8,128)S(1)}, u32[]{:S(2)}, u32[]{:S(2)}) collective-permute-start(f32[8,3,8,128]{3,2,1,0:T(8,128)S(1)} %get-tuple-element.55), channel_id=1, source_target_pairs={{0,16},{16,0},{1,17},{17,1},{2,18},{18,2},{3,19},{19,3},{4,20},{20... | collective-permute-start | bytes 294920 | tf_op jit(solution)/shard_map/ppermute | solution.py:566
  73.3 6.9 %collective-permute-start.6 = (f32[16,4,384]{2,1,0:T(4,128)S(1)}, f32[16,4,384]{2,1,0:T(4,128)S(1)}, u32[]{:S(2)}, u32[]{:S(2)}) collective-permute-start(f32[16,4,384]{2,1,0:T(4,128)S(1)} %get-tuple-element.59), channel_id=1, source_target_pairs={{0,1},{1,2},{2,3},{3,4},{4,5},{5,6},{6,7},{7,8},{8,9},{9,10},{10,1... | collective-permute-start | bytes 294920 | tf_op jit(solution)/shard_map/ppermute | solution.py:575
  76.8 5.4 %collective-permute-start.7 = (f32[16,4,384]{2,1,0:T(4,128)S(1)}, f32[16,4,384]{2,1,0:T(4,128)S(1)}, u32[]{:S(2)}, u32[]{:S(2)}) collective-permute-start(f32[16,4,384]{2,1,0:T(4,128)S(1)} %get-tuple-element.60), channel_id=1, source_target_pairs={{1,0},{2,1},{3,2},{4,3},{5,4},{6,5},{7,6},{8,7},{9,8},{10,9},{11,1... | collective-permute-start | bytes 294920 | tf_op jit(solution)/shard_map/ppermute | solution.py:576

commit v3 on v2

--- a/solution.py
+++ b/solution.py
@@ -66,6 +66,26 @@
 
 def half():
     return lax.axis_index("gz_1")
+
+
+def xy_index():
+    return lax.axis_size("xy_1") * lax.axis_index("xy_0") + lax.axis_index("xy_1")
+
+
+def block(chip, per):
+    return pl.ds(pl.multiple_of(chip * per, 8), per)
+
+
+def to_partners(blocks, outs, per):
+    me = lax.axis_index("gz_0")
+    for d, out in enumerate(outs):
+        out[...] = blocks[block(jnp.bitwise_xor(me, d), per), :]
+
+
+def from_partners(parts, blocks, per):
+    me = lax.axis_index("gz_0")
+    for d, part in enumerate(parts):
+        blocks[block(jnp.bitwise_xor(me, d), per), :] = part[...]
 
 
 def put_rows(send, per, v, lj, value):
@@ -191,11 +211,12 @@
     count, per = (37, R1) if first else (8, R3)
 
     def merge(*refs):
+        send = refs[-1]
         if first:
-            keep, got, tabs, lu, send = refs
+            keep, got, tabs, lu, *outs = refs[:-1]
             fixed = lu
         else:
-            keep, got, fixed, tabs, lu, send = refs
+            keep, got, fixed, tabs, lu, *outs = refs[:-1]
         lower = half() == 0
         for lj in range(3):
             for v in range(count):
@@ -223,6 +244,7 @@
                 values += [fixed[0, 34, lj], fixed[1, 35, lj], fixed[1, 36, lj]]
             for v, value in enumerate(values):
                 put_rows(send, per, v, lj, value)
+        to_partners(send, outs, per)
 
     return merge
 
@@ -230,7 +252,14 @@
 def make_split(first):
     count, per = (11, R2) if first else (8, R3)
 
-    def split(lu, fixed, back, first_back, tabs, keep, give):
+    def split(*refs):
+        parts = refs[:NSEG]
+        if first:
+            lu, tabs, keep, give, back = refs[NSEG:]
+            fixed, first_back = lu, back
+        else:
+            lu, fixed, first_back, tabs, keep, give, back = refs[NSEG:]
+        from_partners(parts, back, per)
         lower = half() == 0
         for lj in range(3):
             g0 = [get_rows(back, per, c, lj) for c in range(4)]
@@ -258,7 +287,16 @@
 def make_owner(first):
     out_rows = R2 if first else R3
 
-    def owner(recv, fixed, tabs, back):
+    def owner(*refs):
+        parts, back = refs[:NSEG], refs[-1]
+        if first:
+            tabs, recv, *outs = refs[NSEG:-1]
+            fixed = recv
+        else:
+            fixed, tabs, *outs = refs[NSEG:-2]
+            recv = refs[-2]
+        from_partners(parts, recv, R1 if first else R3)
+
         def get(ref, per, k, v):
             return ref[pl.ds(per * k + 6 * v, 8), :]
 
@@ -303,12 +341,13 @@
                     below = get(fixed, R1, k - 1, 35 + e)[:6] if k > 0 else none
                     back[pl.ds(R2 * k + 54 + 6 * e, 6), :] = below
                 back[pl.ds(R2 * k + 66, 6), :] = none
+        to_partners(back, outs, out_rows)
 
     return owner
 
 
 def make_apply(first):
-    def apply(r, ps, keep, got, first_keep, first_got, tabs, other, u, zlow, zup, elo, ehi, dots, hscr, st):
+    def apply(r, ps, keep, got, first_keep, first_got, tabs, other, u, zlow, zup, near, far, dots, hscr, st):
         core = half()
 
         def get(n, v, own=keep, other=got):
@@ -369,10 +408,13 @@
             for c in range(4):
                 zlow[c, rows, lanes] = pushed[c]
 
+        even = xy_index() % 2 == 0
+
         def edges(z, carry):
             for c in range(4):
-                elo[z, pl.ds(c, 1), :] = u[z, c, pl.ds(0, 1), :]
-                ehi[z, pl.ds(c, 1), :] = u[z, c, pl.ds(15, 1), :]
+                first_row, last_row = u[z, c, pl.ds(0, 1), :], u[z, c, pl.ds(15, 1), :]
+                near[z, pl.ds(c, 1), :] = jnp.where(even, last_row, first_row)
+                far[z, pl.ds(c, 1), :] = jnp.where(even, first_row, last_row)
             return carry
 
         lax.fori_loop(0, NZ, edges, 0)
@@ -425,14 +467,23 @@
     lax.fori_loop(0, NZ, level, 0)
 
 
-def with_halo(part, lo, hi, z, c, xi, lj, row):
+def halo_masks():
+    row = lax.broadcasted_iota(I32, (8, 128), 0)
+    index = xy_index()
+    last = lax.axis_size("xy_0") * lax.axis_size("xy_1") - 1
+    return index % 2 == 0, ((row == 0) & (index > 0), (row == 7) & (index < last))
+
+
+def with_halo(part, near, far, z, c, xi, lj, masks):
     rows, lanes = tile(xi, lj)
-    edge = (lo if xi == 0 else hi)[z, pl.ds(c, 1), lanes]
-    return part[z, c, rows, lanes] - jnp.where(row == (0 if xi == 0 else 7), edge, 0.0)
-
-
-def second_sweep(part, lo, hi, u, ps, image, keep, give, dots, hscr, st):
-    row = lax.broadcasted_iota(I32, (8, 128), 0)
+    even, inside = masks
+    a, b = near[z, pl.ds(c, 1), lanes], far[z, pl.ds(c, 1), lanes]
+    edge = jnp.where(even, b, a) if xi == 0 else jnp.where(even, a, b)
+    return part[z, c, rows, lanes] - jnp.where(inside[xi], edge, 0.0)
+
+
+def second_sweep(part, near, far, u, ps, image, keep, give, dots, hscr, st):
+    masks = halo_masks()
     zero = jnp.zeros((8, 128), F32)
     for n in range(6):
         for c in range(4):
@@ -442,7 +493,7 @@
         for n, (xi, lj) in enumerate(COLS):
             rows, lanes = tile(xi, lj)
             blk = [ps[z, n, e] for e in range(16)]
-            img = [with_halo(part, lo, hi, z, c, xi, lj, row) for c in range(4)]
+            img = [with_halo(part, near, far, z, c, xi, lj, masks) for c in range(4)]
             for c in range(4):
                 image[z, c, rows, lanes] = img[c]
             acc = acc + fsum(img[c] * u[z, c, rows, lanes] for c in range(4))
@@ -487,8 +538,8 @@
                     (keep if xi == core else give)[4 + c, lj] = st[n, c]
 
 
-def last_dots(part, lo, hi, u, w, da, db, dc, y, sums):
-    row = lax.broadcasted_iota(I32, (8, 128), 0)
+def last_dots(part, near, far, u, w, da, db, dc, y, sums):
+    masks = halo_masks()
     zero = jnp.zeros((8, 128), F32)
 
     def level(z, carry):
@@ -496,7 +547,7 @@
         for xi, lj in COLS:
             rows, lanes = tile(xi, lj)
             for c in range(4):
-                val = with_halo(part, lo, hi, z, c, xi, lj, row)
+                val = with_halo(part, near, far, z, c, xi, lj, masks)
                 y[z, c, rows, lanes] = val
                 au = au + val * u[z, c, rows, lanes]
                 aw = aw + val * w[z, c, rows, lanes]
@@ -557,9 +608,18 @@
 KC = (NZ, 6, 20, 8, 128)
 
 
-def exchange(buf, per):
-    buf = lax.all_to_all(buf.reshape(NSEG, per, 128), "gz_0", 0, 0, tiled=True)
-    return buf.reshape(NSEG * per, 128)
+def exchange(parts):
+    count = lax.axis_size("gz_0")
+    moved = [
+        lax.ppermute(part, "gz_0", [(i, i ^ d) for i in range(count)])
+        for d, part in enumerate(parts)
+        if d > 0
+    ]
+    return [parts[0]] + moved
+
+
+def blocks_of(per):
+    return [(per, 128)] * NSEG
 
 
 def swap(buf):
@@ -570,11 +630,11 @@
     return (count, 3, 8, 128)
 
 
-def halo(elo, ehi):
+def halo(near, far):
     count = lax.axis_size(XY)
-    lo = lax.ppermute(ehi, XY, [(i, i + 1) for i in range(count - 1)])
-    hi = lax.ppermute(elo, XY, [(i + 1, i) for i in range(count - 1)])
-    return lo, hi
+    near = lax.ppermute(near, XY, [(i, i ^ 1) for i in range(count)])
+    around = [((i + 1) % count, ((i ^ 1) + 1) % count) for i in range(count)]
+    return near, lax.ppermute(far, XY, around)
 
 
 def apply_m(first, r, ps, inflow, first_inflow, tabs, other):
@@ -601,31 +661,39 @@
         + [pltpu.SMEM(v.shape, F32) for v in hbm_args[3:]],
         sems=((3, NZ), (4,)),
     )(*hbm_args)
-    lu, send = call(make_merge(True), ((2, *part_of(37)), (NSEG * R1, 128)), "merge1", 3)(
-        keep, swap(give), tabs
-    )
-    fixed = exchange(send, R1)
-    (back,) = call(make_owner(True), ((NSEG * R2, 128),), "owner1", 3)(fixed, fixed, tabs)
-    back1 = exchange(back, R2)
-    keep, give = call(make_split(True), (part_of(11),) * 2, "split1", 5)(lu, lu, back1, back1, tabs)
+    lu, *send = call(
+        make_merge(True), ((2, *part_of(37)), *blocks_of(R1)), "merge1", 3, scratch=((NSEG * R1, 128),)
+    )(keep, swap(give), tabs)
+    fixed, *back = call(
+        make_owner(True),
+        ((NSEG * R1, 128), *blocks_of(R2)),
+        "owner1",
+        NSEG + 1,
+        scratch=((NSEG * R2, 128),),
+    )(*exchange(send), tabs)
+    keep, give, back1 = call(
+        make_split(True), (part_of(11), part_of(11), (NSEG * R2, 128)), "split1", NSEG + 2
+    )(*exchange(back), lu, tabs)
     inflow1 = (keep, swap(give))
-    u, zlow, zup, elo, ehi, da = apply_m(True, load, ps, inflow1, inflow1, tabs, load)
-    lo, hi = halo(elo, ehi)
+    u, zlow, zup, near, far, da = apply_m(True, load, ps, inflow1, inflow1, tabs, load)
+    near, far = halo(near, far)
     part = operate(u, kc, zlow, zup)
     image, keep, give, dc = call(
         second_sweep, (FIELD, part_of(8), part_of(8), (1, 8, 128)), "second_sweep", 5, scratch=SCR
-    )(part, lo, hi, u, ps)
-    lu2, send = call(make_merge(False), ((2, *part_of(8)), (NSEG * R3, 128)), "merge2", 4)(
-        keep, swap(give), lu, tabs
-    )
-    recv = exchange(send, R3)
-    (back,) = call(make_owner(False), ((NSEG * R3, 128),), "owner2", 3)(recv, fixed, tabs)
-    back2 = exchange(back, R3)
-    keep, give = call(make_split(False), (part_of(8),) * 2, "split2", 5)(lu2, lu, back2, back1, tabs)
-    w, zlow, zup, elo, ehi, db = apply_m(False, image, ps, (keep, swap(give)), inflow1, tabs, load)
-    lo, hi = halo(elo, ehi)
+    )(part, near, far, u, ps)
+    lu2, *send = call(
+        make_merge(False), ((2, *part_of(8)), *blocks_of(R3)), "merge2", 4, scratch=((NSEG * R3, 128),)
+    )(keep, swap(give), lu, tabs)
+    back = call(
+        make_owner(False), blocks_of(R3), "owner2", NSEG + 2, scratch=((NSEG * R3, 128),) * 2
+    )(*exchange(send), fixed, tabs)
+    keep, give = call(
+        make_split(False), (part_of(8),) * 2, "split2", NSEG + 4, scratch=((NSEG * R3, 128),)
+    )(*exchange(back), lu2, lu, back1, tabs)
+    w, zlow, zup, near, far, db = apply_m(False, image, ps, (keep, swap(give)), inflow1, tabs, load)
+    near, far = halo(near, far)
     part = operate(w, kc, zlow, zup)
-    y, sums = call(last_dots, (FIELD, (128, 1, 128)), "last_dots", 8)(part, lo, hi, u, w, da, db, dc)
+    y, sums = call(last_dots, (FIELD, (128, 1, 128)), "last_dots", 8)(part, near, far, u, w, da, db, dc)
     sums = lax.all_to_all(sums, ALL, 0, 0, tiled=True)
     return tuple(call(combine, (FIELD, FIELD), "combine", 6)(sums, load, u, image, w, y))
 

time: 106 us -> 100 us (0.943)
  blocking collectives: 53.9 us -> 18.4 us
  starting transfers between devices: 17.9 us -> 36.1 us
  waiting for transfers between devices: 8.43 us -> 19.9 us
    all_to_all x4 -> x0, blocking collectives: 33.7 us -> none  [exchange(): buf = lax.all_to_all(buf.reshape(NSEG, per, 128), 'gz_0', 0, 0, tiled=True)]
    ppermute x4 -> x16, starting transfers between devices: 9.54 us -> 27.1 us  [the longest x12 15.7 us: exchange(): lax.ppermute(part, 'gz_0', [(i, i ^ d) for i in range(count)])]
    ppermute x4 -> x16, waiting for transfers between devices: 4.11 us -> 15.6 us  [the longest x12 15.2 us: exchange(): lax.ppermute(part, 'gz_0', [(i, i ^ d) for i in range(count)])]
    all_to_all x1, blocking collectives: 20.2 us -> 18.4 us  [per_device(): sums = lax.all_to_all(sums, ALL, 0, 0, tiled=True)]
  transfers between devices with their start and end apart: 8 -> 20, of which waited for: 6 -> 14; matrix products, arithmetic and copies ran while one was open for 0% -> 0% of each run, Pallas kernels for 4% -> 5%
where the time goes in v3:
time: 100 us
  starting transfers between devices  36.1 us (36%)
  Pallas kernels  25 us (25%)
  waiting for transfers between devices  19.9 us (20%)
  blocking collectives  18.4 us (18%)
    all_to_all x1, blocking collectives, per_device(): sums = lax.all_to_all(sums, ALL, 0, 0, tiled=True)  18.4 us
    ppermute x12, starting transfers between devices, exchange(): lax.ppermute(part, 'gz_0', [(i, i ^ d) for i in range(count)])  15.7 us
    ppermute x12, waiting for transfers between devices, exchange(): lax.ppermute(part, 'gz_0', [(i, i ^ d) for i in range(count)])  15.2 us
    ppermute x2, starting transfers between devices, halo(): return (near, lax.ppermute(far, XY, around))  9.47 us
    ppermute x4, starting transfers between devices, swap(): return lax.ppermute(buf, 'gz_1', [(0, 1), (1, 0)])  9 us
    pallas_call x1, Pallas kernels, per_device(): call(first_sweep, (part_of(37), part_of(37), TABS, FIELD, PS, KC), 'first...  8.99 us
    pallas_call x2, Pallas kernels, operate(): call(operator, (FIELD,), 'operator', 4, scratch=(PLANE,))(u, kc, zlow, zup)  4.56 us
    pallas_call x2, Pallas kernels, apply_m(): call(make_apply(first), outs, 'apply', 8, scratch=SCR)  4.56 us
  transfers between devices with their start and end apart: 20, of which 14 were waited for; matrix products, arithmetic and copies ran while one was open for 0% of the time, Pallas kernels for 5%

profile of v3, /device:TPU:1, one launch (start us, length us, event | category | flops | bytes accessed | tf_op | source)
XLA Modules:
  0.0 100.2 jit_solution(4462352191045977230)
XLA Ops:
  0.6 9.0 %first_sweep.1 = (f32[37,3,8,128]{3,2,1,0:T(8,128)S(1)}, f32[37,3,8,128]{3,2,1,0:T(8,128)S(1)}, f32[46,8,128]{2,1,0:T(8,128)S(1)}, f32[16,4,16,384]{3,2,1,0:T(8,...) custom-call(f32[16,4,16,384]{3,2,1,0:T(8,128)} %r_hbm.1, s32[16,16,384]{2,1,0:T(8,128)} %mat_hbm.1, ...), custom_call_target="tpu_custom_call" | custom-call | tf_op jit(solution)/shard_map/first_sweep/pallas_call | solution.py:654
  9.6 1.5 %collective-permute-start = (f32[37,3,8,128]{3,2,1,0:T(8,128)S(1)}, f32[37,3,8,128]{3,2,1,0:T(8,128)S(1)}, u32[]{:S(2)}, u32[]{:S(2)}) collective-permute-start(f32[37,3,8,128]{3,2,1,0:T(8,128)S(1)} %get-tuple-element.53), channel_id=1, source_target_pairs={{0,16},{16,0},{1,17},{17,1},{2,18},{18,2},{3,19},{19,3},{4,20},{20... | collective-permute-start | bytes 1363976 | tf_op jit(solution)/shard_map/ppermute | solution.py:626
  11.1 1.4 %collective-permute-done.refs_1_ = f32[37,3,8,128]{3,2,1,0:T(8,128)S(1)} collective-permute-done((f32[37,3,8,128]{3,2,1,0:T(8,128)S(1)}, f32[37,3,8,128]{3,2,1,0:T(8,128)S(1)}, u32[]{:S(2)}, u32[]{:S(2)}) %collective-permute-start) | collective-permute-done | bytes 454688 | tf_op jit(solution)/shard_map/ppermute | solution.py:626
  13.1 1.4 %collective-permute-start.1 = (f32[224,128]{1,0:T(8,128)S(1)}, f32[224,128]{1,0:T(8,128)S(1)}, u32[]{:S(2)}, u32[]{:S(2)}) collective-permute-start(f32[224,128]{1,0:T(8,128)S(1)} %get-tuple-element.56), channel_id=1, source_target_pairs={{0,32},{32,0},{64,96},{96,64},{1,33},{33,1},{65,97},{97,65},{2,34}... | collective-permute-start | bytes 344072 | tf_op jit(solution)/shard_map/ppermute | solution.py:614
  14.5 2.5 %collective-permute-start.2 = (f32[224,128]{1,0:T(8,128)S(1)}, f32[224,128]{1,0:T(8,128)S(1)}, u32[]{:S(2)}, u32[]{:S(2)}) collective-permute-start(f32[224,128]{1,0:T(8,128)S(1)} %get-tuple-element.57), channel_id=1, source_target_pairs={{0,64},{32,96},{64,0},{96,32},{1,65},{33,97},{65,1},{97,33},{2,66}... | collective-permute-start | bytes 344072 | tf_op jit(solution)/shard_map/ppermute | solution.py:614
  17.5 4.8 %collective-permute-done.2.refs_2_ = f32[224,128]{1,0:T(8,128)S(1)} collective-permute-done((f32[224,128]{1,0:T(8,128)S(1)}, f32[224,128]{1,0:T(8,128)S(1)}, u32[]{:S(2)}, u32[]{:S(2)}) %collective-permute-start.2) | collective-permute-done | bytes 114720 | tf_op jit(solution)/shard_map/ppermute | solution.py:614
  22.3 2.6 %collective-permute-done.3.refs_3_ = f32[224,128]{1,0:T(8,128)S(1)} collective-permute-done((f32[224,128]{1,0:T(8,128)S(1)}, f32[224,128]{1,0:T(8,128)S(1)}, u32[]{:S(2)}, u32[]{:S(2)}) %collective-permute-start.3) | collective-permute-done | bytes 114720 | tf_op jit(solution)/shard_map/ppermute | solution.py:614
  25.2 1.9 %collective-permute-start.5 = (f32[72,128]{1,0:T(8,128)S(1)}, f32[72,128]{1,0:T(8,128)S(1)}, u32[]{:S(2)}, u32[]{:S(2)}) collective-permute-start(f32[72,128]{1,0:T(8,128)S(1)} %get-tuple-element.61), channel_id=1, source_target_pairs={{0,64},{32,96},{64,0},{96,32},{1,65},{33,97},{65,1},{97,33},{2,66}... | collective-permute-start | bytes 110600 | tf_op jit(solution)/shard_map/ppermute | solution.py:614
  27.1 2.0 %collective-permute-start.6 = (f32[72,128]{1,0:T(8,128)S(1)}, f32[72,128]{1,0:T(8,128)S(1)}, u32[]{:S(2)}, u32[]{:S(2)}) collective-permute-start(f32[72,128]{1,0:T(8,128)S(1)} %get-tuple-element.62), channel_id=1, source_target_pairs={{0,96},{32,64},{64,32},{96,0},{1,97},{33,65},{65,33},{97,1},{2,98}... | collective-permute-start | bytes 110600 | tf_op jit(solution)/shard_map/ppermute | solution.py:614
  29.8 1.5 %collective-permute-done.6.refs_3_ = f32[72,128]{1,0:T(8,128)S(1)} collective-permute-done((f32[72,128]{1,0:T(8,128)S(1)}, f32[72,128]{1,0:T(8,128)S(1)}, u32[]{:S(2)}, u32[]{:S(2)}) %collective-permute-start.6) | collective-permute-done | bytes 36896 | tf_op jit(solution)/shard_map/ppermute | solution.py:614
  31.5 2.1 %collective-permute-start.7 = (f32[11,3,8,128]{3,2,1,0:T(8,128)S(1)}, f32[11,3,8,128]{3,2,1,0:T(8,128)S(1)}, u32[]{:S(2)}, u32[]{:S(2)}) collective-permute-start(f32[11,3,8,128]{3,2,1,0:T(8,128)S(1)} %get-tuple-element.65), channel_id=1, source_target_pairs={{0,16},{16,0},{1,17},{17,1},{2,18},{18,2},{3,19},{19,3},{4,20},{20... | collective-permute-start | bytes 405512 | tf_op jit(solution)/shard_map/ppermute | solution.py:626
  33.7 1.0 collective-permute-done.7.got.first_got
  34.6 2.3 %apply.2 = (f32[16,4,16,384]{3,2,1,0:T(8,128)S(1)}, f32[4,16,384]{2,1,0:T(8,128)S(1)}, f32[4,16,384]{2,1,0:T(8,128)S(1)}, f32[16,4,384]{2,1,0:T(4,128)S(1)}, f32...) custom-call(f32[16,4,16,384]{3,2,1,0:T(8,128)S(1)} %get-tuple-element.50.r.other, ...), custom_call_target="tpu_custom_call" | custom-call | tf_op jit(solution)/shard_map/apply/pallas_call | solution.py:642
  37.0 1.8 %collective-permute-start.8 = (f32[16,4,384]{2,1,0:T(4,128)S(1)}, f32[16,4,384]{2,1,0:T(4,128)S(1)}, u32[]{:S(2)}, u32[]{:S(2)}) collective-permute-start(f32[16,4,384]{2,1,0:T(4,128)S(1)} %get-tuple-element.70), channel_id=1, source_target_pairs={{0,1},{1,0},{2,3},{3,2},{4,5},{5,4},{6,7},{7,6},{8,9},{9,8},{10,11... | collective-permute-start | bytes 294920 | tf_op jit(solution)/shard_map/ppermute | solution.py:635
  38.7 4.7 %collective-permute-start.9 = (f32[16,4,384]{2,1,0:T(4,128)S(1)}, f32[16,4,384]{2,1,0:T(4,128)S(1)}, u32[]{:S(2)}, u32[]{:S(2)}) collective-permute-start(f32[16,4,384]{2,1,0:T(4,128)S(1)} %get-tuple-element.71), channel_id=1, source_target_pairs={{1,2},{2,1},{3,4},{4,3},{5,6},{6,5},{7,8},{8,7},{9,10},{10,9},{11,... | collective-permute-start | bytes 294920 | tf_op jit(solution)/shard_map/ppermute | solution.py:637
  43.4 2.4 %operator.2.part = f32[16,4,16,384]{3,2,1,0:T(8,128)S(1)} custom-call(f32[16,4,16,384]{3,2,1,0:T(8,128)S(1)} %get-tuple-element.66.u, f32[16,6,20,8,128]{4,3,2,1,0:T(8,128)S(1)} %get-tuple-element.67.kc, f32[4,16,384]{2,1,0:T(8,128)S(1)} %get-tuple-element.68.zlow, f32[4,16,384]{2,1,0:T(8,128)S(1)} %get-tuple-element.69.zup), custom_call_target="tpu_custom_call" | custom-call | tf_op jit(solution)/shard_map/operator/pallas_call | solution.py:648
  45.8 1.8 %second_sweep.1 = (f32[16,4,16,384]{3,2,1,0:T(8,128)S(1)}, f32[8,3,8,128]{3,2,1,0:T(8,128)S(1)}, f32[8,3,8,128]{3,2,1,0:T(8,128)S(1)}, f32[1,8,128]{2,1,0:T(8,128)S(1)}) custom-call(f32[16,4,16,384]{3,2,1,0:T(8,128)S(1)} %operator.2.part, f32[16,4,384]{2,1,0:T(4,128)S(1)} %collective-permute-done.8.near, f32[16,4,384]{2,1,0:T(4,128)S(1)} %collective-permute-done.9.far, ...), custom_call_target="tpu_custom_call" | custom-call | tf_op jit(solution)/shard_map/second_sweep/pallas_call | solution.py:681
  47.6 1.6 %collective-permute-start.10 = (f32[8,3,8,128]{3,2,1,0:T(8,128)S(1)}, f32[8,3,8,128]{3,2,1,0:T(8,128)S(1)}, u32[]{:S(2)}, u32[]{:S(2)}) collective-permute-start(f32[8,3,8,128]{3,2,1,0:T(8,128)S(1)} %get-tuple-element.74), channel_id=1, source_target_pairs={{0,16},{16,0},{1,17},{17,1},{2,18},{18,2},{3,19},{19,3},{4,20},{20... | collective-permute-start | bytes 294920 | tf_op jit(solution)/shard_map/ppermute | solution.py:626
  49.2 0.9 collective-permute-done.10.refs_1_
  50.4 3.4 %collective-permute-start.12 = (f32[56,128]{1,0:T(8,128)S(1)}, f32[56,128]{1,0:T(8,128)S(1)}, u32[]{:S(2)}, u32[]{:S(2)}) collective-permute-start(f32[56,128]{1,0:T(8,128)S(1)} %get-tuple-element.77), channel_id=1, source_target_pairs={{0,64},{32,96},{64,0},{96,32},{1,65},{33,97},{65,1},{97,33},{2,66}... | collective-permute-start | bytes 86024 | tf_op jit(solution)/shard_map/ppermute | solution.py:614
  54.3 1.1 %collective-permute-done.12.refs_2_ = f32[56,128]{1,0:T(8,128)S(1)} collective-permute-done((f32[56,128]{1,0:T(8,128)S(1)}, f32[56,128]{1,0:T(8,128)S(1)}, u32[]{:S(2)}, u32[]{:S(2)}) %collective-permute-start.12) | collective-permute-done | bytes 28704 | tf_op jit(solution)/shard_map/ppermute | solution.py:614
  55.4 2.4 %collective-permute-done.13.refs_3_ = f32[56,128]{1,0:T(8,128)S(1)} collective-permute-done((f32[56,128]{1,0:T(8,128)S(1)}, f32[56,128]{1,0:T(8,128)S(1)}, u32[]{:S(2)}, u32[]{:S(2)}) %collective-permute-start.13) | collective-permute-done | bytes 28704 | tf_op jit(solution)/shard_map/ppermute | solution.py:614
  58.0 1.6 %collective-permute-start.15 = (f32[56,128]{1,0:T(8,128)S(1)}, f32[56,128]{1,0:T(8,128)S(1)}, u32[]{:S(2)}, u32[]{:S(2)}) collective-permute-start(f32[56,128]{1,0:T(8,128)S(1)} %get-tuple-element.82), channel_id=1, source_target_pairs={{0,64},{32,96},{64,0},{96,32},{1,65},{33,97},{65,1},{97,33},{2,66}... | collective-permute-start | bytes 86024 | tf_op jit(solution)/shard_map/ppermute | solution.py:614
  59.7 2.2 %collective-permute-start.16 = (f32[56,128]{1,0:T(8,128)S(1)}, f32[56,128]{1,0:T(8,128)S(1)}, u32[]{:S(2)}, u32[]{:S(2)}) collective-permute-start(f32[56,128]{1,0:T(8,128)S(1)} %get-tuple-element.83), channel_id=1, source_target_pairs={{0,96},{32,64},{64,32},{96,0},{1,97},{33,65},{65,33},{97,1},{2,98}... | collective-permute-start | bytes 86024 | tf_op jit(solution)/shard_map/ppermute | solution.py:614
  62.4 1.3 %collective-permute-done.16.refs_3_ = f32[56,128]{1,0:T(8,128)S(1)} collective-permute-done((f32[56,128]{1,0:T(8,128)S(1)}, f32[56,128]{1,0:T(8,128)S(1)}, u32[]{:S(2)}, u32[]{:S(2)}) %collective-permute-start.16) | collective-permute-done | bytes 28704 | tf_op jit(solution)/shard_map/ppermute | solution.py:614
  63.9 3.9 %collective-permute-start.17 = (f32[8,3,8,128]{3,2,1,0:T(8,128)S(1)}, f32[8,3,8,128]{3,2,1,0:T(8,128)S(1)}, u32[]{:S(2)}, u32[]{:S(2)}) collective-permute-start(f32[8,3,8,128]{3,2,1,0:T(8,128)S(1)} %get-tuple-element.87), channel_id=1, source_target_pairs={{0,16},{16,0},{1,17},{17,1},{2,18},{18,2},{3,19},{19,3},{4,20},{20... | collective-permute-start | bytes 294920 | tf_op jit(solution)/shard_map/ppermute | solution.py:626
  67.7 0.9 collective-permute-done.17.got
  68.7 2.3 %apply.3 = (f32[16,4,16,384]{3,2,1,0:T(8,128)S(1)}, f32[4,16,384]{2,1,0:T(8,128)S(1)}, f32[4,16,384]{2,1,0:T(8,128)S(1)}, f32[16,4,384]{2,1,0:T(4,128)S(1)}, f32...) custom-call(f32[16,4,16,384]{3,2,1,0:T(8,128)S(1)} %get-tuple-element.72.r.image, ...), custom_call_target="tpu_custom_call" | custom-call | tf_op jit(solution)/shard_map/apply/pallas_call | solution.py:642
  71.0 4.8 %collective-permute-start.19 = (f32[16,4,384]{2,1,0:T(4,128)S(1)}, f32[16,4,384]{2,1,0:T(4,128)S(1)}, u32[]{:S(2)}, u32[]{:S(2)}) collective-permute-start(f32[16,4,384]{2,1,0:T(4,128)S(1)} %get-tuple-element.92), channel_id=1, source_target_pairs={{1,2},{2,1},{3,4},{4,3},{5,6},{6,5},{7,8},{8,7},{9,10},{10,9},{11,... | collective-permute-start | bytes 294920 | tf_op jit(solution)/shard_map/ppermute | solution.py:637
  75.8 2.2 %operator.3.part = f32[16,4,16,384]{3,2,1,0:T(8,128)S(1)} custom-call(f32[16,4,16,384]{3,2,1,0:T(8,128)S(1)} %get-tuple-element.88.u.w, f32[16,6,20,8,128]{4,3,2,1,0:T(8,128)S(1)} %get-tuple-element.67.kc, f32[4,16,384]{2,1,0:T(8,128)S(1)} %get-tuple-element.89.zlow, f32[4,16,384]{2,1,0:T(8,128)S(1)} %get-tuple-element.90.zup), custom_call_target="tpu_custom_call" | custom-call | tf_op jit(solution)/shard_map/operator/pallas_call | solution.py:648
  79.2 18.4 %all_to_all.5.sums = f32[128,1,128]{2,1,0:T(1,128)S(1)} all-to-all(f32[128,1,128]{2,1,0:T(1,128)S(1)} %get-tuple-element.96), channel_id=1, replica_groups=mesh['gz_0'=4,'gz_1'=2,'xy_0'=4,'xy_1'=4] {'gz_0','gz_1','xy_0','xy_1'}, dimensions={0} | all-to-all | bytes 131072 | tf_op jit(solution)/shard_map/all_to_all | solution.py:697
  97.6 2.6 %combine.1 = (f32[16,4,16,384]{3,2,1,0:T(8,128)}, f32[16,4,16,384]{3,2,1,0:T(8,128)}) custom-call(f32[128,1,128]{2,1,0:T(1,128)S(1)} %all_to_all.5.sums, f32[16,4,16,384]{3,2,1,0:T(8,128)S(1)} %get-tuple-element.50.r.other, f32[16,4,16,384]{3,2,1,0:T(8,128)S(1)} %get-tuple-element.66.u, f32[16,4,16,384]{3,2,1,0:T(8,128)S(1)} %get-tuple-element.72.r.image, ...), custom_call_target="tpu_custom_call" | custom-call | tf_op jit(solution)/shard_map/combine/pallas_call | solution.py:698
  (23 shorter events, 5.5 us)
Async XLA Ops:
  9.6 2.9 %collective-permute-start = (f32[37,3,8,128]{3,2,1,0:T(8,128)S(1)}, f32[37,3,8,128]{3,2,1,0:T(8,128)S(1)}, u32[]{:S(2)}, u32[]{:S(2)}) collective-permute-start(f32[37,3,8,128]{3,2,1,0:T(8,128)S(1)} %get-tuple-element.53), channel_id=1, source_target_pairs={{0,16},{16,0},{1,17},{17,1},{2,18},{18,2},{3,19},{19,3},{4,20},{20... | collective-permute-start | bytes 1363976 | tf_op jit(solution)/shard_map/ppermute | solution.py:626
  13.1 4.4 %collective-permute-start.1 = (f32[224,128]{1,0:T(8,128)S(1)}, f32[224,128]{1,0:T(8,128)S(1)}, u32[]{:S(2)}, u32[]{:S(2)}) collective-permute-start(f32[224,128]{1,0:T(8,128)S(1)} %get-tuple-element.56), channel_id=1, source_target_pairs={{0,32},{32,0},{64,96},{96,64},{1,33},{33,1},{65,97},{97,65},{2,34}... | collective-permute-start | bytes 344072 | tf_op jit(solution)/shard_map/ppermute | solution.py:614
  14.5 7.8 %collective-permute-start.2 = (f32[224,128]{1,0:T(8,128)S(1)}, f32[224,128]{1,0:T(8,128)S(1)}, u32[]{:S(2)}, u32[]{:S(2)}) collective-permute-start(f32[224,128]{1,0:T(8,128)S(1)} %get-tuple-element.57), channel_id=1, source_target_pairs={{0,64},{32,96},{64,0},{96,32},{1,65},{33,97},{65,1},{97,33},{2,66}... | collective-permute-start | bytes 344072 | tf_op jit(solution)/shard_map/ppermute | solution.py:614
  17.0 7.9 %collective-permute-start.3 = (f32[224,128]{1,0:T(8,128)S(1)}, f32[224,128]{1,0:T(8,128)S(1)}, u32[]{:S(2)}, u32[]{:S(2)}) collective-permute-start(f32[224,128]{1,0:T(8,128)S(1)} %get-tuple-element.58), channel_id=1, source_target_pairs={{0,96},{32,64},{64,32},{96,0},{1,97},{33,65},{65,33},{97,1},{2,98}... | collective-permute-start | bytes 344072 | tf_op jit(solution)/shard_map/ppermute | solution.py:614
  25.1 3.9 %collective-permute-start.4 = (f32[72,128]{1,0:T(8,128)S(1)}, f32[72,128]{1,0:T(8,128)S(1)}, u32[]{:S(2)}, u32[]{:S(2)}) collective-permute-start(f32[72,128]{1,0:T(8,128)S(1)} %get-tuple-element.60), channel_id=1, source_target_pairs={{0,32},{32,0},{64,96},{96,64},{1,33},{33,1},{65,97},{97,65},{2,34}... | collective-permute-start | bytes 110600 | tf_op jit(solution)/shard_map/ppermute | solution.py:614
  25.2 4.6 %collective-permute-start.5 = (f32[72,128]{1,0:T(8,128)S(1)}, f32[72,128]{1,0:T(8,128)S(1)}, u32[]{:S(2)}, u32[]{:S(2)}) collective-permute-start(f32[72,128]{1,0:T(8,128)S(1)} %get-tuple-element.61), channel_id=1, source_target_pairs={{0,64},{32,96},{64,0},{96,32},{1,65},{33,97},{65,1},{97,33},{2,66}... | collective-permute-start | bytes 110600 | tf_op jit(solution)/shard_map/ppermute | solution.py:614
  27.1 4.2 %collective-permute-start.6 = (f32[72,128]{1,0:T(8,128)S(1)}, f32[72,128]{1,0:T(8,128)S(1)}, u32[]{:S(2)}, u32[]{:S(2)}) collective-permute-start(f32[72,128]{1,0:T(8,128)S(1)} %get-tuple-element.62), channel_id=1, source_target_pairs={{0,96},{32,64},{64,32},{96,0},{1,97},{33,65},{65,33},{97,1},{2,98}... | collective-permute-start | bytes 110600 | tf_op jit(solution)/shard_map/ppermute | solution.py:614
  31.5 3.1 %collective-permute-start.7 = (f32[11,3,8,128]{3,2,1,0:T(8,128)S(1)}, f32[11,3,8,128]{3,2,1,0:T(8,128)S(1)}, u32[]{:S(2)}, u32[]{:S(2)}) collective-permute-start(f32[11,3,8,128]{3,2,1,0:T(8,128)S(1)} %get-tuple-element.65), channel_id=1, source_target_pairs={{0,16},{16,0},{1,17},{17,1},{2,18},{18,2},{3,19},{19,3},{4,20},{20... | collective-permute-start | bytes 405512 | tf_op jit(solution)/shard_map/ppermute | solution.py:626
  37.0 8.9 %collective-permute-start.8 = (f32[16,4,384]{2,1,0:T(4,128)S(1)}, f32[16,4,384]{2,1,0:T(4,128)S(1)}, u32[]{:S(2)}, u32[]{:S(2)}) collective-permute-start(f32[16,4,384]{2,1,0:T(4,128)S(1)} %get-tuple-element.70), channel_id=1, source_target_pairs={{0,1},{1,0},{2,3},{3,2},{4,5},{5,4},{6,7},{7,6},{8,9},{9,8},{10,11... | collective-permute-start | bytes 294920 | tf_op jit(solution)/shard_map/ppermute | solution.py:635
  38.7 7.1 %collective-permute-start.9 = (f32[16,4,384]{2,1,0:T(4,128)S(1)}, f32[16,4,384]{2,1,0:T(4,128)S(1)}, u32[]{:S(2)}, u32[]{:S(2)}) collective-permute-start(f32[16,4,384]{2,1,0:T(4,128)S(1)} %get-tuple-element.71), channel_id=1, source_target_pairs={{1,2},{2,1},{3,4},{4,3},{5,6},{6,5},{7,8},{8,7},{9,10},{10,9},{11,... | collective-permute-start | bytes 294920 | tf_op jit(solution)/shard_map/ppermute | solution.py:637
  47.6 2.5 %collective-permute-start.10 = (f32[8,3,8,128]{3,2,1,0:T(8,128)S(1)}, f32[8,3,8,128]{3,2,1,0:T(8,128)S(1)}, u32[]{:S(2)}, u32[]{:S(2)}) collective-permute-start(f32[8,3,8,128]{3,2,1,0:T(8,128)S(1)} %get-tuple-element.74), channel_id=1, source_target_pairs={{0,16},{16,0},{1,17},{17,1},{2,18},{18,2},{3,19},{19,3},{4,20},{20... | collective-permute-start | bytes 294920 | tf_op jit(solution)/shard_map/ppermute | solution.py:626
  50.4 3.9 %collective-permute-start.11 = (f32[56,128]{1,0:T(8,128)S(1)}, f32[56,128]{1,0:T(8,128)S(1)}, u32[]{:S(2)}, u32[]{:S(2)}) collective-permute-start(f32[56,128]{1,0:T(8,128)S(1)} %get-tuple-element.76), channel_id=1, source_target_pairs={{0,32},{32,0},{64,96},{96,64},{1,33},{33,1},{65,97},{97,65},{2,34}... | collective-permute-start | bytes 86024 | tf_op jit(solution)/shard_map/ppermute | solution.py:614
  50.4 5.0 %collective-permute-start.12 = (f32[56,128]{1,0:T(8,128)S(1)}, f32[56,128]{1,0:T(8,128)S(1)}, u32[]{:S(2)}, u32[]{:S(2)}) collective-permute-start(f32[56,128]{1,0:T(8,128)S(1)} %get-tuple-element.77), channel_id=1, source_target_pairs={{0,64},{32,96},{64,0},{96,32},{1,65},{33,97},{65,1},{97,33},{2,66}... | collective-permute-start | bytes 86024 | tf_op jit(solution)/shard_map/ppermute | solution.py:614
  53.8 3.9 %collective-permute-start.13 = (f32[56,128]{1,0:T(8,128)S(1)}, f32[56,128]{1,0:T(8,128)S(1)}, u32[]{:S(2)}, u32[]{:S(2)}) collective-permute-start(f32[56,128]{1,0:T(8,128)S(1)} %get-tuple-element.78), channel_id=1, source_target_pairs={{0,96},{32,64},{64,32},{96,0},{1,97},{33,65},{65,33},{97,1},{2,98}... | collective-permute-start | bytes 86024 | tf_op jit(solution)/shard_map/ppermute | solution.py:614
  58.0 3.9 %collective-permute-start.14 = (f32[56,128]{1,0:T(8,128)S(1)}, f32[56,128]{1,0:T(8,128)S(1)}, u32[]{:S(2)}, u32[]{:S(2)}) collective-permute-start(f32[56,128]{1,0:T(8,128)S(1)} %get-tuple-element.81), channel_id=1, source_target_pairs={{0,32},{32,0},{64,96},{96,64},{1,33},{33,1},{65,97},{97,65},{2,34}... | collective-permute-start | bytes 86024 | tf_op jit(solution)/shard_map/ppermute | solution.py:614
  58.0 4.3 %collective-permute-start.15 = (f32[56,128]{1,0:T(8,128)S(1)}, f32[56,128]{1,0:T(8,128)S(1)}, u32[]{:S(2)}, u32[]{:S(2)}) collective-permute-start(f32[56,128]{1,0:T(8,128)S(1)} %get-tuple-element.82), channel_id=1, source_target_pairs={{0,64},{32,96},{64,0},{96,32},{1,65},{33,97},{65,1},{97,33},{2,66}... | collective-permute-start | bytes 86024 | tf_op jit(solution)/shard_map/ppermute | solution.py:614
  59.7 3.9 %collective-permute-start.16 = (f32[56,128]{1,0:T(8,128)S(1)}, f32[56,128]{1,0:T(8,128)S(1)}, u32[]{:S(2)}, u32[]{:S(2)}) collective-permute-start(f32[56,128]{1,0:T(8,128)S(1)} %get-tuple-element.83), channel_id=1, source_target_pairs={{0,96},{32,64},{64,32},{96,0},{1,97},{33,65},{65,33},{97,1},{2,98}... | collective-permute-start | bytes 86024 | tf_op jit(solution)/shard_map/ppermute | solution.py:614
  63.9 4.8 %collective-permute-start.17 = (f32[8,3,8,128]{3,2,1,0:T(8,128)S(1)}, f32[8,3,8,128]{3,2,1,0:T(8,128)S(1)}, u32[]{:S(2)}, u32[]{:S(2)}) collective-permute-start(f32[8,3,8,128]{3,2,1,0:T(8,128)S(1)} %get-tuple-element.87), channel_id=1, source_target_pairs={{0,16},{16,0},{1,17},{17,1},{2,18},{18,2},{3,19},{19,3},{4,20},{20... | collective-permute-start | bytes 294920 | tf_op jit(solution)/shard_map/ppermute | solution.py:626
  70.9 7.1 %collective-permute-start.18 = (f32[16,4,384]{2,1,0:T(4,128)S(1)}, f32[16,4,384]{2,1,0:T(4,128)S(1)}, u32[]{:S(2)}, u32[]{:S(2)}) collective-permute-start(f32[16,4,384]{2,1,0:T(4,128)S(1)} %get-tuple-element.91), channel_id=1, source_target_pairs={{0,1},{1,0},{2,3},{3,2},{4,5},{5,4},{6,7},{7,6},{8,9},{9,8},{10,11... | collective-permute-start | bytes 294920 | tf_op jit(solution)/shard_map/ppermute | solution.py:635
  71.0 7.4 %collective-permute-start.19 = (f32[16,4,384]{2,1,0:T(4,128)S(1)}, f32[16,4,384]{2,1,0:T(4,128)S(1)}, u32[]{:S(2)}, u32[]{:S(2)}) collective-permute-start(f32[16,4,384]{2,1,0:T(4,128)S(1)} %get-tuple-element.92), channel_id=1, source_target_pairs={{1,2},{2,1},{3,4},{4,3},{5,6},{6,5},{7,8},{8,7},{9,10},{10,9},{11,... | collective-permute-start | bytes 294920 | tf_op jit(solution)/shard_map/ppermute | solution.py:637

commit v4 on v3

--- a/solution.py
+++ b/solution.py
@@ -13,6 +13,7 @@
 I32 = jnp.int32
 
 NZ = 16
+CHUNK = 4
 NSEG = 4
 COLS = [(xi, lj) for xi in range(2) for lj in range(3)]
 SYM = [(i, j) for i in range(4) for j in range(i, 4)]
@@ -20,8 +21,8 @@
 for _n, (_i, _j) in enumerate(SYM):
     SYMI[(_i, _j)] = _n
     SYMI[(_j, _i)] = _n
-T_P, T_S, T_K, T_C = 0, 16, 26, 36
-NTAB = 46
+T_P, T_S, T_K, T_C, T_L = 0, 16, 26, 36, 46
+NTAB = 56
 NONE = 127
 R1, R2, R3 = 224, 72, 56
 MIB = 1 << 20
@@ -58,6 +59,10 @@
 
 def symm(blk, v):
     return [fsum(blk[SYMI[(i, j)]] * v[j] for j in range(4)) for i in range(4)]
+
+
+def lower_t(low, v):
+    return [fsum(low[SYMI[(i, j)]] * v[j] for j in range(i, 4)) for i in range(4)]
 
 
 def add(a, b):
@@ -113,15 +118,34 @@
             for m in range(count):
                 row = jnp.where(lane == m, src[i, j, m], row)
             tabs[first + e] = row
+    low = {}
+    for j in range(4):
+        diag = tabs[T_S + SYMI[(j, j)]]
+        rest = diag
+        for k in range(j):
+            rest = rest - low[(j, k)] * low[(j, k)]
+        good = rest > 1e-7 * diag
+        safe = jnp.where(good, rest, 1.0)
+        inv = lax.rsqrt(safe)
+        inv = inv * (1.5 - 0.5 * safe * inv * inv)
+        inv = jnp.where(good, inv, 0.0)
+        low[(j, j)] = safe * inv
+        for i in range(j + 1, 4):
+            part = tabs[T_S + SYMI[(i, j)]]
+            for k in range(j):
+                part = part - low[(i, k)] * low[(j, k)]
+            low[(i, j)] = part * inv
+    for (i, j), value in low.items():
+        tabs[T_L + SYMI[(i, j)]] = value
 
 
 def first_sweep(
     r_hbm, mat_hbm, lay_hbm, *refs
 ):
-    tables, (keep, give, tabs, r, ps, kc), (mat, lay, st, fac, piv, stf, cpl, sems, table_sems) = (
+    tables, (keep, give, tabs, r, mat, lay, pb), (st, fac, piv, stf, cpl, sems, table_sems) = (
         refs[:4],
-        refs[4:10],
-        refs[10:],
+        refs[4:11],
+        refs[11:],
     )
     loads = [
         pltpu.make_async_copy(src, dst, table_sems.at[e])
@@ -130,18 +154,16 @@
     for cp in loads:
         cp.start()
 
-    def copies(z):
+    def copies(part):
+        at = pl.ds(part * CHUNK, CHUNK)
         return [
-            pltpu.make_async_copy(src.at[z], dst.at[z], sems.at[e, z])
+            pltpu.make_async_copy(src.at[at], dst.at[at], sems.at[e, part])
             for e, (src, dst) in enumerate(((r_hbm, r), (mat_hbm, mat), (lay_hbm, lay)))
         ]
 
-    def start(z, carry):
-        for cp in copies(z):
+    for part in range(NZ // CHUNK):
+        for cp in copies(part):
             cp.start()
-        return carry
-
-    lax.fori_loop(0, NZ, start, 0)
     for cp in loads:
         cp.wait()
     build_tables(tabs, fac, piv, stf, cpl)
@@ -151,30 +173,32 @@
     one = jnp.ones((8, 128), F32)
     G, X, Q, W = 0, 4, 20, 30
 
-    def spread(z, n, rows, lanes):
-        lay_ids, mat_ids = lay[z, rows, lanes], mat[z, rows, lanes]
-        blk, piv_blk = look(tabs, T_P, 16, lay_ids), look(tabs, T_S, 10, mat_ids)
-        for e, value in enumerate(blk + piv_blk):
-            ps[z, n, e] = value
-        for e, value in enumerate(look(tabs, T_K, 10, mat_ids) + look(tabs, T_C, 10, lay_ids)):
-            kc[z, n, e] = value
-        return blk, piv_blk
+    def blocks(z, n, rows, lanes):
+        blk = look(tabs, T_P, 16, lay[z, rows, lanes])
+        for e in range(16):
+            pb[z, n, e] = blk[e]
+        return blk, look(tabs, T_L, 10, mat[z, rows, lanes])
 
     for n, (xi, lj) in enumerate(COLS):
         rows, lanes = tile(xi, lj)
         g = [r[0, c, rows, lanes] for c in range(4)]
-        spread(0, n, rows, lanes)
-        q = [ps[0, n, 16 + e] for e in range(10)]
+        _, low = blocks(0, n, rows, lanes)
+        q = [
+            fsum(low[SYMI[(i, k)]] * low[SYMI[(j, k)]] for k in range(min(i, j) + 1)) for i, j in SYM
+        ]
         x = [one if i == c else zero for c in range(4) for i in range(4)]
         for v, value in enumerate(g + x + q + symm(q, g)):
             st[n, v] = value
 
     def level(z, carry):
-        for cp in copies(z):
-            cp.wait()
+        @pl.when(z % CHUNK == 0)
+        def _():
+            for cp in copies(z // CHUNK):
+                cp.wait()
+
         for n, (xi, lj) in enumerate(COLS):
             rows, lanes = tile(xi, lj)
-            blk, piv_blk = spread(z, n, rows, lanes)
+            blk, piv_blk = blocks(z, n, rows, lanes)
             g = full(blk, [st[n, G + c] for c in range(4)])
             g = add([r[z, c, rows, lanes] for c in range(4)], g)
             for c in range(4):
@@ -183,13 +207,13 @@
             for c in range(4):
                 for i in range(4):
                     st[n, X + 4 * c + i] = x[c][i]
-            h = symm(piv_blk, g)
+            h = lower_t(piv_blk, g)
+            x = [lower_t(piv_blk, x[c]) for c in range(4)]
             for c in range(4):
                 st[n, W + c] += fsum(x[c][i] * h[i] for i in range(4))
             for c in range(4):
-                sx = symm(piv_blk, x[c])
                 for d in range(c + 1):
-                    st[n, Q + SYMI[(d, c)]] += fsum(x[d][i] * sx[i] for i in range(4))
+                    st[n, Q + SYMI[(d, c)]] += fsum(x[d][i] * x[c][i] for i in range(4))
         return carry
 
     lax.fori_loop(1, NZ, level, 0)
@@ -205,6 +229,22 @@
                 ids = [lay[0, rows, lanes], lay[NZ - 1, rows, lanes], mat[NZ - 1, rows, lanes]]
                 for v, value in enumerate(values + [d.astype(F32) for d in ids]):
                     (keep if xi == core else give)[v, lj] = value
+
+
+def expand(mat, lay, tabs, after, sb, kc, token):
+    token[...] = after[:8]
+
+    def level(z, carry):
+        for n, (xi, lj) in enumerate(COLS):
+            rows, lanes = tile(xi, lj)
+            lay_ids, mat_ids = lay[z, rows, lanes], mat[z, rows, lanes]
+            for e, value in enumerate(look(tabs, T_S, 10, mat_ids)):
+                sb[z, n, e] = value
+            for e, value in enumerate(look(tabs, T_K, 10, mat_ids) + look(tabs, T_C, 10, lay_ids)):
+                kc[z, n, e] = value
+        return carry
+
+    lax.fori_loop(0, NZ, level, 0)
 
 
 def make_merge(first):
@@ -290,7 +330,7 @@
     def owner(*refs):
         parts, back = refs[:NSEG], refs[-1]
         if first:
-            tabs, recv, *outs = refs[NSEG:-1]
+            tabs, _, recv, *outs = refs[NSEG:-1]
             fixed = recv
         else:
             fixed, tabs, *outs = refs[NSEG:-2]
@@ -347,7 +387,7 @@
 
 
 def make_apply(first):
-    def apply(r, ps, keep, got, first_keep, first_got, tabs, other, u, zlow, zup, near, far, dots, hscr, st):
+    def apply(r, pb, sb, keep, got, first_keep, first_got, tabs, other, u, zlow, zup, near, far, dots, hscr, st):
         core = half()
 
         def get(n, v, own=keep, other=got):
@@ -361,11 +401,11 @@
         def up(z, carry):
             for n, (xi, lj) in enumerate(COLS):
                 rows, lanes = tile(xi, lj)
-                g = full([ps[z, n, e] for e in range(16)], [st[n, c] for c in range(4)])
+                g = full([pb[z, n, e] for e in range(16)], [st[n, c] for c in range(4)])
                 g = add([r[z, c, rows, lanes] for c in range(4)], g)
                 for c in range(4):
                     st[n, c] = g[c]
-                h = symm([ps[z, n, 16 + e] for e in range(10)], g)
+                h = symm([sb[z, n, e] for e in range(10)], g)
                 for c in range(4):
                     hscr[z, n, c] = h[c]
             return carry
@@ -391,7 +431,7 @@
                 ar = ar + fsum(w[c] * r[z, c, rows, lanes] for c in range(4))
                 if not first:
                     ao = ao + fsum(w[c] * other[z, c, rows, lanes] for c in range(4))
-                t = full_t([ps[z, n, e] for e in range(16)], w)
+                t = full_t([pb[z, n, e] for e in range(16)], w)
                 for c in range(4):
                     st[n, c] = t[c]
             return ar, ao
@@ -422,12 +462,12 @@
     return apply
 
 
-def operator(u, kc, zlow, zup, out, push):
+def operator(u, kc, zlow, zup, out, dots, push):
     col = lax.broadcasted_iota(I32, (8, 384), 1)
     row = lax.broadcasted_iota(I32, (8, 384), 0)
     push[...] = zlow[...]
 
-    def level(z, carry):
+    def level(z, acc):
         for xi in range(2):
             rows = pl.ds(8 * xi, 8)
             side = []
@@ -458,13 +498,24 @@
                 cb = [kc[z, n, 10 + e] for e in range(10)]
                 fa = symm(cb, above)
                 fb = symm(cb, v)
+                val = []
                 for c in range(4):
                     near = side[c][:, 128 * lj : 128 * (lj + 1)]
-                    out[z, c, rows, lanes] = kv[c] - near - fa[c] - push[c, rows, lanes]
+                    val.append(kv[c] - near - fa[c] - push[c, rows, lanes])
+                    out[z, c, rows, lanes] = val[c]
                     push[c, rows, lanes] = fb[c]
-        return carry
-
-    lax.fori_loop(0, NZ, level, 0)
+                acc = acc + fsum(val[c] * v[c] for c in range(4))
+        return acc
+
+    dots[0] = lax.fori_loop(0, NZ, level, jnp.zeros((8, 128), F32))
+
+
+def edge_dot(near, far, own_near, own_far):
+    index = xy_index()
+    last = lax.axis_size("xy_0") * lax.axis_size("xy_1") - 1
+    inside = (index > 0) & (index < last)
+    outer = jnp.where(inside, far[...], 0.0) * own_far[...]
+    return jnp.sum(near[...] * own_near[...] + outer, axis=0)
 
 
 def halo_masks():
@@ -482,30 +533,29 @@
     return part[z, c, rows, lanes] - jnp.where(inside[xi], edge, 0.0)
 
 
-def second_sweep(part, near, far, u, ps, image, keep, give, dots, hscr, st):
+def second_sweep(part, near, far, pb, sb, image, keep, give, hscr, st):
     masks = halo_masks()
     zero = jnp.zeros((8, 128), F32)
     for n in range(6):
         for c in range(4):
             st[n, c] = zero
 
-    def up(z, acc):
+    def up(z, carry):
         for n, (xi, lj) in enumerate(COLS):
             rows, lanes = tile(xi, lj)
-            blk = [ps[z, n, e] for e in range(16)]
+            blk = [pb[z, n, e] for e in range(16)]
             img = [with_halo(part, near, far, z, c, xi, lj, masks) for c in range(4)]
             for c in range(4):
                 image[z, c, rows, lanes] = img[c]
-            acc = acc + fsum(img[c] * u[z, c, rows, lanes] for c in range(4))
             g = add(img, full(blk, [st[n, c] for c in range(4)]))
             for c in range(4):
                 st[n, c] = g[c]
-            h = symm([ps[z, n, 16 + e] for e in range(10)], g)
+            h = symm([sb[z, n, e] for e in range(10)], g)
             for c in range(4):
                 hscr[z, n, c] = h[c]
-        return acc
-
-    dots[0] = lax.fori_loop(0, NZ, up, zero)
+        return carry
+
+    lax.fori_loop(0, NZ, up, 0)
     up_last = []
     for n in range(6):
         for c in range(4):
@@ -515,7 +565,7 @@
     def down(s, carry):
         z = NZ - 2 - s
         for n in range(6):
-            t = full_t([ps[z + 1, n, e] for e in range(16)], [st[n, c] for c in range(4)])
+            t = full_t([pb[z + 1, n, e] for e in range(16)], [st[n, c] for c in range(4)])
             for c in range(4):
                 st[n, c] = hscr[z, n, c] + t[c]
         return carry
@@ -538,39 +588,34 @@
                     (keep if xi == core else give)[4 + c, lj] = st[n, c]
 
 
-def last_dots(part, near, far, u, w, da, db, dc, y, sums):
-    masks = halo_masks()
-    zero = jnp.zeros((8, 128), F32)
-
-    def level(z, carry):
-        au, aw = carry
-        for xi, lj in COLS:
-            rows, lanes = tile(xi, lj)
-            for c in range(4):
-                val = with_halo(part, near, far, z, c, xi, lj, masks)
-                y[z, c, rows, lanes] = val
-                au = au + val * u[z, c, rows, lanes]
-                aw = aw + val * w[z, c, rows, lanes]
-        return au, aw
-
-    au, aw = lax.fori_loop(0, NZ, level, (zero, zero))
+def last_dots(near, far, *refs):
+    (near_w, far_w, nu, fu, own_nu, own_fu), (da, db, dc, dd, sums) = refs[:6], refs[6:]
     lane = lax.broadcasted_iota(I32, (1, 128), 1)
     line = jnp.zeros((1, 128), F32)
-    for e, part_sum in enumerate((da[0], dc[0], db[0], db[1], au, aw)):
-        line = jnp.where(lane == e, jnp.sum(part_sum), line)
+    curv0 = jnp.sum(dc[0]) - jnp.sum(edge_dot(nu, fu, own_nu, own_fu))
+    curv1 = jnp.sum(dd[0]) - jnp.sum(edge_dot(near, far, near_w, far_w))
+    for e, value in enumerate((jnp.sum(da[0]), curv0, jnp.sum(db[0]), jnp.sum(db[1]), curv1)):
+        line = jnp.where(lane == e, value, line)
     sums[...] = jnp.broadcast_to(line[None], sums.shape)
 
 
-def combine(sums, r, u, image, w, y, sol, res):
-    tot = jnp.sum(sums[...], axis=0)
-    ru, ui, iw, rw, uy, wy = [tot[:, e : e + 1] for e in range(6)]
+def combine(sums, r, u, image, w, part, near, far, sol_hbm, res_hbm, sol, res, sems):
+    tot = fsum([jnp.sum(sums[pl.ds(16 * k, 16)], axis=0) for k in range(8)])
+    ru, ui, iw, rw, wy = [tot[:, e : e + 1] for e in range(5)]
     a0 = ru / ui
     fresh = ru - a0 * (rw + ui) + a0 * a0 * iw
     beta1 = 1.0 + fresh / ru
-    curv = beta1 * beta1 * ui - beta1 * a0 * (uy + iw) + a0 * a0 * wy
+    curv = beta1 * beta1 * ui - beta1 * a0 * (iw + iw) + a0 * a0 * wy
     a1 = fresh / curv
     s0 = jnp.broadcast_to(a0 + a1 * beta1, (8, 128))
     s1 = jnp.broadcast_to(a1 * a0, (8, 128))
+    masks = halo_masks()
+
+    def copies(z):
+        return [
+            pltpu.make_async_copy(src.at[z], dst.at[z], sems.at[e, z])
+            for e, (src, dst) in enumerate(((sol, sol_hbm), (res, res_hbm)))
+        ]
 
     def level(z, carry):
         for xi, lj in COLS:
@@ -578,20 +623,30 @@
             for c in range(4):
                 at = (z, c, rows, lanes)
                 sol[at] = s0 * u[at] - s1 * w[at]
-                res[at] = r[at] - s0 * image[at] + s1 * y[at]
+                y = with_halo(part, near, far, z, c, xi, lj, masks)
+                res[at] = r[at] - s0 * image[at] + s1 * y
+        for cp in copies(z):
+            cp.start()
         return carry
 
     lax.fori_loop(0, NZ, level, 0)
 
-
-def call(body, out, name, nargs, hbm=(), scratch=(), sems=(), limit=10):
+    def finish(z, carry):
+        for cp in copies(z):
+            cp.wait()
+        return carry
+
+    lax.fori_loop(0, NZ, finish, 0)
+
+
+def call(body, out, name, nargs, hbm=(), scratch=(), sems=(), limit=10, to_hbm=False):
     vm = pl.BlockSpec(memory_space=pltpu.VMEM)
     hb = pl.BlockSpec(memory_space=pltpu.HBM)
     return pl.pallas_call(
         body,
         out_shape=[s if hasattr(s, "dtype") else jax.ShapeDtypeStruct(s, F32) for s in out],
         in_specs=[hb if n in hbm else vm for n in range(nargs)],
-        out_specs=[vm for _ in out],
+        out_specs=[hb if to_hbm else vm for _ in out],
         scratch_shapes=[s if hasattr(s, "dtype") else pltpu.VMEM(s, F32) for s in scratch]
         + [pltpu.SemaphoreType.DMA(s) for s in sems],
         compiler_params=pltpu.CompilerParams(vmem_limit_bytes=limit * MIB),
@@ -604,7 +659,8 @@
 PLANE = (4, 16, 384)
 TABS = (NTAB, 8, 128)
 SCR = ((NZ, 6, 4, 8, 128), (6, 4, 8, 128))
-PS = (NZ, 6, 26, 8, 128)
+PB = (NZ, 6, 16, 8, 128)
+SB = (NZ, 6, 10, 8, 128)
 KC = (NZ, 6, 20, 8, 128)
 
 
@@ -637,50 +693,52 @@
     return near, lax.ppermute(far, XY, around)
 
 
-def apply_m(first, r, ps, inflow, first_inflow, tabs, other):
+def apply_m(first, r, pb, sb, inflow, first_inflow, tabs, other):
     outs = (FIELD, PLANE, PLANE, EDGE, EDGE, (2, 8, 128))
-    return call(make_apply(first), outs, "apply", 8, scratch=SCR)(
-        r, ps, *inflow, *first_inflow, tabs, other
+    return call(make_apply(first), outs, "apply", 9, scratch=SCR)(
+        r, pb, sb, *inflow, *first_inflow, tabs, other
     )
 
 
 def operate(u, kc, zlow, zup):
-    return call(operator, (FIELD,), "operator", 4, scratch=(PLANE,))(u, kc, zlow, zup)[0]
+    return call(operator, (FIELD, (1, 8, 128)), "operator", 4, scratch=(PLANE,))(u, kc, zlow, zup)
 
 
 def per_device(load, mat, lay, stf, cpl, piv, fac):
     hbm_args = [load, mat, lay] + [jnp.transpose(t, (1, 2, 0)) for t in (fac, piv, stf, cpl)]
     hbm_args = [pltpu.with_memory_space_constraint(v, pltpu.HBM) for v in hbm_args]
-    keep, give, tabs, load, ps, kc = call(
+    ids = [jax.ShapeDtypeStruct(v.shape, I32) for v in (mat, lay)]
+    keep, give, tabs, load, mat, lay, pb = call(
         first_sweep,
-        (part_of(37), part_of(37), TABS, FIELD, PS, KC),
+        (part_of(37), part_of(37), TABS, FIELD, *ids, PB),
         "first_sweep",
         7,
         hbm=range(7),
-        scratch=[pltpu.VMEM(mat.shape, I32), pltpu.VMEM(lay.shape, I32), (6, 34, 8, 128)]
-        + [pltpu.SMEM(v.shape, F32) for v in hbm_args[3:]],
-        sems=((3, NZ), (4,)),
+        scratch=[(6, 34, 8, 128)] + [pltpu.SMEM(v.shape, F32) for v in hbm_args[3:]],
+        sems=((3, NZ // CHUNK), (4,)),
     )(*hbm_args)
     lu, *send = call(
         make_merge(True), ((2, *part_of(37)), *blocks_of(R1)), "merge1", 3, scratch=((NSEG * R1, 128),)
     )(keep, swap(give), tabs)
+    sent = exchange(send)
+    sb, kc, token = call(expand, (SB, KC, (8, 128)), "expand", 4)(mat, lay, tabs, send[0])
     fixed, *back = call(
         make_owner(True),
         ((NSEG * R1, 128), *blocks_of(R2)),
         "owner1",
-        NSEG + 1,
+        NSEG + 2,
         scratch=((NSEG * R2, 128),),
-    )(*exchange(send), tabs)
+    )(*sent, tabs, token)
     keep, give, back1 = call(
         make_split(True), (part_of(11), part_of(11), (NSEG * R2, 128)), "split1", NSEG + 2
     )(*exchange(back), lu, tabs)
     inflow1 = (keep, swap(give))
-    u, zlow, zup, near, far, da = apply_m(True, load, ps, inflow1, inflow1, tabs, load)
-    near, far = halo(near, far)
-    part = operate(u, kc, zlow, zup)
-    image, keep, give, dc = call(
-        second_sweep, (FIELD, part_of(8), part_of(8), (1, 8, 128)), "second_sweep", 5, scratch=SCR
-    )(part, near, far, u, ps)
+    u, zlow, zup, near_u, far_u, da = apply_m(True, load, pb, sb, inflow1, inflow1, tabs, load)
+    edges_u = halo(near_u, far_u)
+    part, dc = operate(u, kc, zlow, zup)
+    image, keep, give = call(
+        second_sweep, (FIELD, part_of(8), part_of(8)), "second_sweep", 5, scratch=SCR
+    )(part, *edges_u, pb, sb)
     lu2, *send = call(
         make_merge(False), ((2, *part_of(8)), *blocks_of(R3)), "merge2", 4, scratch=((NSEG * R3, 128),)
     )(keep, swap(give), lu, tabs)
@@ -690,12 +748,26 @@
     keep, give = call(
         make_split(False), (part_of(8),) * 2, "split2", NSEG + 4, scratch=((NSEG * R3, 128),)
     )(*exchange(back), lu2, lu, back1, tabs)
-    w, zlow, zup, near, far, db = apply_m(False, image, ps, (keep, swap(give)), inflow1, tabs, load)
-    near, far = halo(near, far)
-    part = operate(w, kc, zlow, zup)
-    y, sums = call(last_dots, (FIELD, (128, 1, 128)), "last_dots", 8)(part, near, far, u, w, da, db, dc)
+    w, zlow, zup, near_w, far_w, db = apply_m(
+        False, image, pb, sb, (keep, swap(give)), inflow1, tabs, load
+    )
+    edges_w = halo(near_w, far_w)
+    part, dd = operate(w, kc, zlow, zup)
+    (sums,) = call(last_dots, ((128, 1, 128),), "last_dots", 12)(
+        *edges_w, near_w, far_w, *edges_u, near_u, far_u, da, db, dc, dd
+    )
     sums = lax.all_to_all(sums, ALL, 0, 0, tiled=True)
-    return tuple(call(combine, (FIELD, FIELD), "combine", 6)(sums, load, u, image, w, y))
+    return tuple(
+        call(
+            combine,
+            (FIELD, FIELD),
+            "combine",
+            8,
+            scratch=(FIELD, FIELD),
+            sems=((2, NZ),),
+            to_hbm=True,
+        )(sums, load, u, image, w, part, *edges_w)
+    )
 
 
 def solution(mesh):

time: 100 us -> 97.8 us (0.978)
  waiting for transfers between devices: 19.9 us -> 15 us
  Pallas kernels: 25 us -> 27.2 us
    ppermute x12, waiting for transfers between devices: 15.2 us -> 10.5 us  [exchange(): lax.ppermute(part, 'gz_0', [(i, i ^ d) for i in range(count)])]
    pallas_call x8 -> x9, Pallas kernels: 23.3 us -> 25.5 us  [the longest x1 7.72 us: per_device(): call(first_sweep, (part_of(37), part_of(37), TABS, FIELD, *ids, PB), 'fir...]
  transfers between devices with their start and end apart: 20 -> 20, of which waited for: 14 -> 13; matrix products, arithmetic and copies ran while one was open for 0% -> 0% of each run, Pallas kernels for 5% -> 10%
where the time goes in v4:
time: 97.8 us; the launch traced here: 97.6 us
  starting transfers between devices  36.2 us (37%)
  Pallas kernels  27.2 us (28%)
  blocking collectives  18.4 us (19%)
  waiting for transfers between devices  15 us (15%)
    all_to_all x1, blocking collectives, per_device(): sums = lax.all_to_all(sums, ALL, 0, 0, tiled=True)  18.4 us
    ppermute x12, starting transfers between devices, exchange(): lax.ppermute(part, 'gz_0', [(i, i ^ d) for i in range(count)])  15.7 us
    ppermute x12, waiting for transfers between devices, exchange(): lax.ppermute(part, 'gz_0', [(i, i ^ d) for i in range(count)])  10.5 us
    ppermute x2, starting transfers between devices, halo(): return (near, lax.ppermute(far, XY, around))  9.47 us
    ppermute x4, starting transfers between devices, swap(): return lax.ppermute(buf, 'gz_1', [(0, 1), (1, 0)])  9.14 us
    pallas_call x1, Pallas kernels, per_device(): call(first_sweep, (part_of(37), part_of(37), TABS, FIELD, *ids, PB), 'fir...  7.72 us
    pallas_call x1, Pallas kernels, per_device(): call(expand, (SB, KC, (8, 128)), 'expand', 4)(mat, lay, tabs, send[0])  4.73 us
    pallas_call x2, Pallas kernels, operate(): call(operator, (FIELD, (1, 8, 128)), 'operator', 4, scratch=(PLANE,))  4.62 us
  transfers between devices with their start and end apart: 20, of which 13 were waited for; matrix products, arithmetic and copies ran while one was open for 0% of the time, Pallas kernels for 10%

profile of v4, /device:TPU:1, one launch (start us, length us, event | category | flops | bytes accessed | tf_op | source)
XLA Modules:
  0.0 97.6 jit_solution(17565743392919540067)
XLA Ops:
  0.6 7.7 %first_sweep.1 = (f32[37,3,8,128]{3,2,1,0:T(8,128)S(1)}, f32[37,3,8,128]{3,2,1,0:T(8,128)S(1)}, f32[56,8,128]{2,1,0:T(8,128)S(1)}, f32[16,4,16,384]{3,2,1,0:T(8,...) custom-call(f32[16,4,16,384]{3,2,1,0:T(8,128)} %r_hbm.1, ...), custom_call_target="tpu_custom_call" | custom-call | tf_op jit(solution)/shard_map/first_sweep/pallas_call | solution.py:711
  8.4 1.5 %collective-permute-start = (f32[37,3,8,128]{3,2,1,0:T(8,128)S(1)}, f32[37,3,8,128]{3,2,1,0:T(8,128)S(1)}, u32[]{:S(2)}, u32[]{:S(2)}) collective-permute-start(f32[37,3,8,128]{3,2,1,0:T(8,128)S(1)} %get-tuple-element.61), channel_id=1, source_target_pairs={{0,16},{16,0},{1,17},{17,1},{2,18},{18,2},{3,19},{19,3},{4,20},{20... | collective-permute-start | bytes 1363976 | tf_op jit(solution)/shard_map/ppermute | solution.py:682
  9.8 1.4 %collective-permute-done.refs_1_ = f32[37,3,8,128]{3,2,1,0:T(8,128)S(1)} collective-permute-done((f32[37,3,8,128]{3,2,1,0:T(8,128)S(1)}, f32[37,3,8,128]{3,2,1,0:T(8,128)S(1)}, u32[]{:S(2)}, u32[]{:S(2)}) %collective-permute-start) | collective-permute-done | bytes 454688 | tf_op jit(solution)/shard_map/ppermute | solution.py:682
  11.8 1.4 %collective-permute-start.1 = (f32[224,128]{1,0:T(8,128)S(1)}, f32[224,128]{1,0:T(8,128)S(1)}, u32[]{:S(2)}, u32[]{:S(2)}) collective-permute-start(f32[224,128]{1,0:T(8,128)S(1)} %get-tuple-element.64), channel_id=1, source_target_pairs={{0,32},{32,0},{64,96},{96,64},{1,33},{33,1},{65,97},{97,65},{2,34}... | collective-permute-start | bytes 344072 | tf_op jit(solution)/shard_map/ppermute | solution.py:670
  13.3 2.5 %collective-permute-start.2 = (f32[224,128]{1,0:T(8,128)S(1)}, f32[224,128]{1,0:T(8,128)S(1)}, u32[]{:S(2)}, u32[]{:S(2)}) collective-permute-start(f32[224,128]{1,0:T(8,128)S(1)} %get-tuple-element.65), channel_id=1, source_target_pairs={{0,64},{32,96},{64,0},{96,32},{1,65},{33,97},{65,1},{97,33},{2,66}... | collective-permute-start | bytes 344072 | tf_op jit(solution)/shard_map/ppermute | solution.py:670
  15.8 4.7 %expand.1 = (f32[16,6,10,8,128]{4,3,2,1,0:T(8,128)S(1)}, f32[16,6,20,8,128]{4,3,2,1,0:T(8,128)S(1)}, f32[8,128]{1,0:T(8,128)S(1)}) custom-call(s32[16,16,384]{2,1,0:T(8,128)S(1)} %get-tuple-element.57.mat, s32[16,16,384]{2,1,0:T(8,128)S(1)} %get-tuple-element.58.lay, f32[56,8,128]{2,1,0:T(8,128)S(1)} %get-tuple-element.59.refs_2_.tabs.refs_4_.refs_5_.refs_3_.refs_7_, ...), custom_call_target="tpu_custom_call" | custom-call | tf_op jit(solution)/shard_map/expand/pallas_call | solution.py:724
  21.0 2.6 %collective-permute-done.3.refs_3_ = f32[224,128]{1,0:T(8,128)S(1)} collective-permute-done((f32[224,128]{1,0:T(8,128)S(1)}, f32[224,128]{1,0:T(8,128)S(1)}, u32[]{:S(2)}, u32[]{:S(2)}) %collective-permute-start.3) | collective-permute-done | bytes 114720 | tf_op jit(solution)/shard_map/ppermute | solution.py:670
  23.9 1.9 %collective-permute-start.5 = (f32[72,128]{1,0:T(8,128)S(1)}, f32[72,128]{1,0:T(8,128)S(1)}, u32[]{:S(2)}, u32[]{:S(2)}) collective-permute-start(f32[72,128]{1,0:T(8,128)S(1)} %get-tuple-element.70), channel_id=1, source_target_pairs={{0,64},{32,96},{64,0},{96,32},{1,65},{33,97},{65,1},{97,33},{2,66}... | collective-permute-start | bytes 110600 | tf_op jit(solution)/shard_map/ppermute | solution.py:670
  25.8 2.0 %collective-permute-start.6 = (f32[72,128]{1,0:T(8,128)S(1)}, f32[72,128]{1,0:T(8,128)S(1)}, u32[]{:S(2)}, u32[]{:S(2)}) collective-permute-start(f32[72,128]{1,0:T(8,128)S(1)} %get-tuple-element.71), channel_id=1, source_target_pairs={{0,96},{32,64},{64,32},{96,0},{1,97},{33,65},{65,33},{97,1},{2,98}... | collective-permute-start | bytes 110600 | tf_op jit(solution)/shard_map/ppermute | solution.py:670
  28.5 1.5 %collective-permute-done.6.refs_3_ = f32[72,128]{1,0:T(8,128)S(1)} collective-permute-done((f32[72,128]{1,0:T(8,128)S(1)}, f32[72,128]{1,0:T(8,128)S(1)}, u32[]{:S(2)}, u32[]{:S(2)}) %collective-permute-start.6) | collective-permute-done | bytes 36896 | tf_op jit(solution)/shard_map/ppermute | solution.py:670
  30.3 2.1 %collective-permute-start.7 = (f32[11,3,8,128]{3,2,1,0:T(8,128)S(1)}, f32[11,3,8,128]{3,2,1,0:T(8,128)S(1)}, u32[]{:S(2)}, u32[]{:S(2)}) collective-permute-start(f32[11,3,8,128]{3,2,1,0:T(8,128)S(1)} %get-tuple-element.74), channel_id=1, source_target_pairs={{0,16},{16,0},{1,17},{17,1},{2,18},{18,2},{3,19},{19,3},{4,20},{20... | collective-permute-start | bytes 405512 | tf_op jit(solution)/shard_map/ppermute | solution.py:682
  32.4 1.0 %collective-permute-done.7.got.first_got = f32[11,3,8,128]{3,2,1,0:T(8,128)S(1)} collective-permute-done((f32[11,3,8,128]{3,2,1,0:T(8,128)S(1)}, f32[11,3,8,128]{3,2,1,0:T(8,128)S(1)}, u32[]{:S(2)}, u32[]{:S(2)}) %collective-permute-start.7) | collective-permute-done | bytes 135200 | tf_op jit(solution)/shard_map/ppermute | solution.py:682
  33.4 2.1 %apply.2 = (f32[16,4,16,384]{3,2,1,0:T(8,128)S(1)}, f32[4,16,384]{2,1,0:T(8,128)S(1)}, f32[4,16,384]{2,1,0:T(8,128)S(1)}, f32[16,4,384]{2,1,0:T(4,128)S(1)}, f32...) custom-call(f32[16,4,16,384]{3,2,1,0:T(8,128)S(1)} %get-tuple-element.55.r.other, ...), custom_call_target="tpu_custom_call" | custom-call | tf_op jit(solution)/shard_map/apply/pallas_call | solution.py:698
  35.5 1.8 %collective-permute-start.8 = (f32[16,4,384]{2,1,0:T(4,128)S(1)}, f32[16,4,384]{2,1,0:T(4,128)S(1)}, u32[]{:S(2)}, u32[]{:S(2)}) collective-permute-start(f32[16,4,384]{2,1,0:T(4,128)S(1)} %get-tuple-element.80.refs_4_), channel_id=1, source_target_pairs={{0,1},{1,0},{2,3},{3,2},{4,5},{5,4},{6,7},{7,6},{8,9},{9,8},{10,11... | collective-permute-start | bytes 294920 | tf_op jit(solution)/shard_map/ppermute | solution.py:691
  37.3 4.7 %collective-permute-start.9 = (f32[16,4,384]{2,1,0:T(4,128)S(1)}, f32[16,4,384]{2,1,0:T(4,128)S(1)}, u32[]{:S(2)}, u32[]{:S(2)}) collective-permute-start(f32[16,4,384]{2,1,0:T(4,128)S(1)} %get-tuple-element.81.refs_5_), channel_id=1, source_target_pairs={{1,2},{2,1},{3,4},{4,3},{5,6},{6,5},{7,8},{8,7},{9,10},{10,9},{11,... | collective-permute-start | bytes 294920 | tf_op jit(solution)/shard_map/ppermute | solution.py:693
  42.0 2.2 %operator.2 = (f32[16,4,16,384]{3,2,1,0:T(8,128)S(1)}, f32[1,8,128]{2,1,0:T(8,128)S(1)}) custom-call(f32[16,4,16,384]{3,2,1,0:T(8,128)S(1)} %get-tuple-element.75.u, f32[16,6,20,8,128]{4,3,2,1,0:T(8,128)S(1)} %get-tuple-element.76.kc, f32[4,16,384]{2,1,0:T(8,128)S(1)} %get-tuple-element.77.zlow, f32[4,16,384]{2,1,0:T(8,128)S(1)} %get-tuple-element.78.zup), custom_call_target="tpu_custom_call" | custom-call | tf_op jit(solution)/shard_map/operator/pallas_call | solution.py:704
  44.2 1.7 %second_sweep.1 = (f32[16,4,16,384]{3,2,1,0:T(8,128)S(1)}, f32[8,3,8,128]{3,2,1,0:T(8,128)S(1)}, f32[8,3,8,128]{3,2,1,0:T(8,128)S(1)}) custom-call(f32[16,4,16,384]{3,2,1,0:T(8,128)S(1)} %get-tuple-element.79.part, f32[16,4,384]{2,1,0:T(4,128)S(1)} %collective-permute-done.8.near.refs_2_, f32[16,4,384]{2,1,0:T(4,128)S(1)} %collective-permute-done.9.far.refs_3_, ...), custom_call_target="tpu_custom_call" | custom-call | tf_op jit(solution)/shard_map/second_sweep/pallas_call | solution.py:739
  45.9 1.7 %collective-permute-start.10 = (f32[8,3,8,128]{3,2,1,0:T(8,128)S(1)}, f32[8,3,8,128]{3,2,1,0:T(8,128)S(1)}, u32[]{:S(2)}, u32[]{:S(2)}) collective-permute-start(f32[8,3,8,128]{3,2,1,0:T(8,128)S(1)} %get-tuple-element.84), channel_id=1, source_target_pairs={{0,16},{16,0},{1,17},{17,1},{2,18},{18,2},{3,19},{19,3},{4,20},{20... | collective-permute-start | bytes 294920 | tf_op jit(solution)/shard_map/ppermute | solution.py:682
  47.6 0.9 collective-permute-done.10.refs_1_
  48.9 3.4 %collective-permute-start.12 = (f32[56,128]{1,0:T(8,128)S(1)}, f32[56,128]{1,0:T(8,128)S(1)}, u32[]{:S(2)}, u32[]{:S(2)}) collective-permute-start(f32[56,128]{1,0:T(8,128)S(1)} %get-tuple-element.87), channel_id=1, source_target_pairs={{0,64},{32,96},{64,0},{96,32},{1,65},{33,97},{65,1},{97,33},{2,66}... | collective-permute-start | bytes 86024 | tf_op jit(solution)/shard_map/ppermute | solution.py:670
  52.7 1.1 %collective-permute-done.12.refs_2_ = f32[56,128]{1,0:T(8,128)S(1)} collective-permute-done((f32[56,128]{1,0:T(8,128)S(1)}, f32[56,128]{1,0:T(8,128)S(1)}, u32[]{:S(2)}, u32[]{:S(2)}) %collective-permute-start.12) | collective-permute-done | bytes 28704 | tf_op jit(solution)/shard_map/ppermute | solution.py:670
  53.8 2.4 %collective-permute-done.13.refs_3_ = f32[56,128]{1,0:T(8,128)S(1)} collective-permute-done((f32[56,128]{1,0:T(8,128)S(1)}, f32[56,128]{1,0:T(8,128)S(1)}, u32[]{:S(2)}, u32[]{:S(2)}) %collective-permute-start.13) | collective-permute-done | bytes 28704 | tf_op jit(solution)/shard_map/ppermute | solution.py:670
  56.5 1.6 %collective-permute-start.15 = (f32[56,128]{1,0:T(8,128)S(1)}, f32[56,128]{1,0:T(8,128)S(1)}, u32[]{:S(2)}, u32[]{:S(2)}) collective-permute-start(f32[56,128]{1,0:T(8,128)S(1)} %get-tuple-element.92), channel_id=1, source_target_pairs={{0,64},{32,96},{64,0},{96,32},{1,65},{33,97},{65,1},{97,33},{2,66}... | collective-permute-start | bytes 86024 | tf_op jit(solution)/shard_map/ppermute | solution.py:670
  58.1 2.2 %collective-permute-start.16 = (f32[56,128]{1,0:T(8,128)S(1)}, f32[56,128]{1,0:T(8,128)S(1)}, u32[]{:S(2)}, u32[]{:S(2)}) collective-permute-start(f32[56,128]{1,0:T(8,128)S(1)} %get-tuple-element.93), channel_id=1, source_target_pairs={{0,96},{32,64},{64,32},{96,0},{1,97},{33,65},{65,33},{97,1},{2,98}... | collective-permute-start | bytes 86024 | tf_op jit(solution)/shard_map/ppermute | solution.py:670
  60.8 1.3 %collective-permute-done.16.refs_3_ = f32[56,128]{1,0:T(8,128)S(1)} collective-permute-done((f32[56,128]{1,0:T(8,128)S(1)}, f32[56,128]{1,0:T(8,128)S(1)}, u32[]{:S(2)}, u32[]{:S(2)}) %collective-permute-start.16) | collective-permute-done | bytes 28704 | tf_op jit(solution)/shard_map/ppermute | solution.py:670
  62.3 3.9 %collective-permute-start.17 = (f32[8,3,8,128]{3,2,1,0:T(8,128)S(1)}, f32[8,3,8,128]{3,2,1,0:T(8,128)S(1)}, u32[]{:S(2)}, u32[]{:S(2)}) collective-permute-start(f32[8,3,8,128]{3,2,1,0:T(8,128)S(1)} %get-tuple-element.97), channel_id=1, source_target_pairs={{0,16},{16,0},{1,17},{17,1},{2,18},{18,2},{3,19},{19,3},{4,20},{20... | collective-permute-start | bytes 294920 | tf_op jit(solution)/shard_map/ppermute | solution.py:682
  66.1 0.9 collective-permute-done.17.got
  67.1 2.2 %apply.3 = (f32[16,4,16,384]{3,2,1,0:T(8,128)S(1)}, f32[4,16,384]{2,1,0:T(8,128)S(1)}, f32[4,16,384]{2,1,0:T(8,128)S(1)}, f32[16,4,384]{2,1,0:T(4,128)S(1)}, f32...) custom-call(f32[16,4,16,384]{3,2,1,0:T(8,128)S(1)} %get-tuple-element.82.r.image, ...), custom_call_target="tpu_custom_call" | custom-call | tf_op jit(solution)/shard_map/apply/pallas_call | solution.py:698
  69.4 4.8 %collective-permute-start.19 = (f32[16,4,384]{2,1,0:T(4,128)S(1)}, f32[16,4,384]{2,1,0:T(4,128)S(1)}, u32[]{:S(2)}, u32[]{:S(2)}) collective-permute-start(f32[16,4,384]{2,1,0:T(4,128)S(1)} %get-tuple-element.99.refs_1_), channel_id=1, source_target_pairs={{1,2},{2,1},{3,4},{4,3},{5,6},{6,5},{7,8},{8,7},{9,10},{10,9},{11,... | collective-permute-start | bytes 294920 | tf_op jit(solution)/shard_map/ppermute | solution.py:693
  74.2 2.4 %operator.3 = (f32[16,4,16,384]{3,2,1,0:T(8,128)S(1)}, f32[1,8,128]{2,1,0:T(8,128)S(1)}) custom-call(f32[16,4,16,384]{3,2,1,0:T(8,128)S(1)} %get-tuple-element.103.u.w, f32[16,6,20,8,128]{4,3,2,1,0:T(8,128)S(1)} %get-tuple-element.76.kc, f32[4,16,384]{2,1,0:T(8,128)S(1)} %get-tuple-element.104.zlow, f32[4,16,384]{2,1,0:T(8,128)S(1)} %get-tuple-element.105.zup), custom_call_target="tpu_custom_call" | custom-call | tf_op jit(solution)/shard_map/operator/pallas_call | solution.py:704
  77.1 18.4 %all_to_all.5.sums = f32[128,1,128]{2,1,0:T(1,128)S(1)} all-to-all(f32[128,1,128]{2,1,0:T(1,128)S(1)} %last_dots.1), channel_id=1, replica_groups=mesh['gz_0'=4,'gz_1'=2,'xy_0'=4,'xy_1'=4] {'gz_0','gz_1','xy_0','xy_1'}, dimensions={0} | all-to-all | bytes 131072 | tf_op jit(solution)/shard_map/all_to_all | solution.py:759
  95.5 2.2 %combine.1 = (f32[16,4,16,384]{3,2,1,0:T(8,128)}, f32[16,4,16,384]{3,2,1,0:T(8,128)}) custom-call(f32[128,1,128]{2,1,0:T(1,128)S(1)} %all_to_all.5.sums, f32[16,4,16,384]{3,2,1,0:T(8,128)S(1)} %get-tuple-element.55.r.other, f32[16,4,16,384]{3,2,1,0:T(8,128)S(1)} %get-tuple-element.75.u, f32[16,4,16,384]{3,2,1,0:T(8,128)S(1)} %get-tuple-element.82.r.image, ...), custom_call_target="tpu_custom_call" | custom-call | tf_op jit(solution)/shard_map/combine/pallas_call | solution.py:761
  (24 shorter events, 4.8 us)
Async XLA Ops:
  8.4 2.9 %collective-permute-start = (f32[37,3,8,128]{3,2,1,0:T(8,128)S(1)}, f32[37,3,8,128]{3,2,1,0:T(8,128)S(1)}, u32[]{:S(2)}, u32[]{:S(2)}) collective-permute-start(f32[37,3,8,128]{3,2,1,0:T(8,128)S(1)} %get-tuple-element.61), channel_id=1, source_target_pairs={{0,16},{16,0},{1,17},{17,1},{2,18},{18,2},{3,19},{19,3},{4,20},{20... | collective-permute-start | bytes 1363976 | tf_op jit(solution)/shard_map/ppermute | solution.py:682
  11.8 8.7 %collective-permute-start.1 = (f32[224,128]{1,0:T(8,128)S(1)}, f32[224,128]{1,0:T(8,128)S(1)}, u32[]{:S(2)}, u32[]{:S(2)}) collective-permute-start(f32[224,128]{1,0:T(8,128)S(1)} %get-tuple-element.64), channel_id=1, source_target_pairs={{0,32},{32,0},{64,96},{96,64},{1,33},{33,1},{65,97},{97,65},{2,34}... | collective-permute-start | bytes 344072 | tf_op jit(solution)/shard_map/ppermute | solution.py:670
  13.3 7.8 %collective-permute-start.2 = (f32[224,128]{1,0:T(8,128)S(1)}, f32[224,128]{1,0:T(8,128)S(1)}, u32[]{:S(2)}, u32[]{:S(2)}) collective-permute-start(f32[224,128]{1,0:T(8,128)S(1)} %get-tuple-element.65), channel_id=1, source_target_pairs={{0,64},{32,96},{64,0},{96,32},{1,65},{33,97},{65,1},{97,33},{2,66}... | collective-permute-start | bytes 344072 | tf_op jit(solution)/shard_map/ppermute | solution.py:670
  15.7 7.9 %collective-permute-start.3 = (f32[224,128]{1,0:T(8,128)S(1)}, f32[224,128]{1,0:T(8,128)S(1)}, u32[]{:S(2)}, u32[]{:S(2)}) collective-permute-start(f32[224,128]{1,0:T(8,128)S(1)} %get-tuple-element.66), channel_id=1, source_target_pairs={{0,96},{32,64},{64,32},{96,0},{1,97},{33,65},{65,33},{97,1},{2,98}... | collective-permute-start | bytes 344072 | tf_op jit(solution)/shard_map/ppermute | solution.py:670
  23.8 3.9 %collective-permute-start.4 = (f32[72,128]{1,0:T(8,128)S(1)}, f32[72,128]{1,0:T(8,128)S(1)}, u32[]{:S(2)}, u32[]{:S(2)}) collective-permute-start(f32[72,128]{1,0:T(8,128)S(1)} %get-tuple-element.69), channel_id=1, source_target_pairs={{0,32},{32,0},{64,96},{96,64},{1,33},{33,1},{65,97},{97,65},{2,34}... | collective-permute-start | bytes 110600 | tf_op jit(solution)/shard_map/ppermute | solution.py:670
  23.9 4.6 %collective-permute-start.5 = (f32[72,128]{1,0:T(8,128)S(1)}, f32[72,128]{1,0:T(8,128)S(1)}, u32[]{:S(2)}, u32[]{:S(2)}) collective-permute-start(f32[72,128]{1,0:T(8,128)S(1)} %get-tuple-element.70), channel_id=1, source_target_pairs={{0,64},{32,96},{64,0},{96,32},{1,65},{33,97},{65,1},{97,33},{2,66}... | collective-permute-start | bytes 110600 | tf_op jit(solution)/shard_map/ppermute | solution.py:670
  25.8 4.2 %collective-permute-start.6 = (f32[72,128]{1,0:T(8,128)S(1)}, f32[72,128]{1,0:T(8,128)S(1)}, u32[]{:S(2)}, u32[]{:S(2)}) collective-permute-start(f32[72,128]{1,0:T(8,128)S(1)} %get-tuple-element.71), channel_id=1, source_target_pairs={{0,96},{32,64},{64,32},{96,0},{1,97},{33,65},{65,33},{97,1},{2,98}... | collective-permute-start | bytes 110600 | tf_op jit(solution)/shard_map/ppermute | solution.py:670
  30.3 3.1 %collective-permute-start.7 = (f32[11,3,8,128]{3,2,1,0:T(8,128)S(1)}, f32[11,3,8,128]{3,2,1,0:T(8,128)S(1)}, u32[]{:S(2)}, u32[]{:S(2)}) collective-permute-start(f32[11,3,8,128]{3,2,1,0:T(8,128)S(1)} %get-tuple-element.74), channel_id=1, source_target_pairs={{0,16},{16,0},{1,17},{17,1},{2,18},{18,2},{3,19},{19,3},{4,20},{20... | collective-permute-start | bytes 405512 | tf_op jit(solution)/shard_map/ppermute | solution.py:682
  35.5 8.7 %collective-permute-start.8 = (f32[16,4,384]{2,1,0:T(4,128)S(1)}, f32[16,4,384]{2,1,0:T(4,128)S(1)}, u32[]{:S(2)}, u32[]{:S(2)}) collective-permute-start(f32[16,4,384]{2,1,0:T(4,128)S(1)} %get-tuple-element.80.refs_4_), channel_id=1, source_target_pairs={{0,1},{1,0},{2,3},{3,2},{4,5},{5,4},{6,7},{7,6},{8,9},{9,8},{10,11... | collective-permute-start | bytes 294920 | tf_op jit(solution)/shard_map/ppermute | solution.py:691
  37.3 6.9 %collective-permute-start.9 = (f32[16,4,384]{2,1,0:T(4,128)S(1)}, f32[16,4,384]{2,1,0:T(4,128)S(1)}, u32[]{:S(2)}, u32[]{:S(2)}) collective-permute-start(f32[16,4,384]{2,1,0:T(4,128)S(1)} %get-tuple-element.81.refs_5_), channel_id=1, source_target_pairs={{1,2},{2,1},{3,4},{4,3},{5,6},{6,5},{7,8},{8,7},{9,10},{10,9},{11,... | collective-permute-start | bytes 294920 | tf_op jit(solution)/shard_map/ppermute | solution.py:693
  45.9 2.6 %collective-permute-start.10 = (f32[8,3,8,128]{3,2,1,0:T(8,128)S(1)}, f32[8,3,8,128]{3,2,1,0:T(8,128)S(1)}, u32[]{:S(2)}, u32[]{:S(2)}) collective-permute-start(f32[8,3,8,128]{3,2,1,0:T(8,128)S(1)} %get-tuple-element.84), channel_id=1, source_target_pairs={{0,16},{16,0},{1,17},{17,1},{2,18},{18,2},{3,19},{19,3},{4,20},{20... | collective-permute-start | bytes 294920 | tf_op jit(solution)/shard_map/ppermute | solution.py:682
  48.8 3.9 %collective-permute-start.11 = (f32[56,128]{1,0:T(8,128)S(1)}, f32[56,128]{1,0:T(8,128)S(1)}, u32[]{:S(2)}, u32[]{:S(2)}) collective-permute-start(f32[56,128]{1,0:T(8,128)S(1)} %get-tuple-element.86), channel_id=1, source_target_pairs={{0,32},{32,0},{64,96},{96,64},{1,33},{33,1},{65,97},{97,65},{2,34}... | collective-permute-start | bytes 86024 | tf_op jit(solution)/shard_map/ppermute | solution.py:670
  48.9 5.0 %collective-permute-start.12 = (f32[56,128]{1,0:T(8,128)S(1)}, f32[56,128]{1,0:T(8,128)S(1)}, u32[]{:S(2)}, u32[]{:S(2)}) collective-permute-start(f32[56,128]{1,0:T(8,128)S(1)} %get-tuple-element.87), channel_id=1, source_target_pairs={{0,64},{32,96},{64,0},{96,32},{1,65},{33,97},{65,1},{97,33},{2,66}... | collective-permute-start | bytes 86024 | tf_op jit(solution)/shard_map/ppermute | solution.py:670
  52.2 3.9 %collective-permute-start.13 = (f32[56,128]{1,0:T(8,128)S(1)}, f32[56,128]{1,0:T(8,128)S(1)}, u32[]{:S(2)}, u32[]{:S(2)}) collective-permute-start(f32[56,128]{1,0:T(8,128)S(1)} %get-tuple-element.88), channel_id=1, source_target_pairs={{0,96},{32,64},{64,32},{96,0},{1,97},{33,65},{65,33},{97,1},{2,98}... | collective-permute-start | bytes 86024 | tf_op jit(solution)/shard_map/ppermute | solution.py:670
  56.4 3.9 %collective-permute-start.14 = (f32[56,128]{1,0:T(8,128)S(1)}, f32[56,128]{1,0:T(8,128)S(1)}, u32[]{:S(2)}, u32[]{:S(2)}) collective-permute-start(f32[56,128]{1,0:T(8,128)S(1)} %get-tuple-element.91), channel_id=1, source_target_pairs={{0,32},{32,0},{64,96},{96,64},{1,33},{33,1},{65,97},{97,65},{2,34}... | collective-permute-start | bytes 86024 | tf_op jit(solution)/shard_map/ppermute | solution.py:670
  56.5 4.3 %collective-permute-start.15 = (f32[56,128]{1,0:T(8,128)S(1)}, f32[56,128]{1,0:T(8,128)S(1)}, u32[]{:S(2)}, u32[]{:S(2)}) collective-permute-start(f32[56,128]{1,0:T(8,128)S(1)} %get-tuple-element.92), channel_id=1, source_target_pairs={{0,64},{32,96},{64,0},{96,32},{1,65},{33,97},{65,1},{97,33},{2,66}... | collective-permute-start | bytes 86024 | tf_op jit(solution)/shard_map/ppermute | solution.py:670
  58.1 3.9 %collective-permute-start.16 = (f32[56,128]{1,0:T(8,128)S(1)}, f32[56,128]{1,0:T(8,128)S(1)}, u32[]{:S(2)}, u32[]{:S(2)}) collective-permute-start(f32[56,128]{1,0:T(8,128)S(1)} %get-tuple-element.93), channel_id=1, source_target_pairs={{0,96},{32,64},{64,32},{96,0},{1,97},{33,65},{65,33},{97,1},{2,98}... | collective-permute-start | bytes 86024 | tf_op jit(solution)/shard_map/ppermute | solution.py:670
  62.3 4.8 %collective-permute-start.17 = (f32[8,3,8,128]{3,2,1,0:T(8,128)S(1)}, f32[8,3,8,128]{3,2,1,0:T(8,128)S(1)}, u32[]{:S(2)}, u32[]{:S(2)}) collective-permute-start(f32[8,3,8,128]{3,2,1,0:T(8,128)S(1)} %get-tuple-element.97), channel_id=1, source_target_pairs={{0,16},{16,0},{1,17},{17,1},{2,18},{18,2},{3,19},{19,3},{4,20},{20... | collective-permute-start | bytes 294920 | tf_op jit(solution)/shard_map/ppermute | solution.py:682
  69.3 7.3 %collective-permute-start.18 = (f32[16,4,384]{2,1,0:T(4,128)S(1)}, f32[16,4,384]{2,1,0:T(4,128)S(1)}, u32[]{:S(2)}, u32[]{:S(2)}) collective-permute-start(f32[16,4,384]{2,1,0:T(4,128)S(1)} %get-tuple-element.98.refs_0_), channel_id=1, source_target_pairs={{0,1},{1,0},{2,3},{3,2},{4,5},{5,4},{6,7},{7,6},{8,9},{9,8},{10,11... | collective-permute-start | bytes 294920 | tf_op jit(solution)/shard_map/ppermute | solution.py:691
  69.4 7.4 %collective-permute-start.19 = (f32[16,4,384]{2,1,0:T(4,128)S(1)}, f32[16,4,384]{2,1,0:T(4,128)S(1)}, u32[]{:S(2)}, u32[]{:S(2)}) collective-permute-start(f32[16,4,384]{2,1,0:T(4,128)S(1)} %get-tuple-element.99.refs_1_), channel_id=1, source_target_pairs={{1,2},{2,1},{3,4},{4,3},{5,6},{6,5},{7,8},{8,7},{9,10},{10,9},{11,... | collective-permute-start | bytes 294920 | tf_op jit(solution)/shard_map/ppermute | solution.py:693
